TPU v7x, 32 devices: a whole 2x2x4 slice. The times are simulated.
32 devices in a mesh: seq: 2 (over core), blk: 8 (over z, x), head: 2 (over y).
Axes of the slice: x: 2, y: 2, z: 4, core: 2. Of those that a mesh axis runs over, the one named last changes fastest.
Arguments:
- hidden: bfloat16 [2048, 1024], P(('seq', 'blk')), may hold values from -6 to 6
- memory: bfloat16 [1024, 1024], P('seq'), may hold values from -6 to 6
- lengths: int32 [2], P('seq'), may hold values from 512 to 1024, as said below
- out_grad: bfloat16 [2048, 1024], P(('seq', 'blk')), may hold values from -6 to 6
- ln_self: float32 [1024], replicated, may hold values from 0.5 to 1.5
- self_query: bfloat16 [1024, 1024], P(None, 'head'), may hold values from -0.046875 to 0.046875
- self_key: bfloat16 [1024, 512], P(None, 'head'), may hold values from -0.1875 to 0.1875
- self_value: bfloat16 [1024, 512], P(None, 'head'), may hold values from -0.1875 to 0.1875
- self_out: bfloat16 [1024, 1024], P(None, 'head'), may hold values from -1 to 1
- rel_bias: float32 [32, 16], P(None, 'head'), may hold values from -4 to 4
- ln_cross: float32 [1024], replicated, may hold values from 0.5 to 1.5
- cross_query: bfloat16 [1024, 1024], P(None, 'head'), may hold values from -0.046875 to 0.046875
- cross_key: bfloat16 [1024, 512], P(None, 'head'), may hold values from -0.1875 to 0.1875
- cross_value: bfloat16 [1024, 512], P(None, 'head'), may hold values from -0.1875 to 0.1875
- cross_out: bfloat16 [1024, 1024], P(None, 'head'), may hold values from -0.5 to 0.5
- ln_ffn: float32 [1024], replicated, may hold values from 0.5 to 1.5
- ffn_gate: bfloat16 [1024, 2816], P(None, 'head'), may hold values from -0.1875 to 0.1875
- ffn_up: bfloat16 [1024, 2816], P(None, 'head'), may hold values from -0.1875 to 0.1875
- feedforward_down_weight: bfloat16 [1024, 2816], P(None, 'head'), may hold values from -0.109375 to 0.109375
Outputs:
- layer_out: bfloat16 [2048, 1024], P(('seq', 'blk'))
- hidden_grad: float32 [2048, 1024], P(('seq', 'blk'))
- memory_grad: float32 [1024, 1024], P(('seq', 'blk', 'head'))
- grad_ln_self: float32 [1024], P(('seq', 'blk'))
- grad_self_query: float32 [1024, 1024], P(('seq', 'blk'), 'head')
- grad_self_key: float32 [1024, 512], P(('seq', 'blk'), 'head')
- grad_self_value: float32 [1024, 512], P(('seq', 'blk'), 'head')
- grad_self_out: float32 [1024, 1024], P(('seq', 'blk'), 'head')
- grad_rel_bias: float32 [32, 16], P(None, 'head')
- grad_ln_cross: float32 [1024], P(('seq', 'blk'))
- grad_cross_query: float32 [1024, 1024], P(('seq', 'blk'), 'head')
- grad_cross_key: float32 [1024, 512], P(('seq', 'blk'), 'head')
- grad_cross_value: float32 [1024, 512], P(('seq', 'blk'), 'head')
- grad_cross_out: float32 [1024, 1024], P(('seq', 'blk'), 'head')
- grad_ln_ffn: float32 [1024], P(('seq', 'blk'))
- grad_ffn_gate: float32 [1024, 2816], P(('seq', 'blk'), 'head')
- grad_ffn_up: float32 [1024, 2816], P(('seq', 'blk'), 'head')
- grad_ffn_down: float32 [1024, 2816], P(('seq', 'blk'), 'head')
Inputs may be any that keep to these rules, and one draw needn't show every extreme that they name: `lengths`: one sequence has all 1024 positions valid; every other has 512 or more.
All inputs are finite; a program needn't handle non-finite values.
Results may differ from a plain program's by a relative error of at most 0.04.
Values may be sent and summed in bfloat16 or wider, within the bound.
A program may use at most 192 MiB of HBM per device.

v0:
```python
import jax
import jax.numpy as jnp
import numpy as np
from jax import lax
from jax.sharding import PartitionSpec as P

HEAD_DIM = 64
BUCKETS = 32
MAX_DIST = 128


EPSILON = 1e-06
MASKED = -1e30
HIGHEST = lax.Precision.HIGHEST


def bucket_of(distance, bucket_count, far_reach):
    exact_span = bucket_count // 2
    thresholds = np.ceil(
        exact_span * (far_reach / exact_span) ** (np.arange(1, exact_span) / exact_span)
    )
    bucket_index = jnp.minimum(distance, exact_span)
    for threshold in thresholds:
        bucket_index = bucket_index + (distance >= int(threshold)).astype(jnp.int32)
    return bucket_index


def block_rows(row_count, limit):
    for candidate in range(min(row_count, limit), 0, -1):
        if row_count % candidate == 0:
            return candidate
    return 1


def matmul(left, right):
    return jnp.dot(left, right, preferred_element_type=jnp.float32)


def matmul_t(left, right):
    return lax.dot_general(
        left, right, (((1,), (1,)), ((), ())), preferred_element_type=jnp.float32
    )


def matmul_tn(left, right):
    return lax.dot_general(
        left, right, (((0,), (0,)), ((), ())), preferred_element_type=jnp.float32
    )


def rms_scale(values, norm_gain):
    return (
        values * lax.rsqrt(jnp.mean(values * values, axis=-1, keepdims=True) + EPSILON) * norm_gain
    )


def rms_back(values, norm_gain, normed_grad):
    scale = lax.rsqrt(jnp.mean(values * values, axis=-1, keepdims=True) + EPSILON)
    unit = values * scale
    unit_grad = normed_grad * norm_gain
    values_grad = scale * (unit_grad - unit * jnp.mean(unit_grad * unit, axis=-1, keepdims=True))
    return (values_grad, jnp.sum(normed_grad * unit, axis=0))


def toeplitz(bias_line, row_count, col_count):
    heads_here, line_length = bias_line.shape
    tiled = jnp.tile(bias_line, (1, row_count + 1))
    tiled = tiled[:, row_count - 1 : row_count - 1 + row_count * (line_length - 1)]
    return tiled.reshape(heads_here, row_count, line_length - 1)[:, :, :col_count]


def diagonal_sums(grid, line_length):
    heads_here, row_count, col_count = grid.shape
    padded = jnp.pad(grid, ((0, 0), (0, 0), (0, line_length - 1 - col_count)))
    flat = padded.reshape(heads_here, row_count * (line_length - 1))
    flat = jnp.pad(flat, ((0, 0), (row_count - 1, line_length + 1)))
    return jnp.sum(flat.reshape(heads_here, row_count + 1, line_length), axis=1)


def score_block(query_matrix, key_block, query_first, key_first, length, bias_table):
    row_count, groups_here, repeat, head_size = query_matrix.shape
    col_count = key_block.shape[0]
    key_grid = key_block.reshape(col_count, groups_here, head_size)
    scores = jnp.einsum(
        "tgrd,pgd->grtp", query_matrix, key_grid, preferred_element_type=jnp.float32
    )
    line_length = row_count + col_count - 1
    distance = query_first - key_first + row_count - 1 - jnp.arange(line_length, dtype=jnp.int32)
    buckets = bucket_of(jnp.maximum(distance, 0), BUCKETS, MAX_DIST)
    one_hot = (buckets[:, None] == jnp.arange(BUCKETS, dtype=jnp.int32)[None, :]).astype(
        jnp.float32
    )
    bias_line = lax.dot_general(bias_table, one_hot, (((0,), (1,)), ((), ())), precision=HIGHEST)
    bias_grid = toeplitz(bias_line, row_count, col_count).reshape(
        groups_here, repeat, row_count, col_count
    )
    query_pos = query_first + jnp.arange(row_count, dtype=jnp.int32)
    key_pos = key_first + jnp.arange(col_count, dtype=jnp.int32)
    allowed = (query_pos[:, None] >= key_pos[None, :]) & (key_pos[None, :] < length)
    return (scores + bias_grid, allowed, one_hot)


def body(
    hidden,
    memory,
    lengths,
    out_grad,
    ln_self,
    self_query,
    self_key,
    self_value,
    self_out,
    rel_bias,
    ln_cross,
    cross_query,
    cross_key,
    cross_value,
    cross_out,
    ln_ffn,
    ffn_gate,
    ffn_up,
    feedforward_down_weight,
):
    tok_rows = hidden.shape[0]
    groups_here = self_key.shape[1] // HEAD_DIM
    heads_here = self_query.shape[1] // HEAD_DIM
    repeat = heads_here // groups_here
    block_count = lax.axis_size("blk")
    seq_rows = tok_rows * block_count
    query_first = lax.axis_index("blk") * tok_rows
    length = lengths[0]
    rows_in = hidden.astype(jnp.float32)

    def head_running_total(partial_sum):
        return lax.psum(partial_sum.astype(jnp.bfloat16), "head").astype(jnp.float32)

    normed_self = rms_scale(rows_in, ln_self).astype(jnp.bfloat16)
    queries = matmul(normed_self, self_query).astype(jnp.bfloat16)
    key_rows = matmul(normed_self, self_key).astype(jnp.bfloat16)
    value_rows = matmul(normed_self, self_value).astype(jnp.bfloat16)
    query_matrix = queries.reshape(tok_rows, groups_here, repeat, HEAD_DIM)
    start_state = (
        jnp.full((groups_here, repeat, tok_rows), MASKED, jnp.float32),
        jnp.zeros((groups_here, repeat, tok_rows), jnp.float32),
        jnp.zeros((groups_here, repeat, tok_rows, HEAD_DIM), jnp.float32),
    )
    first_row = jnp.int32(0)
    key_piece = lax.all_gather(key_rows, "blk", axis=0, tiled=True)
    value_piece = lax.all_gather(value_rows, "blk", axis=0, tiled=True)
    piece_rows = key_piece.shape[0]
    fold_inner_size = block_rows(piece_rows, 1024)

    def visit_block(block_index, current):
        old_max, old_total, old_acc = current
        key_block = lax.dynamic_slice_in_dim(
            key_piece, block_index * fold_inner_size, fold_inner_size, 0
        )
        value_block = lax.dynamic_slice_in_dim(
            value_piece, block_index * fold_inner_size, fold_inner_size, 0
        )
        scores, allowed, one_hot = score_block(
            query_matrix,
            key_block,
            query_first,
            first_row + block_index * fold_inner_size,
            length,
            rel_bias,
        )
        new_max = jnp.maximum(old_max, jnp.max(jnp.where(allowed, scores, MASKED), axis=-1))
        weights = jnp.where(allowed, jnp.exp(scores - new_max[..., None]), 0.0)
        rescale = jnp.exp(old_max - new_max)
        updated_total = old_total * rescale + jnp.sum(weights, axis=-1)
        value_grid = value_block.reshape(fold_inner_size, groups_here, HEAD_DIM)
        updated_accumulator = old_acc * rescale[..., None] + jnp.einsum(
            "grtp,pgd->grtd",
            weights.astype(jnp.bfloat16),
            value_grid,
            preferred_element_type=jnp.float32,
        )
        return (new_max, updated_total, updated_accumulator)

    row_max, row_total, accumulated = lax.fori_loop(
        0, piece_rows // fold_inner_size, visit_block, start_state
    )
    attended_precise = accumulated / row_total[..., None]
    log_total = row_max + jnp.log(row_total)
    attended = (
        jnp.transpose(attended_precise, (2, 0, 1, 3))
        .reshape(tok_rows, heads_here * HEAD_DIM)
        .astype(jnp.bfloat16)
    )
    after_self = rows_in + head_running_total(matmul_t(attended, self_out))
    normed_cross = rms_scale(after_self, ln_cross).astype(jnp.bfloat16)
    cross_queries = matmul(normed_cross, cross_query).astype(jnp.bfloat16)
    share_rows = memory.shape[0] // block_count
    memory_rows = lax.dynamic_slice_in_dim(
        memory, lax.axis_index("blk") * share_rows, share_rows, 0
    )
    memory_keys = matmul(memory, cross_key).astype(jnp.bfloat16)
    memory_values = matmul(memory, cross_value).astype(jnp.bfloat16)
    memory_count = memory.shape[0]
    cross_grid = cross_queries.reshape(tok_rows, groups_here, repeat, HEAD_DIM)
    memory_key_grid = memory_keys.reshape(memory_count, groups_here, HEAD_DIM)
    memory_value_grid = memory_values.reshape(memory_count, groups_here, HEAD_DIM)
    cross_scores = jnp.einsum(
        "tgrd,mgd->grtm", cross_grid, memory_key_grid, preferred_element_type=jnp.float32
    )
    cross_probs = jax.nn.softmax(cross_scores, axis=-1)
    cross_weights = cross_probs.astype(jnp.bfloat16)
    cross_attended = (
        jnp.einsum(
            "grtm,mgd->tgrd", cross_weights, memory_value_grid, preferred_element_type=jnp.float32
        )
        .reshape(tok_rows, heads_here * HEAD_DIM)
        .astype(jnp.bfloat16)
    )
    after_cross = after_self + head_running_total(matmul_t(cross_attended, cross_out))
    normed_ffn = rms_scale(after_cross, ln_ffn).astype(jnp.bfloat16)
    gate_rows = matmul(normed_ffn, ffn_gate)
    upward = matmul(normed_ffn, ffn_up)
    activated, gelu_pull = jax.vjp(
        lambda gate_arg, up_arg: jax.nn.gelu(gate_arg, approximate=True) * up_arg, gate_rows, upward
    )
    inner_rows = activated.astype(jnp.bfloat16)
    final_rows = after_cross + head_running_total(matmul_t(inner_rows, feedforward_down_weight))
    positions = query_first + jnp.arange(tok_rows, dtype=jnp.int32)
    final_grad = out_grad.astype(jnp.float32) * (positions < length).astype(jnp.float32)[:, None]
    ffn_branch_grad = final_grad.astype(jnp.bfloat16)
    grad_ffn_down = matmul_tn(ffn_branch_grad, inner_rows)
    inner_grad = matmul(ffn_branch_grad, feedforward_down_weight)
    gate_grad, up_grad = gelu_pull(inner_grad)
    gate_grad = gate_grad.astype(jnp.bfloat16)
    up_grad = up_grad.astype(jnp.bfloat16)
    grad_ffn_gate = matmul_tn(normed_ffn, gate_grad)
    grad_ffn_up = matmul_tn(normed_ffn, up_grad)
    normed_grad = head_running_total(matmul_t(gate_grad, ffn_gate) + matmul_t(up_grad, ffn_up))
    norm_part, grad_ln_ffn = rms_back(after_cross, ln_ffn, normed_grad)
    cross_cot = final_grad + norm_part
    cross_branch_grad = cross_cot.astype(jnp.bfloat16)
    grad_cross_out = matmul_tn(cross_branch_grad, cross_attended)
    cross_attended_grad = matmul(cross_branch_grad, cross_out).astype(jnp.bfloat16)
    cross_att_grid = cross_attended_grad.reshape(tok_rows, groups_here, repeat, HEAD_DIM)
    cross_prob_grad = jnp.einsum(
        "tgrd,mgd->grtm", cross_att_grid, memory_value_grid, preferred_element_type=jnp.float32
    )
    cross_delta = jnp.sum(cross_probs * cross_prob_grad, axis=-1, keepdims=True)
    cross_score_grad = (cross_probs * (cross_prob_grad - cross_delta)).astype(jnp.bfloat16)
    cross_query_grad = (
        jnp.einsum(
            "grtm,mgd->tgrd", cross_score_grad, memory_key_grid, preferred_element_type=jnp.float32
        )
        .reshape(tok_rows, heads_here * HEAD_DIM)
        .astype(jnp.bfloat16)
    )
    memory_key_part = jnp.einsum(
        "grtm,tgrd->mgd", cross_score_grad, cross_grid, preferred_element_type=jnp.float32
    ).reshape(memory_count, groups_here * HEAD_DIM)
    memory_value_part = jnp.einsum(
        "grtm,tgrd->mgd", cross_weights, cross_att_grid, preferred_element_type=jnp.float32
    ).reshape(memory_count, groups_here * HEAD_DIM)
    memory_key_sum, memory_value_sum = (
        lax.psum_scatter(
            memory_key_part.astype(jnp.bfloat16), "blk", scatter_dimension=0, tiled=True
        ).astype(jnp.float32),
        lax.psum_scatter(
            memory_value_part.astype(jnp.bfloat16), "blk", scatter_dimension=0, tiled=True
        ).astype(jnp.float32),
    )
    memory_key_grad = memory_key_sum.astype(jnp.bfloat16)
    memory_value_grad = memory_value_sum.astype(jnp.bfloat16)
    grad_cross_key = matmul_tn(memory_rows, memory_key_grad)
    grad_cross_value = matmul_tn(memory_rows, memory_value_grad)
    memory_grad = lax.psum_scatter(
        (matmul_t(memory_key_grad, cross_key) + matmul_t(memory_value_grad, cross_value)).astype(
            jnp.bfloat16
        ),
        "head",
        scatter_dimension=0,
        tiled=True,
    ).astype(jnp.float32)
    grad_cross_query = matmul_tn(normed_cross, cross_query_grad)
    normed_grad = head_running_total(matmul_t(cross_query_grad, cross_query))
    norm_part, grad_ln_cross = rms_back(after_self, ln_cross, normed_grad)
    self_cot = cross_cot + norm_part
    self_branch_grad = self_cot.astype(jnp.bfloat16)
    grad_self_out = matmul_tn(self_branch_grad, attended)
    attended_grad = matmul(self_branch_grad, self_out).astype(jnp.bfloat16)
    attended_gradient_matrix = attended_grad.reshape(tok_rows, groups_here, repeat, HEAD_DIM)
    row_delta_terms = jnp.einsum(
        "cskq,skcq->skc", attended_gradient_matrix.astype(jnp.float32), attended_precise
    )
    all_keys, all_values = (
        lax.all_gather(key_rows, "blk", axis=0, tiled=True),
        lax.all_gather(value_rows, "blk", axis=0, tiled=True),
    )
    inner_size = block_rows(seq_rows, 1024)

    def visit_keys(block_index, current):
        query_acc, key_acc, value_acc, bias_acc = current
        block_first = block_index * inner_size
        key_block = lax.dynamic_slice_in_dim(all_keys, block_first, inner_size, 0)
        value_block = lax.dynamic_slice_in_dim(all_values, block_first, inner_size, 0)
        scores, allowed, one_hot = score_block(
            query_matrix, key_block, query_first, block_first, length, rel_bias
        )
        self_probs = jnp.where(allowed, jnp.exp(scores - log_total[..., None]), 0.0)
        key_grid = key_block.reshape(inner_size, groups_here, HEAD_DIM)
        value_grid = value_block.reshape(inner_size, groups_here, HEAD_DIM)
        prob_grad = jnp.einsum(
            "tgrd,pgd->grtp",
            attended_gradient_matrix,
            value_grid,
            preferred_element_type=jnp.float32,
        )
        score_grad = (self_probs * (prob_grad - row_delta_terms[..., None])).astype(jnp.bfloat16)
        query_acc = query_acc + jnp.einsum(
            "grtp,pgd->grtd", score_grad, key_grid, preferred_element_type=jnp.float32
        )
        key_part = jnp.einsum(
            "grtp,tgrd->pgd", score_grad, query_matrix, preferred_element_type=jnp.float32
        ).reshape(inner_size, groups_here * HEAD_DIM)
        value_part = jnp.einsum(
            "grtp,tgrd->pgd",
            self_probs.astype(jnp.bfloat16),
            attended_gradient_matrix,
            preferred_element_type=jnp.float32,
        ).reshape(inner_size, groups_here * HEAD_DIM)
        key_acc = lax.dynamic_update_slice_in_dim(key_acc, key_part, block_first, 0)
        value_acc = lax.dynamic_update_slice_in_dim(value_acc, value_part, block_first, 0)
        line_grad = diagonal_sums(
            score_grad.astype(jnp.float32).reshape(heads_here, tok_rows, inner_size),
            tok_rows + inner_size - 1,
        )
        bias_acc = bias_acc + jnp.dot(line_grad, one_hot, precision=HIGHEST)
        return (query_acc, key_acc, value_acc, bias_acc)

    query_acc, key_acc, value_acc, bias_part = lax.fori_loop(
        0,
        seq_rows // inner_size,
        visit_keys,
        (
            jnp.zeros((groups_here, repeat, tok_rows, HEAD_DIM), jnp.float32),
            jnp.zeros((seq_rows, groups_here * HEAD_DIM), jnp.float32),
            jnp.zeros((seq_rows, groups_here * HEAD_DIM), jnp.float32),
            jnp.zeros((heads_here, BUCKETS), jnp.float32),
        ),
    )
    key_sum, value_sum = (
        lax.psum_scatter(
            key_acc.astype(jnp.bfloat16), "blk", scatter_dimension=0, tiled=True
        ).astype(jnp.float32),
        lax.psum_scatter(
            value_acc.astype(jnp.bfloat16), "blk", scatter_dimension=0, tiled=True
        ).astype(jnp.float32),
    )
    key_grad = key_sum.astype(jnp.bfloat16)
    value_grad = value_sum.astype(jnp.bfloat16)
    query_grad = (
        jnp.transpose(query_acc, (2, 0, 1, 3))
        .reshape(tok_rows, heads_here * HEAD_DIM)
        .astype(jnp.bfloat16)
    )
    grad_self_query = matmul_tn(normed_self, query_grad)
    grad_self_key = matmul_tn(normed_self, key_grad)
    grad_self_value = matmul_tn(normed_self, value_grad)
    normed_grad = head_running_total(
        matmul_t(query_grad, self_query)
        + matmul_t(key_grad, self_key)
        + matmul_t(value_grad, self_value)
    )
    norm_part, grad_ln_self = rms_back(rows_in, ln_self, normed_grad)
    hidden_grad = self_cot + norm_part
    gradient_sums = (
        lax.psum_scatter(grad_ln_self, ("seq", "blk"), scatter_dimension=0, tiled=True),
        lax.psum_scatter(grad_self_query, ("seq", "blk"), scatter_dimension=0, tiled=True),
        lax.psum_scatter(grad_self_key, ("seq", "blk"), scatter_dimension=0, tiled=True),
        lax.psum_scatter(grad_self_value, ("seq", "blk"), scatter_dimension=0, tiled=True),
        lax.psum_scatter(grad_self_out, ("seq", "blk"), scatter_dimension=0, tiled=True),
        lax.psum_scatter(grad_ln_cross, ("seq", "blk"), scatter_dimension=0, tiled=True),
        lax.psum_scatter(grad_cross_query, ("seq", "blk"), scatter_dimension=0, tiled=True),
        lax.psum_scatter(grad_cross_key, ("seq", "blk"), scatter_dimension=0, tiled=True),
        lax.psum_scatter(grad_cross_value, ("seq", "blk"), scatter_dimension=0, tiled=True),
        lax.psum_scatter(grad_cross_out, ("seq", "blk"), scatter_dimension=0, tiled=True),
        lax.psum_scatter(grad_ln_ffn, ("seq", "blk"), scatter_dimension=0, tiled=True),
        lax.psum_scatter(grad_ffn_gate, ("seq", "blk"), scatter_dimension=0, tiled=True),
        lax.psum_scatter(grad_ffn_up, ("seq", "blk"), scatter_dimension=0, tiled=True),
        lax.psum_scatter(grad_ffn_down, ("seq", "blk"), scatter_dimension=0, tiled=True),
    )
    bias_total = lax.psum(bias_part.T, ("seq", "blk"))
    return (
        final_rows.astype(jnp.bfloat16),
        hidden_grad,
        memory_grad,
        gradient_sums[0],
        gradient_sums[1],
        gradient_sums[2],
        gradient_sums[3],
        gradient_sums[4],
        bias_total,
        gradient_sums[5],
        gradient_sums[6],
        gradient_sums[7],
        gradient_sums[8],
        gradient_sums[9],
        gradient_sums[10],
        gradient_sums[11],
        gradient_sums[12],
        gradient_sums[13],
    )


def solution(mesh):
    in_specs = (
        P(("seq", "blk"), None),
        P("seq", None),
        P("seq"),
        P(("seq", "blk"), None),
        P(),
        P(None, "head"),
        P(None, "head"),
        P(None, "head"),
        P(None, "head"),
        P(None, "head"),
        P(),
        P(None, "head"),
        P(None, "head"),
        P(None, "head"),
        P(None, "head"),
        P(),
        P(None, "head"),
        P(None, "head"),
        P(None, "head"),
    )
    out_specs = (
        P(("seq", "blk"), None),
        P(("seq", "blk"), None),
        P(("seq", "blk", "head"), None),
        P(("seq", "blk")),
        P(("seq", "blk"), "head"),
        P(("seq", "blk"), "head"),
        P(("seq", "blk"), "head"),
        P(("seq", "blk"), "head"),
        P(None, "head"),
        P(("seq", "blk")),
        P(("seq", "blk"), "head"),
        P(("seq", "blk"), "head"),
        P(("seq", "blk"), "head"),
        P(("seq", "blk"), "head"),
        P(("seq", "blk")),
        P(("seq", "blk"), "head"),
        P(("seq", "blk"), "head"),
        P(("seq", "blk"), "head"),
    )
    return jax.shard_map(body, mesh=mesh, in_specs=in_specs, out_specs=out_specs, check_vma=False)
```

profile of v0, /device:TPU:0, one launch (start us, length us, event | category | flops | bytes accessed | tf_op | source)
XLA Modules:
  0.0 1332.4 jit_solution(3604391181026458274)
XLA Ops:
  12.5 35.2 %all_gather.8 = bf16[1024,256]{1,0:T(8,128)(2,1)} all-gather(bf16[128,256]{1,0:T(8,128)(2,1)S(1)} %convolution_convert_fusion.14), channel_id=1, replica_groups=mesh['seq'=2,'blk'=8,'head'=2] {'blk'}, dimensions={0}, use_global_device_ids=true | all-gather | bytes 589824 | tf_op jit(solution)/shard_map/all_gather | solution.py:148
  50.2 2.6 tile.24
  52.8 5.9 tile.25
  58.7 4.6 slice.14
  63.3 9.3 reshape.246
  72.6 4.8 slice.15
  77.4 5.3 copy.75
  82.9 3.2 select_reduce_fusion
  89.7 33.4 %all_gather.9 = bf16[1024,256]{1,0:T(8,128)(2,1)} all-gather(bf16[128,256]{1,0:T(8,128)(2,1)S(1)} %convolution_convert_fusion.13), channel_id=1, replica_groups=mesh['seq'=2,'blk'=8,'head'=2] {'blk'}, dimensions={0}, use_global_device_ids=true | all-gather | bytes 589824 | tf_op jit(solution)/shard_map/all_gather | solution.py:149
  125.2 3.9 fusion.76
  132.9 2.6 convolution_convert_fusion.4
  135.5 20.0 %all-reduce.13.cloned.1.call-done = bf16[128,1024]{1,0:T(8,128)(2,1)} async-done(((bf16[128,1024]{1,0:T(8,128)(2,1)}), bf16[128,1024]{1,0:T(8,128)(2,1)}) %all-reduce.13.cloned.1.call-update) | async-done | bytes 262160 | tf_op jit(solution)/shard_map/psum | solution.py:135
  160.7 3.1 fusion.125
  168.9 22.8 %all-reduce.15.cloned.1.call-done = bf16[128,1024]{1,0:T(8,128)(2,1)} async-done(((bf16[128,1024]{1,0:T(8,128)(2,1)}), bf16[128,1024]{1,0:T(8,128)(2,1)}) %all-reduce.15.cloned.1.call-update) | async-done | bytes 262160 | tf_op jit(solution)/shard_map/psum | solution.py:135
  193.9 2.4 fusion.127
  203.0 23.3 %all-reduce.17.cloned.1.call-done = bf16[128,1024]{1,0:T(8,128)(2,1)} async-done(((bf16[128,1024]{1,0:T(8,128)(2,1)}), bf16[128,1024]{1,0:T(8,128)(2,1)}) %all-reduce.17.cloned.1.call-update) | async-done | bytes 262160 | tf_op jit(solution)/shard_map/psum | solution.py:135
  234.3 2.4 fusion.10
  240.2 2.4 fusion.32
  244.6 2.9 fusion.33
  249.5 14.0 %all-reduce.19.cloned.1.call-done = bf16[128,1024]{1,0:T(8,128)(2,1)} async-done(((bf16[128,1024]{1,0:T(8,128)(2,1)}), bf16[128,1024]{1,0:T(8,128)(2,1)}) %all-reduce.19.cloned.1.call-update) | async-done | bytes 262160 | tf_op jit(solution)/shard_map/psum | solution.py:135
  271.0 3.8 fusion.2
  279.8 3.8 fusion.27
  285.7 2.9 convolution_convert_fusion.1
  289.1 38.8 %reduce-scatter.53.cloned.1.call-done = bf16[64,256]{1,0:T(8,128)(2,1)} async-done(((bf16[512,256]{1,0:T(8,128)(2,1)}), bf16[64,256]{1,0:T(8,128)(2,1)}) %reduce-scatter.53.cloned.1.call-update) | async-done | bytes 32784
  329.0 62.4 %reduce-scatter.55.cloned.1.call-done = bf16[64,256]{1,0:T(8,128)(2,1)} async-done(((bf16[512,256]{1,0:T(8,128)(2,1)}), bf16[64,256]{1,0:T(8,128)(2,1)}) %reduce-scatter.55.cloned.1.call-update) | async-done | bytes 32784
  393.2 62.5 %reduce-scatter.49.cloned.1.call-done = bf16[128,256]{1,0:T(8,128)(2,1)} async-done(((bf16[1024,256]{1,0:T(8,128)(2,1)}), bf16[128,256]{1,0:T(8,128)(2,1)}) %reduce-scatter.49.cloned.1.call-update) | async-done | bytes 65552
  457.1 63.2 %reduce-scatter.51.cloned.1.call-done = bf16[128,256]{1,0:T(8,128)(2,1)} async-done(((bf16[1024,256]{1,0:T(8,128)(2,1)}), bf16[128,256]{1,0:T(8,128)(2,1)}) %reduce-scatter.51.cloned.1.call-update) | async-done | bytes 65552
  538.3 3.5 fusion.89
  542.7 3.5 fusion.133
  548.1 3.4 fusion.132
  553.1 2.6 copy.88
  557.6 5.9 reshape.283
  563.5 4.1 reshape.255
  567.7 2.9 pad_convert_fusion
  570.5 7.8 reshape.259
  578.3 2.9 reduce_sum.144
  584.5 58.9 %all-reduce.5 = (f32[1024]{0:T(1024)S(1)}, f32[32,8]{0,1:T(8,128)}, f32[1024]{0:T(1024)S(1)}, f32[1024]{0:T(1024)S(1)}) all-reduce(f32[1024]{0:T(1024)S(1)} %get-tuple-element.85, f32[32,8]{0,1:T(8,128)S(1)} %fusion.52, f32[1024]{0:T(1024)S(1)} %get-tuple-element.83, ...), channel_id=7, replica_groups=mesh['seq'=2,'blk'=8,'head'=2] {'seq','blk'}, use_global_device_ids=true, to_apply=%region_23.24.clone | all-reduce | flops 3328 | bytes 26624
  645.1 2.5 fusion.54
  647.6 39.1 %reduce-scatter.37.cloned.1.call-done = f32[64,256]{1,0:T(8,128)} async-done(((f32[1024,256]{1,0:T(8,128)}), f32[64,256]{1,0:T(8,128)}) %reduce-scatter.37.cloned.1.call-update) | async-done | bytes 65552 | tf_op jit(solution)/shard_map/reduce_scatter | solution.py:381
  686.7 61.0 %reduce-scatter.31.cloned.1.call-done = f32[64,256]{1,0:T(8,128)} async-done(((f32[1024,256]{1,0:T(8,128)}), f32[64,256]{1,0:T(8,128)}) %reduce-scatter.31.cloned.1.call-update) | async-done | bytes 65552 | tf_op jit(solution)/shard_map/reduce_scatter | solution.py:377
  747.7 60.5 %reduce-scatter.29.cloned.1.call-done = f32[64,256]{1,0:T(8,128)} async-done(((f32[1024,256]{1,0:T(8,128)}), f32[64,256]{1,0:T(8,128)}) %reduce-scatter.29.cloned.1.call-update) | async-done | bytes 65552 | tf_op jit(solution)/shard_map/reduce_scatter | solution.py:376
  808.2 65.3 %reduce-scatter.41.cloned.1.call-done = f32[64,512]{1,0:T(8,128)} async-done(((f32[1024,512]{1,0:T(8,128)}), f32[64,512]{1,0:T(8,128)}) %reduce-scatter.41.cloned.1.call-update) | async-done | bytes 131088 | tf_op jit(solution)/shard_map/reduce_scatter | solution.py:383
  873.5 64.8 %reduce-scatter.35.cloned.1.call-done = f32[64,512]{1,0:T(8,128)} async-done(((f32[1024,512]{1,0:T(8,128)}), f32[64,512]{1,0:T(8,128)}) %reduce-scatter.35.cloned.1.call-update) | async-done | bytes 131088 | tf_op jit(solution)/shard_map/reduce_scatter | solution.py:380
  938.3 65.2 %reduce-scatter.33.cloned.1.call-done = f32[64,512]{1,0:T(8,128)} async-done(((f32[1024,512]{1,0:T(8,128)}), f32[64,512]{1,0:T(8,128)}) %reduce-scatter.33.cloned.1.call-update) | async-done | bytes 131088 | tf_op jit(solution)/shard_map/reduce_scatter | solution.py:378
  1003.5 64.8 %reduce-scatter.27.cloned.1.call-done = f32[64,512]{1,0:T(8,128)} async-done(((f32[1024,512]{1,0:T(8,128)}), f32[64,512]{1,0:T(8,128)}) %reduce-scatter.27.cloned.1.call-update) | async-done | bytes 131088 | tf_op jit(solution)/shard_map/reduce_scatter | solution.py:375
  1068.3 85.6 %reduce-scatter.47.cloned.1.call-done = f32[64,1408]{1,0:T(8,128)} async-done(((f32[1024,1408]{1,0:T(8,128)}), f32[64,1408]{1,0:T(8,128)}) %reduce-scatter.47.cloned.1.call-update) | async-done | bytes 360464 | tf_op jit(solution)/shard_map/reduce_scatter | solution.py:387
  1153.8 85.5 %reduce-scatter.45.cloned.1.call-done = f32[64,1408]{1,0:T(8,128)} async-done(((f32[1024,1408]{1,0:T(8,128)}), f32[64,1408]{1,0:T(8,128)}) %reduce-scatter.45.cloned.1.call-update) | async-done | bytes 360464 | tf_op jit(solution)/shard_map/reduce_scatter | solution.py:386
  1239.4 85.7 %reduce-scatter.43.cloned.1.call-done = f32[64,1408]{1,0:T(8,128)} async-done(((f32[1024,1408]{1,0:T(8,128)}), f32[64,1408]{1,0:T(8,128)}) %reduce-scatter.43.cloned.1.call-update) | async-done | bytes 360464 | tf_op jit(solution)/shard_map/reduce_scatter | solution.py:385
  (246 shorter events, 98.4 us)
Async XLA Ops:
  7.2 189.8 %copy-start = (bf16[1024,1408]{1,0:T(8,128)(2,1)S(1)}, bf16[1024,1408]{1,0:T(8,128)(2,1)}, u32[]{:S(2)}) copy-start(bf16[1024,1408]{1,0:T(8,128)(2,1)} %param.37) | copy-start | bytes 8650756
  7.2 42.5 %copy-start.61 = (f32[32,8]{0,1:T(8,128)S(1)}, f32[32,8]{0,1:T(8,128)}, u32[]{:S(2)}) copy-start(f32[32,8]{0,1:T(8,128)} %param.28) | copy-start | bytes 3076
  7.2 148.3 %all-reduce.13.cloned.1.call-start = ((), (), s32[]{:S(2)}) async-start(), calls=%async_computation.16 | async-start | bytes 524288 | tf_op jit(solution)/shard_map/psum | solution.py:135
  9.2 43.6 %copy-start.56 = (s32[1151]{0:T(1024)}, s32[1151]{0:T(1024)S(1)}, u32[]{:S(2)}) copy-start(s32[1151]{0:T(1024)S(1)} %convert_add_fusion.2) | copy-start | bytes 13816
  12.5 70.4 %copy-start.35 = (bf16[128,512]{0,1:T(8,128)(2,1)}, bf16[128,512]{0,1:T(8,128)(2,1)S(1)}, u32[]{:S(2)}) copy-start(bf16[128,512]{0,1:T(8,128)(2,1)S(1)} %copy.74) | copy-start | bytes 393220
  86.1 3.3 copy-start.2
  86.1 3.3 copy-start.39
  86.1 3.3 copy-start.46
  125.2 4.6 copy-start.22
  129.7 26.9 %copy-start.49 = (f32[1024]{0:T(1024)S(1)}, f32[1024]{0:T(1024)}, u32[]{:S(2)}) copy-start(f32[1024]{0:T(1024)} %param.29) | copy-start | bytes 12292
  130.9 60.7 %all-reduce.15.cloned.1.call-start = ((), (), s32[]{:S(2)}) async-start(), calls=%async_computation.17 | async-start | bytes 524288 | tf_op jit(solution)/shard_map/psum | solution.py:135
  132.8 30.9 %copy-start.24 = (bf16[512,256]{0,1:T(8,128)(2,1)}, bf16[512,256]{0,1:T(8,128)(2,1)S(1)}, u32[]{:S(2)}) copy-start(bf16[512,256]{0,1:T(8,128)(2,1)S(1)} %convolution_convert_fusion.3) | copy-start | bytes 786436
  156.7 4.0 copy-start.54
  164.4 27.3 %copy-start.10 = (bf16[128,1024]{1,0:T(8,128)(2,1)S(1)}, bf16[128,1024]{1,0:T(8,128)(2,1)}, u32[]{:S(2)}) copy-start(bf16[128,1024]{1,0:T(8,128)(2,1)} %all-reduce.13.cloned.1.call-done) | copy-start | bytes 786436
  166.5 27.4 %copy-start.50 = (f32[1024]{0:T(1024)S(1)}, f32[1024]{0:T(1024)}, u32[]{:S(2)}) copy-start(f32[1024]{0:T(1024)} %param.34) | copy-start | bytes 12292
  168.3 58.0 %all-reduce.17.cloned.1.call-start = ((), (), s32[]{:S(2)}) async-start(), calls=%async_computation.18 | async-start | bytes 524288 | tf_op jit(solution)/shard_map/psum | solution.py:135
  191.7 4.7 copy-start.8
  202.9 60.6 %all-reduce.19.cloned.1.call-start = ((), (), s32[]{:S(2)}) async-start(), calls=%async_computation.19 | async-start | bytes 524288 | tf_op jit(solution)/shard_map/psum | solution.py:135
  240.2 87.8 %reduce-scatter.53.cloned.1.call-start = ((), (), s32[]{:S(2)}) async-start(), calls=%async_computation.34 | async-start | bytes 294912
  244.5 146.9 %reduce-scatter.55.cloned.1.call-start = ((), (), s32[]{:S(2)}) async-start(), calls=%async_computation.35 | async-start | bytes 294912
  249.3 206.4 %reduce-scatter.49.cloned.1.call-start = ((), (), s32[]{:S(2)}) async-start(), calls=%async_computation.32 | async-start | bytes 589824
  263.5 3.7 copy-start.23
  271.0 5.1 copy-start.36
  279.7 240.6 %reduce-scatter.51.cloned.1.call-start = ((), (), s32[]{:S(2)}) async-start(), calls=%async_computation.33 | async-start | bytes 589824
  285.7 296.1 %reduce-scatter.25.cloned.1.call-start = ((), (), s32[]{:S(2)}) async-start(), calls=%async_computation.20 | async-start | bytes 196608 | tf_op jit(solution)/shard_map/reduce_scatter | solution.py:273
  288.6 39.3 %copy-start.26 = (bf16[1024,256]{1,0:T(8,128)(2,1)S(1)}, bf16[1024,256]{1,0:T(8,128)(2,1)}, u32[]{:S(2)}) copy-start(bf16[1024,256]{1,0:T(8,128)(2,1)} %param.31) | copy-start | bytes 1572868
  288.6 102.8 %copy-start.27 = (bf16[1024,256]{1,0:T(8,128)(2,1)S(1)}, bf16[1024,256]{1,0:T(8,128)(2,1)}, u32[]{:S(2)}) copy-start(bf16[1024,256]{1,0:T(8,128)(2,1)} %param.32) | copy-start | bytes 1572868
  288.6 233.1 %copy-start.20 = (bf16[1024,512]{1,0:T(8,128)(2,1)S(1)}, bf16[1024,512]{1,0:T(8,128)(2,1)}, u32[]{:S(2)}) copy-start(bf16[1024,512]{1,0:T(8,128)(2,1)} %param.24) | copy-start | bytes 3145732
  393.1 129.8 %copy-start.48 = (bf16[64,256]{1,0:T(8,128)(2,1)S(1)}, bf16[64,256]{1,0:T(8,128)(2,1)}, u32[]{:S(2)}) copy-start(bf16[64,256]{1,0:T(8,128)(2,1)} %reduce-scatter.55.cloned.1.call-done) | copy-start | bytes 98308
  393.2 190.1 %all-reduce.21.cloned.1.call-start = ((), (), s32[]{:S(2)}) async-start(), calls=%async_computation.36 | async-start | bytes 1048576 | tf_op jit(solution)/shard_map/psum | solution.py:135
  521.7 3.6 copy-start.47
  522.9 4.7 copy-start.45
  522.9 124.7 %reduce-scatter.39.cloned.1.call-start = ((), (), s32[]{:S(2)}) async-start(), calls=%async_computation.27 | async-start | bytes 1114112 | tf_op jit(solution)/shard_map/reduce_scatter | solution.py:382
  525.2 3.9 copy-start.44
  525.2 161.5 %reduce-scatter.37.cloned.1.call-start = ((), (), s32[]{:S(2)}) async-start(), calls=%async_computation.26 | async-start | bytes 1114112 | tf_op jit(solution)/shard_map/reduce_scatter | solution.py:381
  527.6 3.0 copy-start.17
  527.6 3.0 copy-start.43
  527.6 220.1 %reduce-scatter.31.cloned.1.call-start = ((), (), s32[]{:S(2)}) async-start(), calls=%async_computation.23 | async-start | bytes 1114112 | tf_op jit(solution)/shard_map/reduce_scatter | solution.py:377
  529.1 279.1 %reduce-scatter.29.cloned.1.call-start = ((), (), s32[]{:S(2)}) async-start(), calls=%async_computation.22 | async-start | bytes 1114112 | tf_op jit(solution)/shard_map/reduce_scatter | solution.py:376
  530.5 343.0 %reduce-scatter.41.cloned.1.call-start = ((), (), s32[]{:S(2)}) async-start(), calls=%async_computation.28 | async-start | bytes 2228224 | tf_op jit(solution)/shard_map/reduce_scatter | solution.py:383
  532.4 405.9 %reduce-scatter.35.cloned.1.call-start = ((), (), s32[]{:S(2)}) async-start(), calls=%async_computation.25 | async-start | bytes 2228224 | tf_op jit(solution)/shard_map/reduce_scatter | solution.py:380
  534.4 469.1 %reduce-scatter.33.cloned.1.call-start = ((), (), s32[]{:S(2)}) async-start(), calls=%async_computation.24 | async-start | bytes 2228224 | tf_op jit(solution)/shard_map/reduce_scatter | solution.py:378
  536.3 532.0 %reduce-scatter.27.cloned.1.call-start = ((), (), s32[]{:S(2)}) async-start(), calls=%async_computation.21 | async-start | bytes 2228224 | tf_op jit(solution)/shard_map/reduce_scatter | solution.py:375
  538.2 615.6 %reduce-scatter.47.cloned.1.call-start = ((), (), s32[]{:S(2)}) async-start(), calls=%async_computation.31 | async-start | bytes 6127616 | tf_op jit(solution)/shard_map/reduce_scatter | solution.py:387
  541.8 697.6 %reduce-scatter.45.cloned.1.call-start = ((), (), s32[]{:S(2)}) async-start(), calls=%async_computation.30 | async-start | bytes 6127616 | tf_op jit(solution)/shard_map/reduce_scatter | solution.py:386
  546.2 778.9 %reduce-scatter.43.cloned.1.call-start = ((), (), s32[]{:S(2)}) async-start(), calls=%async_computation.29 | async-start | bytes 6127616 | tf_op jit(solution)/shard_map/reduce_scatter | solution.py:385
  578.3 6.1 copy-start.53
  578.3 746.7 %copy-start.1 = (bf16[1024,1408]{1,0:T(8,128)(2,1)S(1)}, bf16[1024,1408]{1,0:T(8,128)(2,1)}, u32[]{:S(2)}) copy-start(bf16[1024,1408]{1,0:T(8,128)(2,1)} %param.37) | copy-start | bytes 8650756
  (36 other events, 57.3 us)
Sparse Core Ops, SparseCore 0:
  131.1 24.4 all-reduce.12
  168.4 23.1 all-reduce.14
  203.1 23.1 all-reduce.16
  240.3 23.1 all-reduce.18
  266.7 61.2 reduce-scatter.52
  331.1 60.2 reduce-scatter.54
  394.8 60.8 reduce-scatter.48
  459.4 60.8 reduce-scatter.50
  523.1 9.2 reduce-scatter.24
  535.2 28.7 all-reduce.20
  568.7 57.4 reduce-scatter.38
  630.2 56.5 reduce-scatter.36
  691.3 56.3 reduce-scatter.30
  751.7 56.3 reduce-scatter.28
  812.8 60.6 reduce-scatter.40
  877.7 60.5 reduce-scatter.34
  942.9 60.5 reduce-scatter.32
  1007.6 60.5 reduce-scatter.26
  1073.2 80.5 reduce-scatter.46
  1158.6 80.6 reduce-scatter.44
  1244.3 80.6 reduce-scatter.42
where the time goes:
time: 1340 us; the launch traced here: 1330 us
  waiting for transfers between devices  985 us (74%)
  blocking collectives  127 us (9%)
  matrix products  89.7 us (7%)
  local copies, waits for them, and re-layouts  87.5 us (7%)
  other arithmetic  24.5 us (2%)
  between operations  17.1 us (1%)
    unnamed x25, waiting for transfers between devices  227 us
    reduce_scatter x1, waiting for transfers between devices, body(): lax.psum_scatter(grad_ffn_gate, ('seq', 'blk'), scatter_dimension=0, tile...  85.7 us
    reduce_scatter x1, waiting for transfers between devices, body(): lax.psum_scatter(grad_ffn_down, ('seq', 'blk'), scatter_dimension=0, tile...  85.6 us
    reduce_scatter x1, waiting for transfers between devices, body(): lax.psum_scatter(grad_ffn_up, ('seq', 'blk'), scatter_dimension=0, tiled=...  85.5 us
    psum x5, waiting for transfers between devices, head_running_total(): lax.psum(partial_sum.astype(jnp.bfloat16), 'head').astype(jnp.float32)  80.1 us
    reduce_scatter x1, waiting for transfers between devices, body(): lax.psum_scatter(grad_cross_out, ('seq', 'blk'), scatter_dimension=0, til...  65.3 us
    reduce_scatter x1, waiting for transfers between devices, body(): lax.psum_scatter(grad_self_out, ('seq', 'blk'), scatter_dimension=0, tile...  65.2 us
    reduce_scatter x1, waiting for transfers between devices, body(): lax.psum_scatter(grad_self_query, ('seq', 'blk'), scatter_dimension=0, ti...  64.8 us
  transfers between devices with their start and end apart: 21, of which 18 were waited for; matrix products, arithmetic and copies ran while one was open for 8% of the time, Pallas kernels for 0%

commit v1 on v0

--- a/solution.py
+++ b/solution.py
@@ -1,8 +1,14 @@
+import functools
+
 import jax
 import jax.numpy as jnp
 import numpy as np
 from jax import lax
+from jax.experimental import pallas as pl
+from jax.experimental.pallas import tpu as pltpu
 from jax.sharding import PartitionSpec as P
+
+MESH = pl.DeviceIdType.MESH
 
 HEAD_DIM = 64
 BUCKETS = 32
@@ -46,6 +52,143 @@
     return lax.dot_general(
         left, right, (((0,), (0,)), ((), ())), preferred_element_type=jnp.float32
     )
+
+
+def blk_bits(blk_count):
+    return blk_count.bit_length() - 1
+
+
+def reduce_kernel(bits, widths, small_shape, *refs):
+    count = len(widths)
+    parts = refs[:count]
+    small_in = refs[count]
+    outs = refs[count + 1 : 2 * count + 1]
+    small_out = refs[2 * count + 1]
+    rest = refs[2 * count + 2 :]
+    stages = bits + 1
+    landing = [rest[piece * stages : (piece + 1) * stages] for piece in range(count)]
+    small_land, small_acc, send_sem, recv_sem, small_send, small_recv = rest[count * stages :]
+    seq, blk, head = (lax.axis_index(name) for name in ("seq", "blk", "head"))
+    my_bits = [lax.rem(blk // (1 << bit), 2) for bit in range(bits)]
+
+    def partner(stage):
+        if stage == 0:
+            return (1 - seq, blk, head)
+        bit = stage - 1
+        return (seq, blk + (1 - 2 * my_bits[bit]) * (1 << bit), head)
+
+    barrier = pltpu.get_barrier_semaphore()
+    for stage in range(stages):
+        pl.semaphore_signal(barrier, inc=1, device_id=partner(stage), device_id_type=MESH)
+    pl.semaphore_wait(barrier, stages)
+
+    def view(ref, stage, mine):
+        if stage == 0:
+            return ref.at[seq if mine else 1 - seq]
+        index = [seq]
+        for bit in reversed(range(bits)):
+            if bit < stage - 1:
+                index.append(my_bits[bit])
+            elif bit == stage - 1:
+                index.append(my_bits[bit] if mine else 1 - my_bits[bit])
+            else:
+                index.append(slice(None))
+        return ref.at[tuple(index)]
+
+    def copy_of(piece, stage):
+        return pltpu.make_async_remote_copy(
+            src_ref=view(parts[piece], stage, False),
+            dst_ref=landing[piece][stage],
+            send_sem=send_sem.at[piece, stage],
+            recv_sem=recv_sem.at[piece, stage],
+            device_id=partner(stage),
+            device_id_type=MESH,
+        )
+
+    def fold(piece, stage):
+        mine = view(parts[piece], stage, True)
+        got = landing[piece][stage]
+        if stage == stages - 1:
+            outs[piece][...] = mine[...].astype(jnp.float32) + got[...].astype(jnp.float32)
+            return
+        lead = got.shape[:-2]
+        total = int(np.prod(lead))
+        for flat in range(total):
+            index = tuple(int(value) for value in np.unravel_index(flat, lead))
+            mine[index] = (
+                mine[index].astype(jnp.float32) + got[index].astype(jnp.float32)
+            ).astype(jnp.bfloat16)
+
+    def small_copy(stage):
+        return pltpu.make_async_remote_copy(
+            src_ref=small_acc.at[stage],
+            dst_ref=small_land.at[stage],
+            send_sem=small_send.at[stage],
+            recv_sem=small_recv.at[stage],
+            device_id=partner(stage),
+            device_id_type=MESH,
+        )
+
+    small_acc[0] = small_in[...]
+    for step in range(count + stages):
+        for stage in reversed(range(stages + 1)):
+            piece = step - stage
+            if not 0 <= piece < count:
+                continue
+            if stage > 0:
+                copy_of(piece, stage - 1).wait_recv()
+                fold(piece, stage - 1)
+            if stage < stages:
+                copy_of(piece, stage).start()
+        if step <= stages:
+            if step > 0:
+                small_copy(step - 1).wait_recv()
+                total = small_acc[step - 1] + small_land[step - 1]
+                if step < stages:
+                    small_acc[step] = total
+                else:
+                    small_out[...] = total
+            if step < stages:
+                small_copy(step).start()
+    for piece in range(count):
+        for stage in range(stages):
+            copy_of(piece, stage).wait_send()
+    for stage in range(stages):
+        small_copy(stage).wait_send()
+
+
+def reduce_gradients(parts, small, blk_count):
+    bits = blk_bits(blk_count)
+    stages = bits + 1
+    rows = parts[0].shape[0] // (2 * blk_count)
+    widths = [part.shape[1] for part in parts]
+    lead = (2,) * (bits + 1)
+    shaped = [part.reshape(*lead, rows, part.shape[1]) for part in parts]
+    scratch = []
+    for width in widths:
+        for stage in range(stages):
+            scratch.append(pltpu.VMEM((2,) * (bits - stage) + (rows, width), jnp.bfloat16))
+    scratch += [
+        pltpu.VMEM((stages, *small.shape), jnp.float32),
+        pltpu.VMEM((stages, *small.shape), jnp.float32),
+        pltpu.SemaphoreType.DMA((len(parts), stages)),
+        pltpu.SemaphoreType.DMA((len(parts), stages)),
+        pltpu.SemaphoreType.DMA((stages,)),
+        pltpu.SemaphoreType.DMA((stages,)),
+    ]
+    vmem = pl.BlockSpec(memory_space=pltpu.VMEM)
+    return pl.pallas_call(
+        functools.partial(reduce_kernel, bits, widths, small.shape),
+        out_shape=[jax.ShapeDtypeStruct((rows, width), jnp.float32) for width in widths]
+        + [jax.ShapeDtypeStruct(small.shape, jnp.float32)],
+        in_specs=[vmem] * (len(parts) + 1),
+        out_specs=[vmem] * (len(parts) + 1),
+        scratch_shapes=scratch,
+        compiler_params=pltpu.CompilerParams(
+            collective_id=0, has_side_effects=True, vmem_limit_bytes=56 * 1024 * 1024
+        ),
+        name="grad_reduce",
+    )(*shaped, small)
 
 
 def rms_scale(values, norm_gain):
@@ -145,8 +288,8 @@
         jnp.zeros((groups_here, repeat, tok_rows, HEAD_DIM), jnp.float32),
     )
     first_row = jnp.int32(0)
-    key_piece = lax.all_gather(key_rows, "blk", axis=0, tiled=True)
-    value_piece = lax.all_gather(value_rows, "blk", axis=0, tiled=True)
+    both = lax.all_gather(jnp.concatenate([key_rows, value_rows], axis=1), "blk", axis=0, tiled=True)
+    key_piece, value_piece = jnp.split(both, 2, axis=1)
     piece_rows = key_piece.shape[0]
     fold_inner_size = block_rows(piece_rows, 1024)
 
@@ -289,10 +432,7 @@
     row_delta_terms = jnp.einsum(
         "cskq,skcq->skc", attended_gradient_matrix.astype(jnp.float32), attended_precise
     )
-    all_keys, all_values = (
-        lax.all_gather(key_rows, "blk", axis=0, tiled=True),
-        lax.all_gather(value_rows, "blk", axis=0, tiled=True),
-    )
+    all_keys, all_values = key_piece, value_piece
     inner_size = block_rows(seq_rows, 1024)
 
     def visit_keys(block_index, current):
@@ -370,23 +510,27 @@
     )
     norm_part, grad_ln_self = rms_back(rows_in, ln_self, normed_grad)
     hidden_grad = self_cot + norm_part
+    big = [
+        grad_ffn_gate, grad_ffn_up, grad_ffn_down, grad_cross_out, grad_cross_query,
+        grad_cross_key, grad_cross_value, grad_self_out, grad_self_query, grad_self_key,
+        grad_self_value,
+    ]
+    width = ln_self.shape[0]
+    bias_flat = bias_part.reshape(-1)
+    small = jnp.stack(
+        [grad_ln_self, grad_ln_cross, grad_ln_ffn, jnp.pad(bias_flat, (0, width - bias_flat.size))]
+        + [jnp.zeros_like(grad_ln_self)] * 4
+    )
+    sums = reduce_gradients([part.astype(jnp.bfloat16) for part in big], small, block_count)
+    small_sum = sums[-1]
+    share = width // (lax.axis_size("seq") * block_count)
+    first = (lax.axis_index("seq") * block_count + lax.axis_index("blk")) * share
+    ln_sums = lax.dynamic_slice(small_sum, (0, first), (3, share))
+    bias_total = small_sum[3, : bias_flat.size].reshape(heads_here, BUCKETS).T
     gradient_sums = (
-        lax.psum_scatter(grad_ln_self, ("seq", "blk"), scatter_dimension=0, tiled=True),
-        lax.psum_scatter(grad_self_query, ("seq", "blk"), scatter_dimension=0, tiled=True),
-        lax.psum_scatter(grad_self_key, ("seq", "blk"), scatter_dimension=0, tiled=True),
-        lax.psum_scatter(grad_self_value, ("seq", "blk"), scatter_dimension=0, tiled=True),
-        lax.psum_scatter(grad_self_out, ("seq", "blk"), scatter_dimension=0, tiled=True),
-        lax.psum_scatter(grad_ln_cross, ("seq", "blk"), scatter_dimension=0, tiled=True),
-        lax.psum_scatter(grad_cross_query, ("seq", "blk"), scatter_dimension=0, tiled=True),
-        lax.psum_scatter(grad_cross_key, ("seq", "blk"), scatter_dimension=0, tiled=True),
-        lax.psum_scatter(grad_cross_value, ("seq", "blk"), scatter_dimension=0, tiled=True),
-        lax.psum_scatter(grad_cross_out, ("seq", "blk"), scatter_dimension=0, tiled=True),
-        lax.psum_scatter(grad_ln_ffn, ("seq", "blk"), scatter_dimension=0, tiled=True),
-        lax.psum_scatter(grad_ffn_gate, ("seq", "blk"), scatter_dimension=0, tiled=True),
-        lax.psum_scatter(grad_ffn_up, ("seq", "blk"), scatter_dimension=0, tiled=True),
-        lax.psum_scatter(grad_ffn_down, ("seq", "blk"), scatter_dimension=0, tiled=True),
-    )
-    bias_total = lax.psum(bias_part.T, ("seq", "blk"))
+        ln_sums[0], sums[8], sums[9], sums[10], sums[7], ln_sums[1], sums[4], sums[5], sums[6],
+        sums[3], ln_sums[2], sums[0], sums[1], sums[2],
+    )
     return (
         final_rows.astype(jnp.bfloat16),
         hidden_grad,

time: 1340 us -> 666 us (0.50)
  waiting for transfers between devices: 985 us -> 314 us
  Pallas kernels: 0 us -> 129 us
  blocking collectives: 127 us -> 0 us
    reduce_scatter x11 -> x0, waiting for transfers between devices: 677 us -> none  [the longest x1 85.7 us: body(): lax.psum_scatter(grad_ffn_gate, ('seq', 'blk'), scatter_dimension=0, tile...]
    pallas_call x0 -> x1, Pallas kernels: none -> 129 us  [reduce_gradients(): pl.pallas_call(functools.partial(reduce_kernel, bits, widths, small.shape...]
    all_gather x2 -> x0, blocking collectives: 68.6 us -> none  [the longest x1 35.2 us: body(): key_piece = lax.all_gather(key_rows, 'blk', axis=0, tiled=True)]
    unnamed x1 -> x0, blocking collectives: 58.9 us -> none
    unnamed x25 -> x15, waiting for transfers between devices: 227 us -> 200 us
    psum x5, waiting for transfers between devices: 80.1 us -> 102 us  [head_running_total(): lax.psum(partial_sum.astype(jnp.bfloat16), 'head').astype(jnp.float32)]
    unnamed x135 -> x152, local copies, waits for them, and re-layouts: 29.3 us -> 26.2 us
  transfers between devices with their start and end apart: 21 -> 11, of which waited for: 18 -> 11; matrix products, arithmetic and copies ran while one was open for 8% -> 18% of each run, Pallas kernels for 0% -> 0%
where the time goes in v1:
time: 666 us; the launch traced here: 655 us
  waiting for transfers between devices  314 us (47%)
  Pallas kernels  129 us (19%)
  local copies, waits for them, and re-layouts  89.7 us (13%)
  matrix products  80.2 us (12%)
  other arithmetic  24.4 us (4%)
  between operations  15.6 us (2%)
    unnamed x15, waiting for transfers between devices  200 us
    pallas_call x1, Pallas kernels, reduce_gradients(): pl.pallas_call(functools.partial(reduce_kernel, bits, widths, small.shape...  129 us
    psum x5, waiting for transfers between devices, head_running_total(): lax.psum(partial_sum.astype(jnp.bfloat16), 'head').astype(jnp.float32)  102 us
    unnamed x152, local copies, waits for them, and re-layouts  26.2 us
    dot_general x11, matrix products, matmul_tn(): lax.dot_general(left, right, (((0,), (0,)), ((), ())), preferred_element_...  22.2 us
    dot_general x11, matrix products, matmul(): return jnp.dot(left, right, preferred_element_type=jnp.float32)  17.2 us
    dot_general x11, matrix products, matmul_t(): lax.dot_general(left, right, (((1,), (1,)), ((), ())), preferred_element_...  14.8 us
  transfers between devices with their start and end apart: 11, of which 11 were waited for; matrix products, arithmetic and copies ran while one was open for 18% of the time, Pallas kernels for 0%

profile of v1, /device:TPU:0, one launch (start us, length us, event | category | flops | bytes accessed | tf_op | source)
XLA Modules:
  0.0 655.1 jit_solution(1456312505462180140)
XLA Ops:
  15.1 2.6 tile.24
  17.7 5.9 tile.25
  23.6 4.6 slice.30
  28.2 9.3 %reshape.282 = f32[8,128,1150]{2,1,0:T(8,128)} reshape(f32[8,147200]{1,0:T(8,128)} %slice.30) | data formatting | bytes 9420800 | tf_op jit(solution)/shard_map/while/body/eval_jaxpr/reshape | solution.py:212
  37.5 4.8 slice.31
  42.3 5.3 copy.75
  47.8 1.9 convolution_convert_fusion.14
  49.7 5.4 all-gather.2.cloned.1.call-done
  55.1 2.2 fusion.116
  57.3 2.0 copy.73
  59.4 3.2 select_reduce_fusion
  62.6 1.9 copy-done.3
  65.9 2.0 copy.76
  68.0 3.9 fusion.76
  74.0 2.6 convolution_convert_fusion.15
  76.5 19.3 %all-reduce.10.cloned.1.call-done = bf16[128,1024]{1,0:T(8,128)(2,1)} async-done(((bf16[128,1024]{1,0:T(8,128)(2,1)}), bf16[128,1024]{1,0:T(8,128)(2,1)}) %all-reduce.10.cloned.1.call-update) | async-done | bytes 262160 | tf_op jit(solution)/shard_map/psum | solution.py:278
  97.0 2.3 convolution_convert_fusion.22
  101.0 3.1 fusion.117
  104.1 2.1 convolution_convert_fusion.21
  108.6 22.8 %all-reduce.12.cloned.1.call-done = bf16[128,1024]{1,0:T(8,128)(2,1)} async-done(((bf16[128,1024]{1,0:T(8,128)(2,1)}), bf16[128,1024]{1,0:T(8,128)(2,1)}) %all-reduce.12.cloned.1.call-update) | async-done | bytes 262160 | tf_op jit(solution)/shard_map/psum | solution.py:278
  133.7 2.5 fusion.119
  140.0 2.6 convolution_convert_fusion
  145.5 3.6 convolution_convert_fusion.1
  149.1 19.7 %all-reduce.14.cloned.1.call-done = bf16[128,1024]{1,0:T(8,128)(2,1)} async-done(((bf16[128,1024]{1,0:T(8,128)(2,1)}), bf16[128,1024]{1,0:T(8,128)(2,1)}) %all-reduce.14.cloned.1.call-update) | async-done | bytes 262160 | tf_op jit(solution)/shard_map/psum | solution.py:278
  168.8 1.8 fusion.61
  178.5 3.5 convolution_convert_fusion.2
  183.4 2.1 fusion.33
  189.9 11.9 %all-reduce.16.cloned.1.call-done = bf16[128,1024]{1,0:T(8,128)(2,1)} async-done(((bf16[128,1024]{1,0:T(8,128)(2,1)}), bf16[128,1024]{1,0:T(8,128)(2,1)}) %all-reduce.16.cloned.1.call-update) | async-done | bytes 262160 | tf_op jit(solution)/shard_map/psum | solution.py:278
  204.8 3.7 fusion.2
  210.1 2.1 copy.112
  212.2 2.6 copy.88
  214.8 3.3 pad.16
  218.1 5.9 reshape.335
  224.1 5.5 reshape.302
  229.9 4.0 pad_convert_fusion
  235.5 2.1 copy.114
  237.6 7.8 %reshape.307 = f32[8,129,1151]{2,1,0:T(8,128)} reshape(f32[8,148479]{1,0:T(8,128)} %pad_convert_fusion) | data formatting | bytes 9502656 | tf_op jit(solution)/shard_map/while/body/eval_jaxpr/reshape | solution.py:220
  247.0 2.7 reduce_sum.146
  253.3 13.5 %reduce-scatter.20.cloned.1.call-done = bf16[64,256]{1,0:T(8,128)(2,1)} async-done(((bf16[512,256]{1,0:T(8,128)(2,1)}), bf16[64,256]{1,0:T(8,128)(2,1)}) %reduce-scatter.20.cloned.1.call-update) | async-done | bytes 32784
  267.8 63.1 %reduce-scatter.22.cloned.1.call-done = bf16[64,256]{1,0:T(8,128)(2,1)} async-done(((bf16[512,256]{1,0:T(8,128)(2,1)}), bf16[64,256]{1,0:T(8,128)(2,1)}) %reduce-scatter.22.cloned.1.call-update) | async-done | bytes 32784
  333.0 2.0 convolution_convert_fusion.9
  335.0 60.3 %reduce-scatter.16.cloned.1.call-done = bf16[128,256]{1,0:T(8,128)(2,1)} async-done(((bf16[1024,256]{1,0:T(8,128)(2,1)}), bf16[128,256]{1,0:T(8,128)(2,1)}) %reduce-scatter.16.cloned.1.call-update) | async-done | bytes 65552
  396.7 63.2 %reduce-scatter.18.cloned.1.call-done = bf16[128,256]{1,0:T(8,128)(2,1)} async-done(((bf16[1024,256]{1,0:T(8,128)(2,1)}), bf16[128,256]{1,0:T(8,128)(2,1)}) %reduce-scatter.18.cloned.1.call-update) | async-done | bytes 65552
  462.6 2.0 convolution_convert_fusion.10
  464.7 7.2 %reduce-scatter.14.cloned.1.call-done = bf16[32,1024]{1,0:T(8,128)(2,1)} async-done(((bf16[64,1024]{1,0:T(8,128)(2,1)}), bf16[32,1024]{1,0:T(8,128)(2,1)}) %reduce-scatter.14.cloned.1.call-update) | async-done | bytes 65552 | tf_op jit(solution)/shard_map/reduce_scatter | solution.py:416
  475.8 27.8 %all-reduce.18.cloned.1.call-done = (bf16[128,1024]{1,0:T(8,128)(2,1)}, bf16[128,1024]{1,0:T(8,128)(2,1)}) async-done(((bf16[128,1024]{1,0:T(8,128)(2,1)}, bf16[128,1024]{1,0:T(8,128)(2,1)}), (bf16[128,1024]{1,0:T(8,128)(2,1)}, bf16[128,1024]{1,0:T(8,128)(2,1)})) %all-reduce.18.cloned.1.call-update) | async-done | bytes 524304 | tf_op jit(solution)/shard_map/psum | solution.py:278
  505.5 129.2 %grad_reduce.1 = (f32[64,1408]{1,0:T(8,128)}, f32[64,1408]{1,0:T(8,128)}, f32[64,1408]{1,0:T(8,128)}, f32[64,512]{1,0:T(8,128)}, f32[64,512]{1,0:T(8,128)}, /*in...) custom-call(bf16[2,2,2,2,64,1408]{5,4,3,2,1,0:T(8,128)(2,1)} %bitcas, ...), custom_call_target="tpu_custom_call" | custom-call | tf_op jit(solution)/shard_map/grad_reduce/pallas_call | solution.py:180
  637.5 2.5 fusion.54
  (241 shorter events, 73.6 us)
Async XLA Ops:
  7.2 129.6 %copy-start = (bf16[1024,1408]{1,0:T(8,128)(2,1)S(1)}, bf16[1024,1408]{1,0:T(8,128)(2,1)}, u32[]{:S(2)}) copy-start(bf16[1024,1408]{1,0:T(8,128)(2,1)} %param.37) | copy-start | bytes 8650756
  7.2 7.4 %copy-start.67 = (f32[32,8]{0,1:T(8,128)S(1)}, f32[32,8]{0,1:T(8,128)}, u32[]{:S(2)}) copy-start(f32[32,8]{0,1:T(8,128)} %param.28) | copy-start | bytes 3076
  7.2 47.9 %all-gather.2.cloned.1.call-start = ((), (), s32[]{:S(2)}) async-start(), calls=%async_computation.5 | async-start | bytes 1179648 | tf_op jit(solution)/shard_map/all_gather | solution.py:291
  12.0 83.8 %all-reduce.10.cloned.1.call-start = ((), (), s32[]{:S(2)}) async-start(), calls=%async_computation.6 | async-start | bytes 524288 | tf_op jit(solution)/shard_map/psum | solution.py:278
  14.5 44.8 %copy-start.28 = (bf16[128,512]{0,1:T(8,128)(2,1)}, bf16[128,512]{0,1:T(8,128)(2,1)S(1)}, u32[]{:S(2)}) copy-start(bf16[128,512]{0,1:T(8,128)(2,1)S(1)} %copy.74) | copy-start | bytes 393220
  14.6 9.0 %copy-start.63 = (s32[1151]{0:T(1024)}, s32[1151]{0:T(1024)S(1)}, u32[]{:S(2)}) copy-start(s32[1151]{0:T(1024)S(1)} %convert_add_fusion.2) | copy-start | bytes 13816
  49.7 51.3 %copy-start.22 = (bf16[512,256]{0,1:T(8,128)(2,1)}, bf16[512,256]{0,1:T(8,128)(2,1)S(1)}, u32[]{:S(2)}) copy-start(bf16[512,256]{0,1:T(8,128)(2,1)S(1)} %convolution_convert_fusion.14) | copy-start | bytes 786436
  71.9 24.0 %copy-start.2 = (bf16[128,1024]{1,0:T(8,128)(2,1)S(1)}, bf16[128,1024]{1,0:T(8,128)(2,1)}, u32[]{:S(2)}) copy-start(bf16[128,1024]{1,0:T(8,128)(2,1)} %param.19) | copy-start | bytes 786436
  71.9 25.1 %copy-start.51 = (f32[1024]{0:T(1024)S(1)}, f32[1024]{0:T(1024)}, u32[]{:S(2)}) copy-start(f32[1024]{0:T(1024)} %param.29) | copy-start | bytes 12292
  73.7 57.7 %all-reduce.12.cloned.1.call-start = ((), (), s32[]{:S(2)}) async-start(), calls=%async_computation.7 | async-start | bytes 524288 | tf_op jit(solution)/shard_map/psum | solution.py:278
  97.0 7.1 %copy-start.61 = (f32[128]{0:T(128)}, f32[128]{0:T(128)S(1)}, u32[]{:S(2)}) copy-start(f32[128]{0:T(128)S(1)} %add_rsqrt_fusion.1) | copy-start | bytes 1540
  104.1 27.3 %copy-start.9 = (bf16[128,1024]{1,0:T(8,128)(2,1)S(1)}, bf16[128,1024]{1,0:T(8,128)(2,1)}, u32[]{:S(2)}) copy-start(bf16[128,1024]{1,0:T(8,128)(2,1)} %all-reduce.10.cloned.1.call-done) | copy-start | bytes 786436
  106.2 27.3 %copy-start.56 = (f32[1024]{0:T(1024)S(1)}, f32[1024]{0:T(1024)}, u32[]{:S(2)}) copy-start(f32[1024]{0:T(1024)} %param.34) | copy-start | bytes 12292
  108.1 60.8 %all-reduce.14.cloned.1.call-start = ((), (), s32[]{:S(2)}) async-start(), calls=%async_computation.8 | async-start | bytes 524288 | tf_op jit(solution)/shard_map/psum | solution.py:278
  138.2 5.5 copy-start.27
  145.4 23.4 %copy-start.6 = (f32[128,1024]{1,0:T(8,128)S(1)}, f32[128,1024]{1,0:T(8,128)}, u32[]{:S(2)}) copy-start(f32[128,1024]{1,0:T(8,128)} %copy-done.5) | copy-start | bytes 1572868
  145.4 25.2 %copy-start.32 = (bf16[128,1024]{1,0:T(8,128)(2,1)S(1)}, bf16[128,1024]{1,0:T(8,128)(2,1)}, u32[]{:S(2)}) copy-start(bf16[128,1024]{1,0:T(8,128)(2,1)} %param.22) | copy-start | bytes 786436
  145.5 56.3 %all-reduce.16.cloned.1.call-start = ((), (), s32[]{:S(2)}) async-start(), calls=%async_computation.9 | async-start | bytes 524288 | tf_op jit(solution)/shard_map/psum | solution.py:278
  149.1 25.1 %copy-start.10 = (f32[4,2,128,512]{2,3,1,0:T(8,128)S(1)}, f32[4,2,128,512]{2,3,1,0:T(8,128)}, u32[]{:S(2)}) copy-start(f32[4,2,128,512]{2,3,1,0:T(8,128)} %get-tuple-element.149) | copy-start | bytes 6291460
  178.4 88.4 %reduce-scatter.20.cloned.1.call-start = ((), (), s32[]{:S(2)}) async-start(), calls=%async_computation.13 | async-start | bytes 294912
  183.4 147.6 %reduce-scatter.22.cloned.1.call-start = ((), (), s32[]{:S(2)}) async-start(), calls=%async_computation.14 | async-start | bytes 294912
  186.4 17.9 %copy-start.21 = (bf16[1024,512]{1,0:T(8,128)(2,1)S(1)}, bf16[1024,512]{1,0:T(8,128)(2,1)}, u32[]{:S(2)}) copy-start(bf16[1024,512]{1,0:T(8,128)(2,1)} %param.27) | copy-start | bytes 3145732
  187.9 16.9 %copy-start.43 = (f32[4,2,128,64]{2,3,1,0:T(8,128)S(1)}, f32[4,2,128,64]{2,3,1,0:T(8,128)}, u32[]{:S(2)}) copy-start(f32[4,2,128,64]{2,3,1,0:T(8,128)} %get-tuple-element.147) | copy-start | bytes 786436
  187.9 16.9 %copy-start.58 = (f32[4,2,128]{2,1,0:T(2,128)S(1)}, f32[4,2,128]{2,1,0:T(2,128)}, u32[]{:S(2)}) copy-start(f32[4,2,128]{2,1,0:T(2,128)} %get-tuple-element.137) | copy-start | bytes 12292
  187.9 16.9 %copy-start.59 = (f32[4,2,128]{2,1,0:T(2,128)S(1)}, f32[4,2,128]{2,1,0:T(2,128)}, u32[]{:S(2)}) copy-start(f32[4,2,128]{2,1,0:T(2,128)} %get-tuple-element.140) | copy-start | bytes 12292
  187.9 207.4 %reduce-scatter.16.cloned.1.call-start = ((), (), s32[]{:S(2)}) async-start(), calls=%async_computation.11 | async-start | bytes 589824
  189.9 14.9 %copy-start.60 = (f32[4,2,128]{2,1,0:T(2,128)S(1)}, f32[4,2,128]{2,1,0:T(2,128)}, u32[]{:S(2)}) copy-start(f32[4,2,128]{2,1,0:T(2,128)} %get-tuple-element.139) | copy-start | bytes 12292
  204.3 47.6 %copy-start.12 = (f32[128,1024]{1,0:T(8,128)}, f32[128,1024]{1,0:T(8,128)S(1)}, u32[]{:S(2)}) copy-start(f32[128,1024]{1,0:T(8,128)S(1)} %fusion.57) | copy-start | bytes 1572868
  229.6 230.3 %reduce-scatter.18.cloned.1.call-start = ((), (), s32[]{:S(2)}) async-start(), calls=%async_computation.12 | async-start | bytes 589824
  247.0 224.9 %reduce-scatter.14.cloned.1.call-start = ((), (), s32[]{:S(2)}) async-start(), calls=%async_computation.10 | async-start | bytes 196608 | tf_op jit(solution)/shard_map/reduce_scatter | solution.py:416
  249.8 17.0 %copy-start.24 = (bf16[1024,256]{1,0:T(8,128)(2,1)S(1)}, bf16[1024,256]{1,0:T(8,128)(2,1)}, u32[]{:S(2)}) copy-start(bf16[1024,256]{1,0:T(8,128)(2,1)} %param.31) | copy-start | bytes 1572868
  249.8 81.2 %copy-start.25 = (bf16[1024,256]{1,0:T(8,128)(2,1)S(1)}, bf16[1024,256]{1,0:T(8,128)(2,1)}, u32[]{:S(2)}) copy-start(bf16[1024,256]{1,0:T(8,128)(2,1)} %param.32) | copy-start | bytes 1572868
  251.8 209.5 %copy-start.18 = (bf16[1024,512]{1,0:T(8,128)(2,1)S(1)}, bf16[1024,512]{1,0:T(8,128)(2,1)}, u32[]{:S(2)}) copy-start(bf16[1024,512]{1,0:T(8,128)(2,1)} %param.24) | copy-start | bytes 3145732
  332.7 129.9 %copy-start.45 = (bf16[64,256]{1,0:T(8,128)(2,1)S(1)}, bf16[64,256]{1,0:T(8,128)(2,1)}, u32[]{:S(2)}) copy-start(bf16[64,256]{1,0:T(8,128)(2,1)} %reduce-scatter.20.cloned.1.call-done) | copy-start | bytes 98308
  332.7 170.9 %all-reduce.18.cloned.1.call-start = ((), (), s32[]{:S(2)}) async-start(), calls=%async_computation.15 | async-start | bytes 1048576 | tf_op jit(solution)/shard_map/psum | solution.py:278
  395.3 78.1 %copy-start.41 = (bf16[128,256]{1,0:T(8,128)(2,1)S(1)}, bf16[128,256]{1,0:T(8,128)(2,1)}, u32[]{:S(2)}) copy-start(bf16[128,256]{1,0:T(8,128)(2,1)} %reduce-scatter.16.cloned.1.call-done) | copy-start | bytes 196612
  460.0 14.6 %copy-start.42 = (bf16[128,256]{1,0:T(8,128)(2,1)S(1)}, bf16[128,256]{1,0:T(8,128)(2,1)}, u32[]{:S(2)}) copy-start(bf16[128,256]{1,0:T(8,128)(2,1)} %reduce-scatter.18.cloned.1.call-done) | copy-start | bytes 196612
  461.4 43.5 %copy-start.57 = (f32[1024]{0:T(1024)S(1)}, f32[1024]{0:T(1024)}, u32[]{:S(2)}) copy-start(f32[1024]{0:T(1024)} %get-tuple-element.120) | copy-start | bytes 12292
  505.5 132.0 %copy-start.33 = (bf16[128,1024]{1,0:T(8,128)(2,1)S(1)}, bf16[128,1024]{1,0:T(8,128)(2,1)}, u32[]{:S(2)}) copy-start(bf16[128,1024]{1,0:T(8,128)(2,1)} %get-tuple-element.127) | copy-start | bytes 786436
  634.8 10.7 %copy-start.46 = (f32[64,512]{1,0:T(8,128)S(1)}, f32[64,512]{1,0:T(8,128)}, u32[]{:S(2)}) copy-start(f32[64,512]{1,0:T(8,128)} %get-tuple-element.185) | copy-start | bytes 393220
  637.5 5.5 copy-start.48
  637.5 6.1 copy-start.47
  637.5 6.8 %copy-start.53 = (f32[64,256]{1,0:T(8,128)S(1)}, f32[64,256]{1,0:T(8,128)}, u32[]{:S(2)}) copy-start(f32[64,256]{1,0:T(8,128)} %get-tuple-element.183) | copy-start | bytes 196612
  637.5 7.4 %copy-start.52 = (f32[64,256]{1,0:T(8,128)S(1)}, f32[64,256]{1,0:T(8,128)}, u32[]{:S(2)}) copy-start(f32[64,256]{1,0:T(8,128)} %get-tuple-element.184) | copy-start | bytes 196612
  637.5 8.7 %copy-start.40 = (f32[64,1408]{1,0:T(8,128)S(1)}, f32[64,1408]{1,0:T(8,128)}, u32[]{:S(2)}) copy-start(f32[64,1408]{1,0:T(8,128)} %get-tuple-element.187) | copy-start | bytes 1081348
  637.5 9.4 %copy-start.39 = (f32[64,1408]{1,0:T(8,128)S(1)}, f32[64,1408]{1,0:T(8,128)}, u32[]{:S(2)}) copy-start(f32[64,1408]{1,0:T(8,128)} %get-tuple-element.188) | copy-start | bytes 1081348
  637.5 10.1 %copy-start.38 = (f32[64,1408]{1,0:T(8,128)S(1)}, f32[64,1408]{1,0:T(8,128)}, u32[]{:S(2)}) copy-start(f32[64,1408]{1,0:T(8,128)} %get-tuple-element.189) | copy-start | bytes 1081348
  637.5 10.8 %copy-start.1 = (bf16[1024,1408]{1,0:T(8,128)(2,1)S(1)}, bf16[1024,1408]{1,0:T(8,128)(2,1)}, u32[]{:S(2)}) copy-start(bf16[1024,1408]{1,0:T(8,128)(2,1)} %param.37) | copy-start | bytes 8650756
  (31 other events, 86.3 us)
Sparse Core Ops, SparseCore 0:
  12.2 42.9 all-gather.1
  73.8 21.9 all-reduce.9
  108.2 23.1 all-reduce.11
  145.6 23.1 all-reduce.13
  178.6 23.1 all-reduce.15
  205.5 61.2 reduce-scatter.19
  270.7 60.2 reduce-scatter.21
  334.3 60.9 reduce-scatter.15
  399.0 60.8 reduce-scatter.17
  462.6 9.2 reduce-scatter.13
  474.8 28.7 all-reduce.17

commit v2 on v0

v2 whole, which is shorter than its diff:
```python
import functools

import jax
import jax.numpy as jnp
import numpy as np
from jax import lax
from jax.experimental import pallas as pl
from jax.experimental.pallas import tpu as pltpu
from jax.sharding import PartitionSpec as P

MESH = pl.DeviceIdType.MESH
HEAD_DIM = 64
BUCKETS = 32
MAX_DIST = 128
EPSILON = 1e-06
MASKED = -1e30
BF = jnp.bfloat16
F32 = jnp.float32
TILE = 256
GELU_A = float(np.sqrt(2.0 / np.pi))
GELU_B = 0.044715

NAMES = ("sk", "sv", "sq", "ck", "cv", "so", "cq", "co", "fg", "fu", "fd")


def bucket_starts():
    exact = BUCKETS // 2
    far = np.ceil(exact * (MAX_DIST / exact) ** (np.arange(1, exact) / exact))
    return [*range(1, exact + 1), *(int(value) for value in far)]


def dot(left, right):
    return jnp.dot(left, right, preferred_element_type=F32)


def dot_nt(left, right):
    return lax.dot_general(left, right, (((1,), (1,)), ((), ())), preferred_element_type=F32)


def lane_tiles(width, step=512):
    return [(first, min(step, width - first)) for first in range(0, width, step)]


def layer_kernel(shapes, stop, *refs):
    bits, rows, width, groups, mem_rows = shapes
    stages = bits + 1
    blk_count = 1 << bits
    pairs = groups // 2
    half_count = blk_count // 2
    long = half_count > 4
    refs = list(refs)

    def take(count):
        taken, refs[:count] = refs[:count], []
        return taken

    lengths, rel_bias, hidden, out_grad, ln_self, ln_cross, ln_ffn, memory_in = take(8)
    weights_in = dict(zip(NAMES, take(11)))
    layer_out, hidden_grad, memory_grad = take(3)
    grads_out = dict(zip(NAMES, take(11)))
    (small_out,) = take(1)
    weight = dict(zip(NAMES, take(11)))
    landing = {name: take(stages) for name in NAMES}
    (memory, kbuf, vbuf, vT, kT, tab, near, scores, qs, cqs, ags, att_self, att_cross) = take(13)
    (lse, probs, mk, mv, mkT, mvT, pushed, landed) = take(8)
    (after_self, after_cross, cot, ns, ns_t, nc, nc_t, nf, nf_t, bg, bg_t) = take(11)
    (att_tok, catt_tok, inner, gate_grad, up_grad, qgrad) = take(6)
    (dkv,) = take(1)
    dkv_land = take(bits)
    (dmem,) = take(1)
    dmem_land = take(bits)
    (mem_push, mem_land, small, small_land, bias_sum) = take(5)
    (load_sem, hx_send, hx_recv, ag_send, ag_recv, rs_send, rs_recv) = take(7)
    (dk_send, dk_recv, dm_send, dm_recv, mg_send, mg_recv, sm_send, sm_recv) = take(8)

    seq, blk, head = (lax.axis_index(name) for name in ("seq", "blk", "head"))
    mine = [lax.rem(blk // (1 << bit), 2) for bit in range(bits)]

    def across(bit):
        return (seq, blk + (1 - 2 * mine[bit]) * (1 << bit), head)

    other_seq = (1 - seq, blk, head)
    other_head = (seq, blk, 1 - head)

    loads = {
        name: pltpu.make_async_copy(weights_in[name], weight[name], load_sem.at[slot])
        for slot, name in enumerate(NAMES)
    }
    memory_load = pltpu.make_async_copy(memory_in, memory, load_sem.at[len(NAMES)])
    for name in ("sk", "sv", "sq"):
        loads[name].start()
    memory_load.start()
    for name in NAMES[3:]:
        loads[name].start()

    barrier = pltpu.get_barrier_semaphore()
    friends = [other_seq, other_head, *(across(bit) for bit in range(bits))]
    for friend in friends:
        pl.semaphore_signal(barrier, inc=1, device_id=friend, device_id_type=MESH)

    def whole(name, lanes=slice(None)):
        value = weight[name][(Ellipsis, lanes)]
        return value.reshape(width, value.shape[-1])

    def row_tile(name, tile):
        value = weight[name][tile // 2, tile % 2]
        return value.reshape(TILE, value.shape[-1])

    def inverse_norm(values):
        return lax.rsqrt(jnp.mean(values * values, axis=-1, keepdims=True) + EPSILON)

    def norm_into(values, gain, plain, turned):
        result = (values * inverse_norm(values) * gain[...]).astype(BF)
        plain[...] = result
        turned[...] = result.T

    def norm_back(values, gain, normed_grad, slot):
        scale = inverse_norm(values)
        unit = values * scale
        unit_grad = normed_grad * gain[...]
        line = jnp.sum(normed_grad * unit, axis=0, keepdims=True)
        for tile in range(width // 128):
            small[0, slot * (width // 128) + tile : slot * (width // 128) + tile + 1, :] = line[
                :, tile * 128 : (tile + 1) * 128
            ]
        return scale * (unit_grad - unit * jnp.mean(unit_grad * unit, axis=-1, keepdims=True))

    def hx(which, tile):
        return pltpu.make_async_remote_copy(
            src_ref=pushed.at[which, tile],
            dst_ref=landed.at[which, tile],
            send_sem=hx_send.at[which, tile],
            recv_sem=hx_recv.at[which, tile],
            device_id=other_head,
            device_id_type=MESH,
        )

    def push(which, tile, value):
        pushed[which, tile] = value.astype(BF)
        hx(which, tile).start()

    def summed(which, tile):
        hx(which, tile).wait_recv()
        return pushed[which, tile].astype(F32) + landed[which, tile].astype(F32)

    tiles = width // TILE

    def summed_all(which):
        return jnp.concatenate([summed(which, tile) for tile in range(tiles)], axis=1)

    def bit_order(name):
        if name in ("fd", "cq", "sq"):
            return [*range(1, bits), 0]
        return list(range(bits))

    def bit_view(order, stage, keep):
        index = []
        for bit in reversed(range(bits)):
            place = order.index(bit)
            if place < stage:
                index.append(mine[bit])
            elif place == stage:
                index.append(mine[bit] if keep else 1 - mine[bit])
            else:
                index.append(slice(None))
        return tuple(index)

    def rs_view(name, stage, keep):
        if stage == 0:
            return weight[name].at[seq if keep else 1 - seq]
        return weight[name].at[(seq, *bit_view(bit_order(name), stage - 1, keep))]

    def rs_copy(name, stage):
        slot = NAMES.index(name)
        target = other_seq if stage == 0 else across(bit_order(name)[stage - 1])
        return pltpu.make_async_remote_copy(
            src_ref=rs_view(name, stage, False),
            dst_ref=landing[name][stage],
            send_sem=rs_send.at[slot, stage],
            recv_sem=rs_recv.at[slot, stage],
            device_id=target,
            device_id_type=MESH,
        )

    def rs_start(name):
        rs_copy(name, 0).start()

    def fold_into(kept, got):
        lead = got.shape[:-2]
        total = int(np.prod(lead))

        def body(flat, carry):
            index, left = [], flat
            for extent in reversed(lead):
                index.append(lax.rem(left, extent))
                left = left // extent
            index = tuple(reversed(index))
            kept[index] = (kept[index].astype(F32) + got[index].astype(F32)).astype(BF)
            return carry

        if total == 1:
            kept[...] = (kept[...].astype(F32) + got[...].astype(F32)).astype(BF)
        else:
            lax.fori_loop(0, total, body, 0)

    def rs_step(name, stage):
        rs_copy(name, stage).wait_recv()
        kept, got = rs_view(name, stage, True), landing[name][stage]
        if stage == stages - 1:
            grads_out[name][...] = kept[...].astype(F32) + got[...].astype(F32)
        else:
            fold_into(kept, got)
            rs_copy(name, stage + 1).start()

    def part_copy(buffer, land, send, recv, stage):
        order = list(range(bits))
        return pltpu.make_async_remote_copy(
            src_ref=buffer.at[bit_view(order, stage, False)],
            dst_ref=land[stage],
            send_sem=send.at[stage],
            recv_sem=recv.at[stage],
            device_id=across(order[stage]),
            device_id_type=MESH,
        )

    def part_step(buffer, land, send, recv, stage):
        order = list(range(bits))
        part_copy(buffer, land, send, recv, stage).wait_recv()
        kept = buffer.at[bit_view(order, stage, True)]
        if stage == bits - 1:
            return kept[...].astype(F32) + land[stage][...].astype(F32)
        fold_into(kept, land[stage])
        part_copy(buffer, land, send, recv, stage + 1).start()

    def dkv_args(pair):
        return (
            dkv.at[pair],
            [land.at[pair] for land in dkv_land],
            dk_send.at[pair],
            dk_recv.at[pair],
        )

    dmem_args = (dmem, dmem_land, dm_send, dm_recv)

    def ag_copy(which, step):
        bit = bits - 1 - step
        index = (slice(None),) + tuple(
            slice(None) if place > bit else mine[place] for place in reversed(range(bits))
        )
        buffer = (kbuf, vbuf)[which]
        return pltpu.make_async_remote_copy(
            src_ref=buffer.at[index],
            dst_ref=buffer.at[index],
            send_sem=ag_send.at[which, step],
            recv_sem=ag_recv.at[which, step],
            device_id=across(bit),
            device_id_type=MESH,
        )

    def ag_next(step):
        for which in range(2):
            ag_copy(which, step).wait_recv()
            if step + 1 < bits:
                ag_copy(which, step + 1).start()

    def half_index(chunk):
        index, left = [], chunk
        for _ in range(bits - 1):
            index.append(left % 2 if isinstance(left, int) else lax.rem(left, 2))
            left = left // 2
        return tuple(reversed(index))

    def chunk_of(buffer, pair, chunk):
        return buffer[(pair, *half_index(chunk))].reshape(2 * rows, 128)

    lane = lax.broadcasted_iota(jnp.int32, (rows, 128), 1)
    low = lane < HEAD_DIM
    swap_row = lax.broadcasted_iota(jnp.int32, (128, 128), 0)
    swap_col = lax.broadcasted_iota(jnp.int32, (128, 128), 1)
    swap = (swap_row == lax.rem(swap_col + HEAD_DIM, 128)).astype(F32).astype(BF)

    def split_heads(values, target):
        for group in range(groups):
            tile = values[:, group * 128 : (group + 1) * 128]
            swapped = dot(tile, swap)
            plain = tile.astype(F32)
            first, second = (plain, swapped) if group % 2 == 0 else (swapped, plain)
            here = low if group % 2 == 0 else jnp.logical_not(low)
            target[group, :rows, :] = jnp.where(here, first, 0.0).astype(BF)
            target[group, rows:, :] = jnp.where(here, second, 0.0).astype(BF)

    def join_heads(values):
        return jnp.concatenate([values[:, :rows], values[:, rows:]], axis=0).T

    def head_deltas(values, attended, group):
        turned = values[:, group * 128 : (group + 1) * 128].astype(F32).T
        laid = jnp.concatenate([turned[:HEAD_DIM, :], turned[HEAD_DIM:, :]], axis=1)
        return jnp.sum(laid * attended[group], axis=0, keepdims=True)

    length = lengths[0]
    key_row = lax.broadcasted_iota(jnp.int32, (rows, 2 * rows), 0)

    def kind_of(block):
        return jnp.clip(block - blk + 2, 0, 3)

    def self_scores(group, chunk):
        raw = dot_nt(chunk_of(kbuf, group // 2, chunk), qs[group])
        parts = []
        for inner_block in range(2):
            block = 2 * chunk + inner_block
            part = raw[inner_block * rows : (inner_block + 1) * rows, :]
            part = part + tab[kind_of(block), group]
            parts.append(jnp.where(key_row + block * rows < length, part, MASKED))
        return jnp.concatenate(parts, axis=0)

    x = hidden[...].astype(F32)
    norm_into(x, ln_self, ns, ns_t)
    loads["sk"].wait()
    keys = dot(ns[...], whole("sk")).astype(BF)
    for pair in range(pairs):
        kbuf[(pair, *reversed(mine))] = keys[:, pair * 128 : (pair + 1) * 128]
    pl.semaphore_wait(barrier, len(friends))
    ag_copy(0, 0).start()
    loads["sv"].wait()
    values = dot(ns[...], whole("sv")).astype(BF)
    for pair in range(pairs):
        vbuf[(pair, *reversed(mine))] = values[:, pair * 128 : (pair + 1) * 128]
    ag_copy(1, 0).start()
    loads["sq"].wait()
    split_heads(dot(ns[...], whole("sq")).astype(BF), qs)
    ag_next(0)

    memory_load.wait()
    for source, plain, turned in (("ck", mk, mkT), ("cv", mv, mvT)):
        loads[source].wait()
        result = dot(memory[...], whole(source)).astype(BF)
        for pair in range(pairs):
            plain[pair] = result[:, pair * 128 : (pair + 1) * 128]
            turned[pair * 128 : (pair + 1) * 128, :] = result[:, pair * 128 : (pair + 1) * 128].T
    if bits > 1:
        ag_next(1)

    starts = bucket_starts()
    distance = lane - lax.broadcasted_iota(jnp.int32, (rows, 128), 0)

    def bias_of(which, head_slot):
        shifted = distance + (rows if which == 1 else 0)
        value = jnp.full((rows, 128), rel_bias[0, head_slot], F32)
        for bucket, start in enumerate(starts):
            value = jnp.where(shifted >= start, rel_bias[bucket + 1, head_slot], value)
        if which == 2:
            value = jnp.where(shifted >= 0, value, MASKED)
        return value

    def bias_tables(head_slot, carry):
        group = head_slot // 2
        lanes = pl.ds(pl.multiple_of(lax.rem(head_slot, 2) * rows, rows), rows)
        tab[0, group, :, lanes] = jnp.full((rows, rows), rel_bias[BUCKETS - 1, head_slot], F32)
        tab[1, group, :, lanes] = bias_of(1, head_slot)
        tab[2, group, :, lanes] = bias_of(2, head_slot)
        tab[3, group, :, lanes] = jnp.full((rows, rows), MASKED, F32)
        return carry

    lax.fori_loop(0, 2 * groups, bias_tables, 0)
    for step in range(2, bits):
        ag_next(step)

    def turn_chunk(chunk):
        for pair in range(pairs):
            vT[chunk, pair * 128 : (pair + 1) * 128, :] = chunk_of(vbuf, pair, chunk).T
            kT[chunk, pair * 128 : (pair + 1) * 128, :] = chunk_of(kbuf, pair, chunk).T

    if not long:
        for chunk in range(half_count):
            turn_chunk(chunk)

    def turned_of(kept, buffer, group, chunk):
        if not long:
            return kept[chunk, group * HEAD_DIM : (group + 1) * HEAD_DIM, :]
        first = (group % 2) * HEAD_DIM
        return chunk_of(buffer, group // 2, chunk).T[first : first + HEAD_DIM, :]

    def attend(group):
        tops = jnp.full((1, 2 * rows), MASKED, F32)

        def first_pass(chunk, top):
            part = self_scores(group, chunk)
            if not long:
                scores[group % 2, chunk] = part
            return jnp.maximum(top, jnp.max(part, axis=0, keepdims=True))

        def second_pass(chunk, state):
            total, acc = state
            part = self_scores(group, chunk) if long else scores[group % 2, chunk]
            part = jnp.exp(part - tops)
            total = total + jnp.sum(part, axis=0, keepdims=True)
            return total, acc + dot(turned_of(vT, vbuf, group, chunk), part.astype(BF))

        state = (jnp.zeros((1, 2 * rows), F32), jnp.zeros((HEAD_DIM, 2 * rows), F32))
        if not long:
            for chunk in range(half_count):
                tops = first_pass(chunk, tops)
            for chunk in range(half_count):
                state = second_pass(chunk, state)
        else:
            tops = lax.fori_loop(0, half_count, first_pass, tops)
            state = lax.fori_loop(0, half_count, second_pass, state)
        total, acc = state
        precise = acc / total
        att_self[group] = precise
        lse[group] = tops + jnp.log(total)
        att_tok[:, group * 128 : (group + 1) * 128] = join_heads(precise).astype(BF)

    for group in range(groups):
        attend(group)

    loads["so"].wait()
    for tile in range(tiles):
        push(0, tile, dot_nt(att_tok[...], row_tile("so", tile)))
    valid = lax.broadcasted_iota(jnp.int32, (rows, 1), 0) + blk * rows < length
    bg[...] = jnp.where(valid, out_grad[...].astype(F32), 0.0).astype(BF)
    bg_t[...] = bg[...].T
    after_self[...] = x + summed_all(0)

    norm_into(after_self[...], ln_cross, nc, nc_t)
    loads["cq"].wait()
    split_heads(dot(nc[...], whole("cq")).astype(BF), cqs)
    for group in range(groups):
        part = dot_nt(mk[group // 2], cqs[group])
        part = jnp.exp(part - jnp.max(part, axis=0, keepdims=True))
        part = part * (1.0 / jnp.sum(part, axis=0, keepdims=True))
        probs[group] = part
        acc = dot(mvT[group * HEAD_DIM : (group + 1) * HEAD_DIM, :], part.astype(BF))
        att_cross[group] = acc
        catt_tok[:, group * 128 : (group + 1) * 128] = join_heads(acc).astype(BF)
    loads["co"].wait()
    for tile in range(tiles):
        push(1, tile, dot_nt(catt_tok[...], row_tile("co", tile)))
    after_cross[...] = after_self[...] + summed_all(1)

    norm_into(after_cross[...], ln_ffn, nf, nf_t)
    for name in ("fg", "fu", "fd"):
        loads[name].wait()
    for first, size in lane_tiles(inner.shape[1]):
        lanes = slice(first, first + size)
        gate = dot(nf[...], whole("fg", lanes))
        up = dot(nf[...], whole("fu", lanes))
        back = dot(bg[...], whole("fd", lanes))
        bent = jnp.tanh(GELU_A * (gate + GELU_B * gate * gate * gate))
        share = 0.5 * (1.0 + bent)
        slope = share + 0.5 * gate * (1.0 - bent * bent) * (
            GELU_A * (1.0 + 3.0 * GELU_B * gate * gate)
        )
        bell = gate * share
        inner[:, lanes] = (bell * up).astype(BF)
        gate_grad[:, lanes] = (back * up * slope).astype(BF)
        up_grad[:, lanes] = (back * bell).astype(BF)
    for tile in range(tiles):
        push(
            2,
            tile,
            dot_nt(gate_grad[...], row_tile("fg", tile)) + dot_nt(up_grad[...], row_tile("fu", tile)),
        )
    for tile in range(tiles):
        push(3, tile, dot_nt(inner[...], row_tile("fd", tile)))

    def weight_grad(name, turned, right):
        for first, size in lane_tiles(right.shape[1]):
            lanes = slice(first, first + size)
            for tile in range(tiles):
                result = dot(turned[tile * TILE : (tile + 1) * TILE, :], right[:, lanes]).astype(BF)
                shape = weight[name].shape[2:-1]
                weight[name][(tile // 2, tile % 2, Ellipsis, lanes)] = result.reshape(*shape, size)
        rs_start(name)

    weight_grad("fd", bg_t, inner)
    weight_grad("fg", nf_t, gate_grad)
    weight_grad("fu", nf_t, up_grad)
    normed_grad = summed_all(2)
    cot[...] = jnp.where(valid, out_grad[...].astype(F32), 0.0) + norm_back(
        after_cross[...], ln_ffn, normed_grad, 2
    )
    bg[...] = cot[...].astype(BF)
    bg_t[...] = bg[...].T

    for name in ("fd", "fg", "fu"):
        rs_step(name, 0)
    back = dot(bg[...], whole("co")).astype(BF)
    split_heads(back, ags)
    for pair in range(pairs):
        key_part = value_part = None
        for group in (2 * pair, 2 * pair + 1):
            prob = probs[group]
            prob_grad = dot_nt(mv[pair], ags[group])
            score_grad = (prob * (prob_grad - head_deltas(back, att_cross, group))).astype(BF)
            turned = dot(mkT[group * HEAD_DIM : (group + 1) * HEAD_DIM, :], score_grad)
            qgrad[:, group * 128 : (group + 1) * 128] = join_heads(turned).astype(BF)
            key_new = dot(score_grad, cqs[group])
            value_new = dot(prob.astype(BF), ags[group])
            key_part = key_new if key_part is None else key_part + key_new
            value_part = value_new if value_part is None else value_part + value_new
        shape = dmem.shape[:-1]
        dmem[..., pair * 128 : (pair + 1) * 128] = key_part.astype(BF).reshape(*shape, 128)
        dmem[..., (pairs + pair) * 128 : (pairs + pair + 1) * 128] = value_part.astype(BF).reshape(
            *shape, 128
        )
    for tile in range(tiles):
        push(4, tile, dot_nt(qgrad[...], row_tile("cq", tile)))
    part_copy(*dmem_args, 0).start()
    weight_grad("co", bg_t, catt_tok)
    weight_grad("cq", nc_t, qgrad)
    for tile in range(tiles):
        lanes = slice(tile * TILE, (tile + 1) * TILE)
        layer_out[:, lanes] = (after_cross[:, lanes] + summed(3, tile)).astype(BF)
    normed_grad = summed_all(4)
    cot[...] = cot[...] + norm_back(after_self[...], ln_cross, normed_grad, 1)
    bg[...] = cot[...].astype(BF)
    bg_t[...] = bg[...].T

    back = dot(bg[...], whole("so")).astype(BF)
    split_heads(back, ags)
    part_step(*dmem_args, 0)
    rs_step("fg", 1)
    rs_step("fd", 1)
    near[1] = jnp.zeros(near.shape[1:], BF)
    for name in ("co", "cq"):
        rs_step(name, 0)
    for pair in range(pairs):
        members = (2 * pair, 2 * pair + 1)
        deltas = [head_deltas(back, att_self, group) for group in members]

        def visit(chunk, state, pair=pair, members=members, deltas=deltas):
            state = list(state)
            key_part = value_part = None
            values_here = chunk_of(vbuf, pair, chunk)
            for slot, group in enumerate(members):
                prob = jnp.exp(self_scores(group, chunk) - lse[group])
                prob_grad = dot_nt(values_here, ags[group])
                score_grad = (prob * (prob_grad - deltas[slot])).astype(BF)
                lhs = turned_of(kT, kbuf, group, chunk)
                state[2 * slot] = state[2 * slot] + dot(lhs, score_grad)
                key_new = dot(score_grad, qs[group])
                value_new = dot(prob.astype(BF), ags[group])
                key_part = key_new if key_part is None else key_part + key_new
                value_part = value_new if value_part is None else value_part + value_new
                for inner_block in range(2):
                    kind = kind_of(2 * chunk + inner_block)
                    piece = score_grad[inner_block * rows : (inner_block + 1) * rows, :]
                    near[lax.rem(kind, 3), group] = piece
                    is_far = (kind == 0).astype(F32)
                    state[2 * slot + 1] = state[2 * slot + 1] + is_far * jnp.sum(
                        piece.astype(F32), axis=0, keepdims=True
                    )
            where_to = (pair, *half_index(chunk))
            dkv[(*where_to, slice(None), slice(None), slice(0, 128))] = key_part.astype(BF).reshape(
                2, rows, 128
            )
            dkv[(*where_to, slice(None), slice(None), slice(128, 256))] = value_part.astype(
                BF
            ).reshape(2, rows, 128)
            return tuple(state)

        state = (jnp.zeros((HEAD_DIM, 2 * rows), F32), jnp.zeros((1, 2 * rows), F32)) * 2
        if not long:
            for chunk in range(half_count):
                state = visit(chunk, state)
        else:
            state = lax.fori_loop(0, half_count, visit, state)
        part_copy(*dkv_args(pair), 0).start()
        for slot, group in enumerate(members):
            qgrad[:, group * 128 : (group + 1) * 128] = join_heads(state[2 * slot]).astype(BF)
            bias_sum[BUCKETS : BUCKETS + 1, group * 2 * rows : (group + 1) * 2 * rows] = state[
                2 * slot + 1
            ]
    part_step(*dkv_args(0), 0)
    part_step(*dmem_args, 1)
    weight_grad("so", bg_t, att_tok)
    rs_step("fu", 1)
    part_step(*dkv_args(1), 0)
    rs_step("fg", 2)
    mem_sum = None
    for step in range(2, bits):
        mem_sum = part_step(*dmem_args, step)
    for step in range(1, bits - 1):
        part_step(*dkv_args(0), step)
    query_part = [
        dot_nt(qgrad[...], row_tile("sq", tile)) for tile in range(tiles)
    ]
    weight_grad("sq", ns_t, qgrad)
    for step in range(1, bits - 1):
        part_step(*dkv_args(1), step)
    sums = [part_step(*dkv_args(pair), bits - 1).astype(BF) for pair in range(pairs)]
    kgrad = jnp.concatenate([value[:, :128] for value in sums], axis=1)
    vgrad = jnp.concatenate([value[:, 128:] for value in sums], axis=1)
    for tile in range(tiles):
        push(
            5,
            tile,
            query_part[tile]
            + dot_nt(kgrad, row_tile("sk", tile))
            + dot_nt(vgrad, row_tile("sv", tile)),
        )
    weight_grad("sk", ns_t, kgrad)
    weight_grad("sv", ns_t, vgrad)

    share = mem_rows // blk_count
    mem_sum = mem_sum.astype(BF)
    mkg, mvg = mem_sum[:, : pairs * 128], mem_sum[:, pairs * 128 :]
    mem_part = dot_nt(mkg, whole("ck")) + dot_nt(mvg, whole("cv"))
    half = share // 2
    mem_push[0] = mem_part[:half, :].astype(BF)
    mem_push[1] = mem_part[half:, :].astype(BF)
    mem_copy = pltpu.make_async_remote_copy(
        src_ref=mem_push.at[1 - head],
        dst_ref=mem_land,
        send_sem=mg_send,
        recv_sem=mg_recv,
        device_id=other_head,
        device_id_type=MESH,
    )
    mem_copy.start()
    own_rows = memory[pl.ds(pl.multiple_of(blk * share, share), share), :]
    own_turned = own_rows.T
    weight_grad("ck", own_turned, mkg)
    weight_grad("cv", own_turned, mvg)

    def bucket_line(group, lower, upper):
        line = jnp.zeros((1, 2 * rows), F32)
        wide = jnp.concatenate([distance, distance], axis=1)
        for kind in (1, 2):
            shifted = wide + (rows if kind == 1 else 0)
            here = shifted >= lower
            if upper is not None:
                here = jnp.logical_and(here, shifted < upper)
            piece = near[kind, group].astype(F32)
            line = line + jnp.sum(jnp.where(here, piece, 0.0), axis=0, keepdims=True)
        return line

    bounds = [0, *starts, None]
    for group in range(groups):
        lanes = slice(group * 2 * rows, (group + 1) * 2 * rows)
        for bucket in range(BUCKETS):
            line = bucket_line(group, bounds[bucket], bounds[bucket + 1])
            if bucket == BUCKETS - 1:
                line = line + bias_sum[BUCKETS : BUCKETS + 1, lanes]
            bias_sum[bucket : bucket + 1, lanes] = line
    bias_lane = lax.broadcasted_iota(jnp.int32, (BUCKETS, 128), 1)
    bias_grad = jnp.zeros((BUCKETS, 128), F32)
    for head_slot in range(2 * groups):
        column = jnp.sum(
            bias_sum[:BUCKETS, head_slot * rows : (head_slot + 1) * rows], axis=1, keepdims=True
        )
        bias_grad = jnp.where(bias_lane == head_slot, column, bias_grad)
    first_bias = 3 * (width // 128)
    small[0, first_bias : first_bias + BUCKETS, :] = bias_grad

    normed_grad = summed_all(5)
    hidden_grad[...] = cot[...] + norm_back(hidden[...].astype(F32), ln_self, normed_grad, 0)

    def small_copy(stage):
        return pltpu.make_async_remote_copy(
            src_ref=small.at[stage],
            dst_ref=small_land.at[stage],
            send_sem=sm_send.at[stage],
            recv_sem=sm_recv.at[stage],
            device_id=other_seq if stage == 0 else across(stage - 1),
            device_id_type=MESH,
        )

    small_copy(0).start()
    done = {"fd": 2, "fg": 3, "fu": 2, "co": 1, "cq": 1}
    order = ("fu", "fd", "fg", "co", "cq", "so", "sq", "sk", "sv", "ck", "cv")
    for sweep in range(stages):
        small_copy(sweep).wait_recv()
        total = small[sweep] + small_land[sweep]
        if sweep < stages - 1:
            small[sweep + 1] = total
            small_copy(sweep + 1).start()
        else:
            small_out[...] = total
        for name in order:
            at = done.get(name, 0)
            if at < stages:
                rs_step(name, at)
                done[name] = at + 1
    mem_copy.wait_recv()
    memory_grad[...] = mem_push[head].astype(F32) + mem_land[...].astype(F32)

    for name in NAMES:
        for stage in range(stages):
            rs_copy(name, stage).wait_send()
    for stage in range(stages):
        small_copy(stage).wait_send()
    for which in range(6):
        for tile in range(tiles):
            hx(which, tile).wait_send()
    for which in range(2):
        for step in range(bits):
            ag_copy(which, step).wait_send()
    for step in range(bits):
        part_copy(*dmem_args, step).wait_send()
        for pair in range(pairs):
            part_copy(*dkv_args(pair), step).wait_send()
    mem_copy.wait_send()


def run_layer(lengths, rel_bias, hidden, out_grad, gains, memory, weights, blk_count, stop=None):
    bits = blk_count.bit_length() - 1
    stages = bits + 1
    rows, width = hidden.shape
    groups = weights["sk"].shape[1] // HEAD_DIM
    heads = weights["sq"].shape[1] // HEAD_DIM
    mem_rows = memory.shape[0]
    if rows != 128 or heads != 2 * groups or bucket_starts()[-1] > rows or 1 << bits != blk_count:
        raise ValueError("unexpected sizes")
    pairs = groups // 2
    half_count = blk_count // 2
    stored = 1 if half_count > 4 else half_count
    piece = width // (2 * blk_count)
    lead = (2,) * (bits + 1)
    widths = {name: weights[name].shape[1] for name in NAMES}
    shaped = [weights[name].reshape(*lead, piece, widths[name]) for name in NAMES]
    units = widths["fg"]
    share = mem_rows // blk_count
    small_rows = 3 * (width // 128) + BUCKETS

    vm, sem = pltpu.VMEM, pltpu.SemaphoreType.DMA
    scratch = [vm((*lead, piece, widths[name]), BF) for name in NAMES]
    for name in NAMES:
        for stage in range(stages):
            scratch.append(vm((2,) * (bits - stage) + (piece, widths[name]), BF))
    by_bit = (2,) * bits
    scratch += [
        vm(memory.shape, BF),
        vm((pairs, *by_bit, rows, 128), BF),
        vm((pairs, *by_bit, rows, 128), BF),
        vm((stored, groups * HEAD_DIM, 2 * rows), BF),
        vm((stored, groups * HEAD_DIM, 2 * rows), BF),
        vm((4, groups, rows, 2 * rows), F32),
        vm((3, groups, rows, 2 * rows), BF),
        vm((2, stored, 2 * rows, 2 * rows), F32),
        vm((groups, 2 * rows, 128), BF),
        vm((groups, 2 * rows, 128), BF),
        vm((groups, 2 * rows, 128), BF),
        vm((groups, HEAD_DIM, 2 * rows), F32),
        vm((groups, HEAD_DIM, 2 * rows), F32),
        vm((groups, 1, 2 * rows), F32),
        vm((groups, mem_rows, 2 * rows), F32),
        vm((pairs, mem_rows, 128), BF),
        vm((pairs, mem_rows, 128), BF),
        vm((groups * HEAD_DIM, mem_rows), BF),
        vm((groups * HEAD_DIM, mem_rows), BF),
        vm((6, width // TILE, rows, TILE), BF),
        vm((6, width // TILE, rows, TILE), BF),
        vm((rows, width), F32),
        vm((rows, width), F32),
        vm((rows, width), F32),
        vm((rows, width), BF),
        vm((width, rows), BF),
        vm((rows, width), BF),
        vm((width, rows), BF),
        vm((rows, width), BF),
        vm((width, rows), BF),
        vm((rows, width), BF),
        vm((width, rows), BF),
        vm((rows, heads * HEAD_DIM), BF),
        vm((rows, heads * HEAD_DIM), BF),
        vm((rows, units), BF),
        vm((rows, units), BF),
        vm((rows, units), BF),
        vm((rows, heads * HEAD_DIM), BF),
        vm((pairs, *by_bit, rows, 256), BF),
    ]
    scratch += [vm((pairs, *(2,) * (bits - 1 - stage), rows, 256), BF) for stage in range(bits)]
    scratch += [vm((*by_bit, share, 2 * groups * HEAD_DIM), BF)]
    scratch += [
        vm((*(2,) * (bits - 1 - stage), share, 2 * groups * HEAD_DIM), BF) for stage in range(bits)
    ]
    scratch += [
        vm((2, share // 2, width), BF),
        vm((share // 2, width), BF),
        vm((stages, small_rows, 128), F32),
        vm((stages, small_rows, 128), F32),
        vm((BUCKETS + 8, heads * rows), F32),
        sem((len(NAMES) + 1,)),
        sem((6, width // TILE)),
        sem((6, width // TILE)),
        sem((2, bits)),
        sem((2, bits)),
        sem((len(NAMES), stages)),
        sem((len(NAMES), stages)),
        sem((pairs, bits)),
        sem((pairs, bits)),
        sem((bits,)),
        sem((bits,)),
        sem,
        sem,
        sem((stages,)),
        sem((stages,)),
    ]
    in_vmem = pl.BlockSpec(memory_space=pltpu.VMEM)
    in_smem = pl.BlockSpec(memory_space=pltpu.SMEM)
    in_any = pl.BlockSpec(memory_space=pl.ANY)
    out_shape = [
        jax.ShapeDtypeStruct((rows, width), BF),
        jax.ShapeDtypeStruct((rows, width), F32),
        jax.ShapeDtypeStruct((share // 2, width), F32),
        *(jax.ShapeDtypeStruct((piece, widths[name]), F32) for name in NAMES),
        jax.ShapeDtypeStruct((small_rows, 128), F32),
    ]
    results = pl.pallas_call(
        functools.partial(layer_kernel, (bits, rows, width, groups, mem_rows), stop),
        out_shape=out_shape,
        in_specs=[in_smem, in_smem, *[in_vmem] * 5, *[in_any] * 12],
        out_specs=[in_vmem] * len(out_shape),
        scratch_shapes=scratch,
        compiler_params=pltpu.CompilerParams(
            collective_id=0, has_side_effects=True, vmem_limit_bytes=62 * 1024 * 1024
        ),
        name="layer",
    )(lengths, rel_bias, hidden, out_grad, *gains, memory, *shaped)
    return results[:3], dict(zip(NAMES, results[3:-1])), results[-1]


def body(
    hidden,
    memory,
    lengths,
    out_grad,
    ln_self,
    self_query,
    self_key,
    self_value,
    self_out,
    rel_bias,
    ln_cross,
    cross_query,
    cross_key,
    cross_value,
    cross_out,
    ln_ffn,
    ffn_gate,
    ffn_up,
    feedforward_down_weight,
):
    width = hidden.shape[1]
    blk_count = lax.axis_size("blk")
    weights = dict(
        sk=self_key,
        sv=self_value,
        sq=self_query,
        ck=cross_key,
        cv=cross_value,
        so=self_out,
        cq=cross_query,
        co=cross_out,
        fg=ffn_gate,
        fu=ffn_up,
        fd=feedforward_down_weight,
    )
    gains = [gain.reshape(1, width) for gain in (ln_self, ln_cross, ln_ffn)]
    (layer_out, hidden_grad, memory_grad), grads, small = run_layer(
        lengths, rel_bias, hidden, out_grad, gains, memory, weights, blk_count
    )
    lines = width // 128
    share = width // (2 * blk_count)
    first = (lax.axis_index("seq") * blk_count + lax.axis_index("blk")) * share
    gain_grads = lax.dynamic_slice(small[: 3 * lines].reshape(3, width), (0, first), (3, share))
    bias_grad = small[3 * lines :, : rel_bias.shape[1]]
    return (
        layer_out,
        hidden_grad,
        memory_grad,
        gain_grads[0],
        grads["sq"],
        grads["sk"],
        grads["sv"],
        grads["so"],
        bias_grad,
        gain_grads[1],
        grads["cq"],
        grads["ck"],
        grads["cv"],
        grads["co"],
        gain_grads[2],
        grads["fg"],
        grads["fu"],
        grads["fd"],
    )


def solution(mesh):
    blocks = P(("seq", "blk"), None)
    by_head = P(None, "head")
    shares = P(("seq", "blk"), "head")
    line = P(("seq", "blk"))
    in_specs = (
        blocks,
        P("seq", None),
        P("seq"),
        blocks,
        P(),
        *[by_head] * 5,
        P(),
        *[by_head] * 4,
        P(),
        *[by_head] * 3,
    )
    out_specs = (
        blocks,
        blocks,
        P(("seq", "blk", "head"), None),
        line,
        *[shares] * 4,
        by_head,
        line,
        *[shares] * 4,
        line,
        *[shares] * 3,
    )
    return jax.shard_map(body, mesh=mesh, in_specs=in_specs, out_specs=out_specs, check_vma=False)
```

time: 1340 us -> 220 us (0.16)
  waiting for transfers between devices: 985 us -> 0 us
  Pallas kernels: 0 us -> 197 us
  blocking collectives: 127 us -> 0 us
  matrix products: 89.7 us -> 0 us
  local copies, waits for them, and re-layouts: 87.5 us -> 21.1 us
  other arithmetic: 24.5 us -> 0 us
  between operations: 17.1 us -> 1.38 us
    reduce_scatter x12 -> x0, waiting for transfers between devices: 677 us -> none  [the longest x1 85.7 us: body(): lax.psum_scatter(grad_ffn_gate, ('seq', 'blk'), scatter_dimension=0, tile...]
    unnamed x25 -> x0, waiting for transfers between devices: 227 us -> none
    pallas_call x0 -> x1, Pallas kernels: none -> 197 us  [run_layer(): pl.pallas_call(functools.partial(layer_kernel, (bits, rows, width, groups...]
    dot_general x46 -> x0, matrix products: 86.7 us -> none  [the longest x11 24.9 us: matmul_tn(): lax.dot_general(left, right, (((0,), (0,)), ((), ())), preferred_element_...]
    psum x5 -> x0, waiting for transfers between devices: 80.1 us -> none  [head_running_total(): lax.psum(partial_sum.astype(jnp.bfloat16), 'head').astype(jnp.float32)]
    all_gather x2 -> x0, blocking collectives: 68.6 us -> none  [the longest x1 35.2 us: body(): key_piece = lax.all_gather(key_rows, 'blk', axis=0, tiled=True)]
    unnamed x1 -> x0, blocking collectives: 58.9 us -> none
    reshape x4 -> x1, local copies, waits for them, and re-layouts: 23.9 us -> 0.01 us  [body(): small[:3 * lines].reshape(3, width)]
  transfers between devices with their start and end apart: 21 -> 0, of which waited for: 18 -> 0; matrix products, arithmetic and copies ran while one was open for 8% -> 0% of each run, Pallas kernels for 0% -> 0%
where the time goes in v2:
time: 220 us; the launch traced here: 219 us
  Pallas kernels  197 us (90%)
  local copies, waits for them, and re-layouts  21.1 us (10%)
    pallas_call x1, Pallas kernels, run_layer(): pl.pallas_call(functools.partial(layer_kernel, (bits, rows, width, groups...  197 us
    unnamed x28, local copies, waits for them, and re-layouts  18.9 us

profile of v2, /device:TPU:0, one launch (start us, length us, event | category | flops | bytes accessed | tf_op | source)
XLA Modules:
  0.0 219.3 jit_solution(13706683233438361650)
XLA Ops:
  1.3 1.4 copy.37.refs_1_
  2.7 196.9 %layer.1 = (bf16[128,1024]{1,0:T(8,128)(2,1)}, f32[128,1024]{1,0:T(8,128)}, f32[32,1024]{1,0:T(8,128)}, f32[64,256]{1,0:T(8,128)}, f32[64,256]{1,0:T(8,128)}, /*...) custom-call(s32[1]{0:T(128)S(6)} %copy.53.refs_0_, ...), custom_call_target="tpu_custom_call" | custom-call | tf_op jit(solution)/shard_map/layer/pallas_call | solution.py:811
  199.6 0.0 copy-start.5
  199.6 0.0 copy-start.4
  199.6 0.0 copy-start.3
  199.6 0.0 copy-start.2
  199.6 0.0 copy-start.1
  199.6 0.0 copy-start
  199.6 0.8 slice.15
  200.4 0.7 slice.17
  201.1 0.7 copy.38
  201.8 0.1 constant_dynamic-slice_fusion
  201.9 0.5 slice_bitcast_fusion
  202.4 1.7 copy.54
  204.1 1.9 copy.55
  206.0 1.6 copy.56
  207.5 1.6 copy.57
  209.1 1.5 copy.58
  210.6 1.5 copy.59
  212.0 1.6 copy.60
  213.6 1.6 copy.61
  215.2 0.0 copy-done.5
  215.2 0.6 copy.62
  215.8 0.0 copy-done.4
  215.8 0.6 copy.63
  216.4 0.0 copy-done.3
  216.4 0.7 copy.64
  217.1 0.0 copy-done.2
  217.1 0.7 copy.65
  217.8 0.0 copy-done.1
  217.8 0.7 copy.66
  218.6 0.0 copy-done
  218.6 0.7 copy.67
  (1 shorter events, 0.0 us)
Async XLA Ops:
  199.6 15.6 %copy-start.5 = (f32[64,256]{1,0:T(8,128)S(1)}, f32[64,256]{1,0:T(8,128)}, u32[]{:S(2)}) copy-start(f32[64,256]{1,0:T(8,128)} %get-tuple-element.98) | copy-start | bytes 196612
  199.6 16.3 %copy-start.4 = (f32[64,256]{1,0:T(8,128)S(1)}, f32[64,256]{1,0:T(8,128)}, u32[]{:S(2)}) copy-start(f32[64,256]{1,0:T(8,128)} %get-tuple-element.99) | copy-start | bytes 196612
  199.6 16.9 %copy-start.3 = (f32[64,512]{1,0:T(8,128)S(1)}, f32[64,512]{1,0:T(8,128)}, u32[]{:S(2)}) copy-start(f32[64,512]{1,0:T(8,128)} %get-tuple-element.100) | copy-start | bytes 393220
  199.6 17.5 %copy-start.2 = (f32[64,1408]{1,0:T(8,128)S(1)}, f32[64,1408]{1,0:T(8,128)}, u32[]{:S(2)}) copy-start(f32[64,1408]{1,0:T(8,128)} %get-tuple-element.102) | copy-start | bytes 1081348
  199.6 18.3 %copy-start.1 = (f32[64,1408]{1,0:T(8,128)S(1)}, f32[64,1408]{1,0:T(8,128)}, u32[]{:S(2)}) copy-start(f32[64,1408]{1,0:T(8,128)} %get-tuple-element.103) | copy-start | bytes 1081348
  199.6 19.0 %copy-start = (f32[64,1408]{1,0:T(8,128)S(1)}, f32[64,1408]{1,0:T(8,128)}, u32[]{:S(2)}) copy-start(f32[64,1408]{1,0:T(8,128)} %get-tuple-element.104) | copy-start | bytes 1081348

commit v3 on v2

--- a/solution.py
+++ b/solution.py
@@ -21,6 +21,10 @@
 GELU_B = 0.044715
 
 NAMES = ("sk", "sv", "sq", "ck", "cv", "so", "cq", "co", "fg", "fu", "fd")
+LEFTS = ("ns", "nc", "nf", "gf", "gc", "gs", "mem")
+LEFT_OF = dict(
+    sk="ns", sv="ns", sq="ns", cq="nc", fg="nf", fu="nf", fd="gf", co="gc", so="gs", ck="mem", cv="mem"
+)
 
 
 def bucket_starts():
@@ -41,7 +45,46 @@
     return [(first, min(step, width - first)) for first in range(0, width, step)]
 
 
+class Stop(Exception):
+    pass
+
+
+class Copies:
+    def __init__(self):
+        self.made, self.started, self.received, self.sent = {}, [], set(), set()
+
+    def start(self, key, copy):
+        self.made[key] = copy
+        self.started.append(key)
+        copy.start()
+
+    def receive(self, key):
+        self.received.add(key)
+        copy = self.made[key]
+        if key[0] == "load":
+            copy.wait()
+        else:
+            copy.wait_recv()
+
+    def drain(self):
+        for key in self.started:
+            if key not in self.received:
+                self.receive(key)
+        for key in self.started:
+            if key[0] != "load":
+                self.made[key].wait_send()
+
+
 def layer_kernel(shapes, stop, *refs):
+    copies = Copies()
+    try:
+        layer_steps(copies, shapes, stop, *refs)
+    except Stop:
+        pass
+    copies.drain()
+
+
+def layer_steps(copies, shapes, stop, *refs):
     bits, rows, width, groups, mem_rows = shapes
     stages = bits + 1
     blk_count = 1 << bits
@@ -58,19 +101,25 @@
     weights_in = dict(zip(NAMES, take(11)))
     layer_out, hidden_grad, memory_grad = take(3)
     grads_out = dict(zip(NAMES, take(11)))
+    results = {"layer_out": layer_out, "hidden_grad": hidden_grad, "memory_grad": memory_grad, **grads_out}
     (small_out,) = take(1)
     weight = dict(zip(NAMES, take(11)))
-    landing = {name: take(stages) for name in NAMES}
+    left_own = dict(zip(LEFTS, take(len(LEFTS))))
+    left_all = dict(zip(LEFTS, take(len(LEFTS))))
+    right_all = dict(zip(NAMES, take(11)))
+    partial = dict(zip(NAMES, take(11)))
+    landing = {name: take(bits - 1) for name in NAMES}
+    staged = dict(zip(results, take(len(results))))
     (memory, kbuf, vbuf, vT, kT, tab, near, scores, qs, cqs, ags, att_self, att_cross) = take(13)
     (lse, probs, mk, mv, mkT, mvT, pushed, landed) = take(8)
-    (after_self, after_cross, cot, ns, ns_t, nc, nc_t, nf, nf_t, bg, bg_t) = take(11)
-    (att_tok, catt_tok, inner, gate_grad, up_grad, qgrad) = take(6)
+    (after_self, after_cross, cot, ns, nc, nf, bg) = take(7)
     (dkv,) = take(1)
     dkv_land = take(bits)
     (dmem,) = take(1)
     dmem_land = take(bits)
     (mem_push, mem_land, small, small_land, bias_sum) = take(5)
     (load_sem, hx_send, hx_recv, ag_send, ag_recv, rs_send, rs_recv) = take(7)
+    (lf_send, lf_recv, rt_send, rt_recv, out_sem) = take(5)
     (dk_send, dk_recv, dm_send, dm_recv, mg_send, mg_recv, sm_send, sm_recv) = take(8)
 
     seq, blk, head = (lax.axis_index(name) for name in ("seq", "blk", "head"))
@@ -81,6 +130,14 @@
 
     other_seq = (1 - seq, blk, head)
     other_head = (seq, blk, 1 - head)
+    next_blk = across(0)
+    member = 2 * seq + mine[0]
+    peers = (other_seq, next_blk, (1 - seq, next_blk[1], head))
+    peer_slots = (
+        2 * (1 - seq) + mine[0],
+        2 * seq + 1 - mine[0],
+        2 * (1 - seq) + 1 - mine[0],
+    )
 
     loads = {
         name: pltpu.make_async_copy(weights_in[name], weight[name], load_sem.at[slot])
@@ -88,31 +145,39 @@
     }
     memory_load = pltpu.make_async_copy(memory_in, memory, load_sem.at[len(NAMES)])
     for name in ("sk", "sv", "sq"):
-        loads[name].start()
-    memory_load.start()
+        copies.start(("load", name), loads[name])
+    copies.start(("load", "memory"), memory_load)
     for name in NAMES[3:]:
-        loads[name].start()
+        copies.start(("load", name), loads[name])
+
+    def checkpoint(place):
+        if stop == place:
+            raise Stop
 
     barrier = pltpu.get_barrier_semaphore()
-    friends = [other_seq, other_head, *(across(bit) for bit in range(bits))]
+    friends = [*peers, other_head, *(across(bit) for bit in range(1, bits))]
     for friend in friends:
         pl.semaphore_signal(barrier, inc=1, device_id=friend, device_id_type=MESH)
 
+    def give(name):
+        slot = list(results).index(name)
+        copies.start(
+            ("load", "out", name),
+            pltpu.make_async_copy(staged[name], results[name], out_sem.at[slot]),
+        )
+
     def whole(name, lanes=slice(None)):
-        value = weight[name][(Ellipsis, lanes)]
-        return value.reshape(width, value.shape[-1])
+        return weight[name][:, lanes]
 
     def row_tile(name, tile):
-        value = weight[name][tile // 2, tile % 2]
-        return value.reshape(TILE, value.shape[-1])
+        return weight[name][tile * TILE : (tile + 1) * TILE, :]
 
     def inverse_norm(values):
         return lax.rsqrt(jnp.mean(values * values, axis=-1, keepdims=True) + EPSILON)
 
-    def norm_into(values, gain, plain, turned):
-        result = (values * inverse_norm(values) * gain[...]).astype(BF)
-        plain[...] = result
-        turned[...] = result.T
+    def norm_into(values, gain, plain, left):
+        plain[...] = (values * inverse_norm(values) * gain[...]).astype(BF)
+        share_left(left, plain[...])
 
     def norm_back(values, gain, normed_grad, slot):
         scale = inverse_norm(values)
@@ -137,10 +202,10 @@
 
     def push(which, tile, value):
         pushed[which, tile] = value.astype(BF)
-        hx(which, tile).start()
+        copies.start(("hx", which, tile), hx(which, tile))
 
     def summed(which, tile):
-        hx(which, tile).wait_recv()
+        copies.receive(("hx", which, tile))
         return pushed[which, tile].astype(F32) + landed[which, tile].astype(F32)
 
     tiles = width // TILE
@@ -148,14 +213,84 @@
     def summed_all(which):
         return jnp.concatenate([summed(which, tile) for tile in range(tiles)], axis=1)
 
-    def bit_order(name):
-        if name in ("fd", "cq", "sq"):
-            return [*range(1, bits), 0]
-        return list(range(bits))
-
-    def bit_view(order, stage, keep):
+    def lanes_of(slot, size):
+        return pl.ds(pl.multiple_of(slot * size, size), size)
+
+    def left_place(name, slot):
+        if name == "mem":
+            return left_all[name].at[slot]
+        return left_all[name].at[(slice(None),) * bits + (lanes_of(slot, rows),)]
+
+    def share_left(name, value):
+        own = left_own[name]
+        turned = value.T
+        own[...] = turned.reshape(own.shape)
+        here = (seq, *(slice(None),) * (bits - 1), mine[0])
+        left_place(name, member)[...] = own[here]
+        slot = LEFTS.index(name)
+        for way, peer in enumerate(peers):
+            there = (peer[0], *(slice(None),) * (bits - 1), mine[0] if way == 0 else 1 - mine[0])
+            copies.start(
+                ("left", name, way),
+                pltpu.make_async_remote_copy(
+                    src_ref=own.at[there],
+                    dst_ref=left_place(name, member),
+                    send_sem=lf_send.at[slot, way],
+                    recv_sem=lf_recv.at[slot, way],
+                    device_id=peer,
+                    device_id_type=MESH,
+                ),
+            )
+
+    def right_copy(name, way):
+        slot = NAMES.index(name)
+        place = right_all[name].at[member if way < 2 else peer_slots[1]]
+        return pltpu.make_async_remote_copy(
+            src_ref=place,
+            dst_ref=place,
+            send_sem=rt_send.at[slot, way],
+            recv_sem=rt_recv.at[slot, way],
+            device_id=next_blk if way == 1 else other_seq,
+            device_id_type=MESH,
+        )
+
+    def share_right(name):
+        for way in (1, 0):
+            copies.start(("right", name, way), right_copy(name, way))
+
+    def pass_right(name):
+        copies.receive(("right", name, 1))
+        copies.start(("right", name, 2), right_copy(name, 2))
+
+    def make_partial(name):
+        left = LEFT_OF[name]
+        for way in range(3):
+            if ("left", left, way) not in copies.received:
+                copies.receive(("left", left, way))
+        copies.receive(("right", name, 0))
+        copies.receive(("right", name, 2))
+        out = partial[name]
+        count, depth, size = right_all[name].shape
+        for first, step in lane_tiles(size):
+            lanes = slice(first, first + step)
+            if left == "mem":
+                total = None
+                for slot in range(count):
+                    part = dot(
+                        left_all[left][slot].reshape(width // 4, depth), right_all[name][slot, :, lanes]
+                    )
+                    total = part if total is None else total + part
+            else:
+                total = dot(
+                    left_all[left][...].reshape(width // 4, count * depth),
+                    right_all[name][:, :, lanes].reshape(count * depth, step),
+                )
+            out[..., lanes] = total.astype(BF).reshape(*out.shape[:-1], step)
+        copies.start(("rs", name, 0), rs_copy(name, 0))
+
+    def bit_view(order, stage, keep, low_bit=0):
         index = []
-        for bit in reversed(range(bits)):
+        for bit in reversed(range(low_bit, bits)):
             place = order.index(bit)
             if place < stage:
                 index.append(mine[bit])
@@ -165,54 +300,39 @@
                 index.append(slice(None))
         return tuple(index)
 
+    rs_order = list(range(1, bits))
+
     def rs_view(name, stage, keep):
-        if stage == 0:
-            return weight[name].at[seq if keep else 1 - seq]
-        return weight[name].at[(seq, *bit_view(bit_order(name), stage - 1, keep))]
+        return partial[name].at[bit_view(rs_order, stage, keep, 1)]
 
     def rs_copy(name, stage):
         slot = NAMES.index(name)
-        target = other_seq if stage == 0 else across(bit_order(name)[stage - 1])
         return pltpu.make_async_remote_copy(
             src_ref=rs_view(name, stage, False),
             dst_ref=landing[name][stage],
             send_sem=rs_send.at[slot, stage],
             recv_sem=rs_recv.at[slot, stage],
-            device_id=target,
+            device_id=across(rs_order[stage]),
             device_id_type=MESH,
         )
-
-    def rs_start(name):
-        rs_copy(name, 0).start()
 
     def fold_into(kept, got):
         lead = got.shape[:-2]
-        total = int(np.prod(lead))
-
-        def body(flat, carry):
-            index, left = [], flat
-            for extent in reversed(lead):
-                index.append(lax.rem(left, extent))
-                left = left // extent
-            index = tuple(reversed(index))
+        for flat in range(int(np.prod(lead))):
+            index = tuple(int(value) for value in np.unravel_index(flat, lead)) if lead else (Ellipsis,)
             kept[index] = (kept[index].astype(F32) + got[index].astype(F32)).astype(BF)
-            return carry
-
-        if total == 1:
-            kept[...] = (kept[...].astype(F32) + got[...].astype(F32)).astype(BF)
-        else:
-            lax.fori_loop(0, total, body, 0)
 
     def rs_step(name, stage):
-        rs_copy(name, stage).wait_recv()
+        copies.receive(("rs", name, stage))
         kept, got = rs_view(name, stage, True), landing[name][stage]
-        if stage == stages - 1:
-            grads_out[name][...] = kept[...].astype(F32) + got[...].astype(F32)
+        if stage == bits - 2:
+            staged[name][...] = kept[...].astype(F32) + got[...].astype(F32)
+            give(name)
         else:
             fold_into(kept, got)
-            rs_copy(name, stage + 1).start()
-
-    def part_copy(buffer, land, send, recv, stage):
+            copies.start(("rs", name, stage + 1), rs_copy(name, stage + 1))
+
+    def part_copy(tag, buffer, land, send, recv, stage):
         order = list(range(bits))
         return pltpu.make_async_remote_copy(
             src_ref=buffer.at[bit_view(order, stage, False)],
@@ -223,24 +343,28 @@
             device_id_type=MESH,
         )
 
-    def part_step(buffer, land, send, recv, stage):
+    def part_start(tag, buffer, land, send, recv, stage):
+        copies.start((tag, stage), part_copy(tag, buffer, land, send, recv, stage))
+
+    def part_step(tag, buffer, land, send, recv, stage):
         order = list(range(bits))
-        part_copy(buffer, land, send, recv, stage).wait_recv()
+        copies.receive((tag, stage))
         kept = buffer.at[bit_view(order, stage, True)]
         if stage == bits - 1:
             return kept[...].astype(F32) + land[stage][...].astype(F32)
         fold_into(kept, land[stage])
-        part_copy(buffer, land, send, recv, stage + 1).start()
+        part_start(tag, buffer, land, send, recv, stage + 1)
 
     def dkv_args(pair):
         return (
+            ("dkv", pair),
             dkv.at[pair],
             [land.at[pair] for land in dkv_land],
             dk_send.at[pair],
             dk_recv.at[pair],
         )
 
-    dmem_args = (dmem, dmem_land, dm_send, dm_recv)
+    dmem_args = ("dmem", dmem, dmem_land, dm_send, dm_recv)
 
     def ag_copy(which, step):
         bit = bits - 1 - step
@@ -259,9 +383,9 @@
 
     def ag_next(step):
         for which in range(2):
-            ag_copy(which, step).wait_recv()
+            copies.receive(("ag", which, step))
             if step + 1 < bits:
-                ag_copy(which, step + 1).start()
+                copies.start(("ag", which, step + 1), ag_copy(which, step + 1))
 
     def half_index(chunk):
         index, left = [], chunk
@@ -313,26 +437,29 @@
             parts.append(jnp.where(key_row + block * rows < length, part, MASKED))
         return jnp.concatenate(parts, axis=0)
 
+    checkpoint(0)
+    pl.semaphore_wait(barrier, len(friends))
     x = hidden[...].astype(F32)
-    norm_into(x, ln_self, ns, ns_t)
-    loads["sk"].wait()
+    norm_into(x, ln_self, ns, "ns")
+    copies.receive(("load", "sk"))
     keys = dot(ns[...], whole("sk")).astype(BF)
     for pair in range(pairs):
         kbuf[(pair, *reversed(mine))] = keys[:, pair * 128 : (pair + 1) * 128]
-    pl.semaphore_wait(barrier, len(friends))
-    ag_copy(0, 0).start()
-    loads["sv"].wait()
+    copies.start(("ag", 0, 0), ag_copy(0, 0))
+    copies.receive(("load", "sv"))
     values = dot(ns[...], whole("sv")).astype(BF)
     for pair in range(pairs):
         vbuf[(pair, *reversed(mine))] = values[:, pair * 128 : (pair + 1) * 128]
-    ag_copy(1, 0).start()
-    loads["sq"].wait()
+    copies.start(("ag", 1, 0), ag_copy(1, 0))
+    copies.receive(("load", "sq"))
     split_heads(dot(ns[...], whole("sq")).astype(BF), qs)
     ag_next(0)
 
-    memory_load.wait()
+    copies.receive(("load", "memory"))
+    share = mem_rows // blk_count
+    share_left("mem", memory[pl.ds(pl.multiple_of(blk * share, share), share), :])
     for source, plain, turned in (("ck", mk, mkT), ("cv", mv, mvT)):
-        loads[source].wait()
+        copies.receive(("load", source))
         result = dot(memory[...], whole(source)).astype(BF)
         for pair in range(pairs):
             plain[pair] = result[:, pair * 128 : (pair + 1) * 128]
@@ -340,14 +467,15 @@
     if bits > 1:
         ag_next(1)
 
+    checkpoint(2)
     starts = bucket_starts()
     distance = lane - lax.broadcasted_iota(jnp.int32, (rows, 128), 0)
 
     def bias_of(which, head_slot):
         shifted = distance + (rows if which == 1 else 0)
-        value = jnp.full((rows, 128), rel_bias[0, head_slot], F32)
+        value = jnp.full((rows, 128), rel_bias[head_slot, 0], F32)
         for bucket, start in enumerate(starts):
-            value = jnp.where(shifted >= start, rel_bias[bucket + 1, head_slot], value)
+            value = jnp.where(shifted >= start, rel_bias[head_slot, bucket + 1], value)
         if which == 2:
             value = jnp.where(shifted >= 0, value, MASKED)
         return value
@@ -355,7 +483,7 @@
     def bias_tables(head_slot, carry):
         group = head_slot // 2
         lanes = pl.ds(pl.multiple_of(lax.rem(head_slot, 2) * rows, rows), rows)
-        tab[0, group, :, lanes] = jnp.full((rows, rows), rel_bias[BUCKETS - 1, head_slot], F32)
+        tab[0, group, :, lanes] = jnp.full((rows, rows), rel_bias[head_slot, BUCKETS - 1], F32)
         tab[1, group, :, lanes] = bias_of(1, head_slot)
         tab[2, group, :, lanes] = bias_of(2, head_slot)
         tab[3, group, :, lanes] = jnp.full((rows, rows), MASKED, F32)
@@ -409,21 +537,24 @@
         precise = acc / total
         att_self[group] = precise
         lse[group] = tops + jnp.log(total)
-        att_tok[:, group * 128 : (group + 1) * 128] = join_heads(precise).astype(BF)
-
+        right_all["so"][member, :, group * 128 : (group + 1) * 128] = join_heads(precise).astype(BF)
+
+    checkpoint(4)
     for group in range(groups):
         attend(group)
 
-    loads["so"].wait()
+    checkpoint(5)
+    copies.receive(("load", "so"))
     for tile in range(tiles):
-        push(0, tile, dot_nt(att_tok[...], row_tile("so", tile)))
+        push(0, tile, dot_nt(right_all["so"][member], row_tile("so", tile)))
     valid = lax.broadcasted_iota(jnp.int32, (rows, 1), 0) + blk * rows < length
     bg[...] = jnp.where(valid, out_grad[...].astype(F32), 0.0).astype(BF)
-    bg_t[...] = bg[...].T
+    share_left("gf", bg[...])
     after_self[...] = x + summed_all(0)
 
-    norm_into(after_self[...], ln_cross, nc, nc_t)
-    loads["cq"].wait()
+    checkpoint(6)
+    norm_into(after_self[...], ln_cross, nc, "nc")
+    copies.receive(("load", "cq"))
     split_heads(dot(nc[...], whole("cq")).astype(BF), cqs)
     for group in range(groups):
         part = dot_nt(mk[group // 2], cqs[group])
@@ -432,59 +563,56 @@
         probs[group] = part
         acc = dot(mvT[group * HEAD_DIM : (group + 1) * HEAD_DIM, :], part.astype(BF))
         att_cross[group] = acc
-        catt_tok[:, group * 128 : (group + 1) * 128] = join_heads(acc).astype(BF)
-    loads["co"].wait()
+        right_all["co"][member, :, group * 128 : (group + 1) * 128] = join_heads(acc).astype(BF)
+    checkpoint(7)
+    copies.receive(("load", "co"))
     for tile in range(tiles):
-        push(1, tile, dot_nt(catt_tok[...], row_tile("co", tile)))
+        push(1, tile, dot_nt(right_all["co"][member], row_tile("co", tile)))
+    share_right("so")
+    share_right("co")
     after_cross[...] = after_self[...] + summed_all(1)
 
-    norm_into(after_cross[...], ln_ffn, nf, nf_t)
+    checkpoint(8)
+    norm_into(after_cross[...], ln_ffn, nf, "nf")
     for name in ("fg", "fu", "fd"):
-        loads[name].wait()
-    for first, size in lane_tiles(inner.shape[1]):
+        copies.receive(("load", name))
+    for first, size in lane_tiles(weight["fg"].shape[1]):
         lanes = slice(first, first + size)
         gate = dot(nf[...], whole("fg", lanes))
         up = dot(nf[...], whole("fu", lanes))
         back = dot(bg[...], whole("fd", lanes))
         bent = jnp.tanh(GELU_A * (gate + GELU_B * gate * gate * gate))
-        share = 0.5 * (1.0 + bent)
-        slope = share + 0.5 * gate * (1.0 - bent * bent) * (
+        opened = 0.5 * (1.0 + bent)
+        slope = opened + 0.5 * gate * (1.0 - bent * bent) * (
             GELU_A * (1.0 + 3.0 * GELU_B * gate * gate)
         )
-        bell = gate * share
-        inner[:, lanes] = (bell * up).astype(BF)
-        gate_grad[:, lanes] = (back * up * slope).astype(BF)
-        up_grad[:, lanes] = (back * bell).astype(BF)
+        bell = gate * opened
+        right_all["fd"][member, :, lanes] = (bell * up).astype(BF)
+        right_all["fg"][member, :, lanes] = (back * up * slope).astype(BF)
+        right_all["fu"][member, :, lanes] = (back * bell).astype(BF)
+    for name in ("fd", "fg", "fu"):
+        share_right(name)
     for tile in range(tiles):
         push(
             2,
             tile,
-            dot_nt(gate_grad[...], row_tile("fg", tile)) + dot_nt(up_grad[...], row_tile("fu", tile)),
+            dot_nt(right_all["fg"][member], row_tile("fg", tile))
+            + dot_nt(right_all["fu"][member], row_tile("fu", tile)),
         )
     for tile in range(tiles):
-        push(3, tile, dot_nt(inner[...], row_tile("fd", tile)))
-
-    def weight_grad(name, turned, right):
-        for first, size in lane_tiles(right.shape[1]):
-            lanes = slice(first, first + size)
-            for tile in range(tiles):
-                result = dot(turned[tile * TILE : (tile + 1) * TILE, :], right[:, lanes]).astype(BF)
-                shape = weight[name].shape[2:-1]
-                weight[name][(tile // 2, tile % 2, Ellipsis, lanes)] = result.reshape(*shape, size)
-        rs_start(name)
-
-    weight_grad("fd", bg_t, inner)
-    weight_grad("fg", nf_t, gate_grad)
-    weight_grad("fu", nf_t, up_grad)
+        push(3, tile, dot_nt(right_all["fd"][member], row_tile("fd", tile)))
+
+    pass_right("so")
+    pass_right("co")
+    pass_right("fd")
     normed_grad = summed_all(2)
     cot[...] = jnp.where(valid, out_grad[...].astype(F32), 0.0) + norm_back(
         after_cross[...], ln_ffn, normed_grad, 2
     )
     bg[...] = cot[...].astype(BF)
-    bg_t[...] = bg[...].T
-
-    for name in ("fd", "fg", "fu"):
-        rs_step(name, 0)
+    share_left("gc", bg[...])
+
+    checkpoint(10)
     back = dot(bg[...], whole("co")).astype(BF)
     split_heads(back, ags)
     for pair in range(pairs):
@@ -494,7 +622,7 @@
             prob_grad = dot_nt(mv[pair], ags[group])
             score_grad = (prob * (prob_grad - head_deltas(back, att_cross, group))).astype(BF)
             turned = dot(mkT[group * HEAD_DIM : (group + 1) * HEAD_DIM, :], score_grad)
-            qgrad[:, group * 128 : (group + 1) * 128] = join_heads(turned).astype(BF)
+            right_all["cq"][member, :, group * 128 : (group + 1) * 128] = join_heads(turned).astype(BF)
             key_new = dot(score_grad, cqs[group])
             value_new = dot(prob.astype(BF), ags[group])
             key_part = key_new if key_part is None else key_part + key_new
@@ -504,27 +632,30 @@
         dmem[..., (pairs + pair) * 128 : (pairs + pair + 1) * 128] = value_part.astype(BF).reshape(
             *shape, 128
         )
+    checkpoint(11)
     for tile in range(tiles):
-        push(4, tile, dot_nt(qgrad[...], row_tile("cq", tile)))
-    part_copy(*dmem_args, 0).start()
-    weight_grad("co", bg_t, catt_tok)
-    weight_grad("cq", nc_t, qgrad)
+        push(4, tile, dot_nt(right_all["cq"][member], row_tile("cq", tile)))
+    part_start(*dmem_args, 0)
+    share_right("cq")
+    make_partial("fd")
+    pass_right("fg")
+    make_partial("co")
     for tile in range(tiles):
         lanes = slice(tile * TILE, (tile + 1) * TILE)
-        layer_out[:, lanes] = (after_cross[:, lanes] + summed(3, tile)).astype(BF)
+        staged["layer_out"][:, lanes] = (after_cross[:, lanes] + summed(3, tile)).astype(BF)
+    give("layer_out")
     normed_grad = summed_all(4)
     cot[...] = cot[...] + norm_back(after_self[...], ln_cross, normed_grad, 1)
     bg[...] = cot[...].astype(BF)
-    bg_t[...] = bg[...].T
-
+    share_left("gs", bg[...])
+
+    checkpoint(12)
     back = dot(bg[...], whole("so")).astype(BF)
     split_heads(back, ags)
     part_step(*dmem_args, 0)
-    rs_step("fg", 1)
-    rs_step("fd", 1)
+    make_partial("fg")
+    pass_right("fu")
     near[1] = jnp.zeros(near.shape[1:], BF)
-    for name in ("co", "cq"):
-        rs_step(name, 0)
     for pair in range(pairs):
         members = (2 * pair, 2 * pair + 1)
         deltas = [head_deltas(back, att_self, group) for group in members]
@@ -566,46 +697,63 @@
                 state = visit(chunk, state)
         else:
             state = lax.fori_loop(0, half_count, visit, state)
-        part_copy(*dkv_args(pair), 0).start()
+        part_start(*dkv_args(pair), 0)
         for slot, group in enumerate(members):
-            qgrad[:, group * 128 : (group + 1) * 128] = join_heads(state[2 * slot]).astype(BF)
+            right_all["sq"][member, :, group * 128 : (group + 1) * 128] = join_heads(
+                state[2 * slot]
+            ).astype(BF)
             bias_sum[BUCKETS : BUCKETS + 1, group * 2 * rows : (group + 1) * 2 * rows] = state[
                 2 * slot + 1
             ]
+    checkpoint(13)
+    share_right("sq")
+    make_partial("fu")
     part_step(*dkv_args(0), 0)
     part_step(*dmem_args, 1)
-    weight_grad("so", bg_t, att_tok)
-    rs_step("fu", 1)
+    pass_right("cq")
+    rs_step("fd", 0)
+    make_partial("so")
     part_step(*dkv_args(1), 0)
-    rs_step("fg", 2)
+    make_partial("cq")
     mem_sum = None
     for step in range(2, bits):
         mem_sum = part_step(*dmem_args, step)
+    mem_sum = mem_sum.astype(BF)
+    right_all["ck"][member] = mem_sum[:, : pairs * 128]
+    right_all["cv"][member] = mem_sum[:, pairs * 128 :]
+    share_right("ck")
+    share_right("cv")
+    query_part = [
+        dot_nt(right_all["sq"][member], row_tile("sq", tile)) for tile in range(tiles)
+    ]
     for step in range(1, bits - 1):
         part_step(*dkv_args(0), step)
-    query_part = [
-        dot_nt(qgrad[...], row_tile("sq", tile)) for tile in range(tiles)
-    ]
-    weight_grad("sq", ns_t, qgrad)
+    rs_step("co", 0)
+    rs_step("fg", 0)
     for step in range(1, bits - 1):
         part_step(*dkv_args(1), step)
+    pass_right("sq")
     sums = [part_step(*dkv_args(pair), bits - 1).astype(BF) for pair in range(pairs)]
-    kgrad = jnp.concatenate([value[:, :128] for value in sums], axis=1)
-    vgrad = jnp.concatenate([value[:, 128:] for value in sums], axis=1)
+    for pair, value in enumerate(sums):
+        right_all["sk"][member, :, pair * 128 : (pair + 1) * 128] = value[:, :128]
+        right_all["sv"][member, :, pair * 128 : (pair + 1) * 128] = value[:, 128:]
+    share_right("sk")
+    share_right("sv")
     for tile in range(tiles):
         push(
             5,
             tile,
             query_part[tile]
-            + dot_nt(kgrad, row_tile("sk", tile))
-            + dot_nt(vgrad, row_tile("sv", tile)),
-        )
-    weight_grad("sk", ns_t, kgrad)
-    weight_grad("sv", ns_t, vgrad)
-
-    share = mem_rows // blk_count
-    mem_sum = mem_sum.astype(BF)
-    mkg, mvg = mem_sum[:, : pairs * 128], mem_sum[:, pairs * 128 :]
+            + dot_nt(right_all["sk"][member], row_tile("sk", tile))
+            + dot_nt(right_all["sv"][member], row_tile("sv", tile)),
+        )
+    pass_right("ck")
+    pass_right("cv")
+    make_partial("sq")
+    rs_step("fu", 0)
+
+    checkpoint(14)
+    mkg, mvg = right_all["ck"][member], right_all["cv"][member]
     mem_part = dot_nt(mkg, whole("ck")) + dot_nt(mvg, whole("cv"))
     half = share // 2
     mem_push[0] = mem_part[:half, :].astype(BF)
@@ -618,12 +766,13 @@
         device_id=other_head,
         device_id_type=MESH,
     )
-    mem_copy.start()
-    own_rows = memory[pl.ds(pl.multiple_of(blk * share, share), share), :]
-    own_turned = own_rows.T
-    weight_grad("ck", own_turned, mkg)
-    weight_grad("cv", own_turned, mvg)
-
+    copies.start(("mem",), mem_copy)
+    pass_right("sk")
+    pass_right("sv")
+    rs_step("so", 0)
+    rs_step("cq", 0)
+
+    checkpoint(15)
     def bucket_line(group, lower, upper):
         line = jnp.zeros((1, 2 * rows), F32)
         wide = jnp.concatenate([distance, distance], axis=1)
@@ -654,8 +803,10 @@
     first_bias = 3 * (width // 128)
     small[0, first_bias : first_bias + BUCKETS, :] = bias_grad
 
+    checkpoint(16)
     normed_grad = summed_all(5)
-    hidden_grad[...] = cot[...] + norm_back(hidden[...].astype(F32), ln_self, normed_grad, 0)
+    staged["hidden_grad"][...] = cot[...] + norm_back(hidden[...].astype(F32), ln_self, normed_grad, 0)
+    give("hidden_grad")
 
     def small_copy(stage):
         return pltpu.make_async_remote_copy(
@@ -667,41 +818,81 @@
             device_id_type=MESH,
         )
 
-    small_copy(0).start()
-    done = {"fd": 2, "fg": 3, "fu": 2, "co": 1, "cq": 1}
-    order = ("fu", "fd", "fg", "co", "cq", "so", "sq", "sk", "sv", "ck", "cv")
-    for sweep in range(stages):
-        small_copy(sweep).wait_recv()
-        total = small[sweep] + small_land[sweep]
-        if sweep < stages - 1:
-            small[sweep + 1] = total
-            small_copy(sweep + 1).start()
+    def small_step(stage):
+        copies.receive(("small", stage))
+        total = small[stage] + small_land[stage]
+        if stage < stages - 1:
+            small[stage + 1] = total
+            copies.start(("small", stage + 1), small_copy(stage + 1))
         else:
             small_out[...] = total
-        for name in order:
-            at = done.get(name, 0)
-            if at < stages:
-                rs_step(name, at)
-                done[name] = at + 1
-    mem_copy.wait_recv()
-    memory_grad[...] = mem_push[head].astype(F32) + mem_land[...].astype(F32)
-
-    for name in NAMES:
-        for stage in range(stages):
-            rs_copy(name, stage).wait_send()
-    for stage in range(stages):
-        small_copy(stage).wait_send()
-    for which in range(6):
-        for tile in range(tiles):
-            hx(which, tile).wait_send()
-    for which in range(2):
-        for step in range(bits):
-            ag_copy(which, step).wait_send()
-    for step in range(bits):
-        part_copy(*dmem_args, step).wait_send()
-        for pair in range(pairs):
-            part_copy(*dkv_args(pair), step).wait_send()
-    mem_copy.wait_send()
+
+    copies.start(("small", 0), small_copy(0))
+    for name in ("ck", "cv", "sk", "sv"):
+        make_partial(name)
+    small_step(0)
+    for name in ("fd", "co", "fg", "fu", "so", "cq"):
+        for step in range(1, bits - 1):
+            rs_step(name, step)
+    rs_step("sq", 0)
+    small_step(1)
+    for step in range(1, bits - 1):
+        rs_step("sq", step)
+    for name in ("ck", "cv", "sk", "sv"):
+        rs_step(name, 0)
+    small_step(2)
+    for step in range(1, bits - 1):
+        for name in ("ck", "cv", "sk", "sv"):
+            rs_step(name, step)
+    for stage in range(3, stages):
+        small_step(stage)
+    copies.receive(("mem",))
+    staged["memory_grad"][...] = mem_push[head].astype(F32) + mem_land[...].astype(F32)
+    give("memory_grad")
+
+
+def finish_kernel(count, lines, width, *refs):
+    sources, small = refs[:count], refs[count]
+    targets = refs[count + 1 : 2 * count + 1]
+    gain_out, bias_out, sems = refs[2 * count + 1 : 2 * count + 4], refs[2 * count + 4], refs[-1]
+    moves = [
+        pltpu.make_async_copy(source, target, sems.at[slot])
+        for slot, (source, target) in enumerate(zip(sources, targets))
+    ]
+    for move in moves:
+        move.start()
+    share = gain_out[0].shape[0]
+    per_line = 128 // share
+    place = lax.axis_index("seq") * lax.axis_size("blk") + lax.axis_index("blk")
+    for slot, target in enumerate(gain_out):
+        line = small[pl.ds(slot * lines + place // per_line, 1), :]
+        for part in range(per_line):
+
+            @pl.when(lax.rem(place, per_line) == part)
+            def _(target=target, line=line, part=part):
+                target[...] = line[0, part * share : (part + 1) * share]
+
+    bias_out[...] = small[3 * lines :, :].T[: bias_out.shape[0], :]
+    for move in moves:
+        move.wait()
+
+
+def finish(results, small, width, share, heads):
+    count = len(results)
+    in_any = pl.BlockSpec(memory_space=pl.ANY)
+    in_vmem = pl.BlockSpec(memory_space=pltpu.VMEM)
+    return pl.pallas_call(
+        functools.partial(finish_kernel, count, width // 128, width),
+        out_shape=[
+            *(jax.ShapeDtypeStruct(result.shape, result.dtype) for result in results),
+            *[jax.ShapeDtypeStruct((share,), F32)] * 3,
+            jax.ShapeDtypeStruct((heads, BUCKETS), F32),
+        ],
+        in_specs=[in_vmem] * (count + 1),
+        out_specs=[*[in_any] * count, *[in_vmem] * 4],
+        scratch_shapes=[pltpu.SemaphoreType.DMA((count,))],
+        name="finish",
+    )(*results, small)
 
 
 def run_layer(lengths, rel_bias, hidden, out_grad, gains, memory, weights, blk_count, stop=None):
@@ -717,19 +908,29 @@
     half_count = blk_count // 2
     stored = 1 if half_count > 4 else half_count
     piece = width // (2 * blk_count)
-    lead = (2,) * (bits + 1)
     widths = {name: weights[name].shape[1] for name in NAMES}
-    shaped = [weights[name].reshape(*lead, piece, widths[name]) for name in NAMES]
-    units = widths["fg"]
     share = mem_rows // blk_count
     small_rows = 3 * (width // 128) + BUCKETS
 
     vm, sem = pltpu.VMEM, pltpu.SemaphoreType.DMA
-    scratch = [vm((*lead, piece, widths[name]), BF) for name in NAMES]
+    high = (2,) * (bits - 1)
+    depth = {name: share if LEFT_OF[name] == "mem" else rows for name in NAMES}
+    scratch = [vm((width, widths[name]), BF) for name in NAMES]
+    scratch += [
+        vm((2, *high, 2, piece, share if left == "mem" else rows), BF) for left in LEFTS
+    ]
+    scratch += [
+        vm((4, *high, piece, share) if left == "mem" else (*high, piece, 4 * rows), BF)
+        for left in LEFTS
+    ]
+    scratch += [vm((4, depth[name], widths[name]), BF) for name in NAMES]
+    scratch += [vm((*high, piece, widths[name]), BF) for name in NAMES]
     for name in NAMES:
-        for stage in range(stages):
-            scratch.append(vm((2,) * (bits - stage) + (piece, widths[name]), BF))
+        for stage in range(bits - 1):
+            scratch.append(vm((2,) * (bits - 2 - stage) + (piece, widths[name]), BF))
     by_bit = (2,) * bits
+    scratch += [vm((rows, width), BF), vm((rows, width), F32), vm((share // 2, width), F32)]
+    scratch += [vm((piece, widths[name]), F32) for name in NAMES]
     scratch += [
         vm(memory.shape, BF),
         vm((pairs, *by_bit, rows, 128), BF),
@@ -756,19 +957,9 @@
         vm((rows, width), F32),
         vm((rows, width), F32),
         vm((rows, width), BF),
-        vm((width, rows), BF),
         vm((rows, width), BF),
-        vm((width, rows), BF),
         vm((rows, width), BF),
-        vm((width, rows), BF),
         vm((rows, width), BF),
-        vm((width, rows), BF),
-        vm((rows, heads * HEAD_DIM), BF),
-        vm((rows, heads * HEAD_DIM), BF),
-        vm((rows, units), BF),
-        vm((rows, units), BF),
-        vm((rows, units), BF),
-        vm((rows, heads * HEAD_DIM), BF),
         vm((pairs, *by_bit, rows, 256), BF),
     ]
     scratch += [vm((pairs, *(2,) * (bits - 1 - stage), rows, 256), BF) for stage in range(bits)]
@@ -787,8 +978,13 @@
         sem((6, width // TILE)),
         sem((2, bits)),
         sem((2, bits)),
-        sem((len(NAMES), stages)),
-        sem((len(NAMES), stages)),
+        sem((len(NAMES), bits - 1)),
+        sem((len(NAMES), bits - 1)),
+        sem((len(LEFTS), 3)),
+        sem((len(LEFTS), 3)),
+        sem((len(NAMES), 3)),
+        sem((len(NAMES), 3)),
+        sem((3 + len(NAMES),)),
         sem((pairs, bits)),
         sem((pairs, bits)),
         sem((bits,)),
@@ -812,13 +1008,15 @@
         functools.partial(layer_kernel, (bits, rows, width, groups, mem_rows), stop),
         out_shape=out_shape,
         in_specs=[in_smem, in_smem, *[in_vmem] * 5, *[in_any] * 12],
-        out_specs=[in_vmem] * len(out_shape),
+        out_specs=[*[in_any] * (len(out_shape) - 1), in_vmem],
         scratch_shapes=scratch,
         compiler_params=pltpu.CompilerParams(
-            collective_id=0, has_side_effects=True, vmem_limit_bytes=62 * 1024 * 1024
+            collective_id=0, has_side_effects=True, vmem_limit_bytes=63 * 1024 * 1024
         ),
         name="layer",
-    )(lengths, rel_bias, hidden, out_grad, *gains, memory, *shaped)
+    )(
+        lengths, rel_bias, hidden, out_grad, *gains, memory, *(weights[name] for name in NAMES)
+    )
     return results[:3], dict(zip(NAMES, results[3:-1])), results[-1]
 
 
@@ -860,29 +1058,30 @@
     )
     gains = [gain.reshape(1, width) for gain in (ln_self, ln_cross, ln_ffn)]
     (layer_out, hidden_grad, memory_grad), grads, small = run_layer(
-        lengths, rel_bias, hidden, out_grad, gains, memory, weights, blk_count
+        lengths, rel_bias.T, hidden, out_grad, gains, memory, weights, blk_count
     )
-    lines = width // 128
-    share = width // (2 * blk_count)
-    first = (lax.axis_index("seq") * blk_count + lax.axis_index("blk")) * share
-    gain_grads = lax.dynamic_slice(small[: 3 * lines].reshape(3, width), (0, first), (3, share))
-    bias_grad = small[3 * lines :, : rel_bias.shape[1]]
+    kept = [layer_out, hidden_grad, memory_grad, *(grads[name] for name in NAMES)]
+    *kept, self_gain, cross_gain, ffn_gain, bias_grad = finish(
+        kept, small, width, width // (2 * blk_count), rel_bias.shape[1]
+    )
+    layer_out, hidden_grad, memory_grad = kept[:3]
+    grads = dict(zip(NAMES, kept[3:]))
     return (
         layer_out,
         hidden_grad,
         memory_grad,
-        gain_grads[0],
+        self_gain,
         grads["sq"],
         grads["sk"],
         grads["sv"],
         grads["so"],
-        bias_grad,
-        gain_grads[1],
+        bias_grad.T,
+        cross_gain,
         grads["cq"],
         grads["ck"],
         grads["cv"],
         grads["co"],
-        gain_grads[2],
+        ffn_gain,
         grads["fg"],
         grads["fu"],
         grads["fd"],

time: 220 us -> 164 us (0.75)
  Pallas kernels: 197 us -> 163 us
  local copies, waits for them, and re-layouts: 21.1 us -> 0 us
    pallas_call x1, Pallas kernels: 197 us -> 159 us  [run_layer(): pl.pallas_call(functools.partial(layer_kernel, (bits, rows, width, groups...]
    unnamed x28 -> x0, local copies, waits for them, and re-layouts: 18.9 us -> none
    pallas_call x0 -> x1, Pallas kernels: none -> 4.03 us  [finish(): pl.pallas_call(functools.partial(finish_kernel, count, width // 128, widt...]
where the time goes in v3:
time: 164 us
  Pallas kernels  163 us (99%)
    pallas_call x1, Pallas kernels, run_layer(): pl.pallas_call(functools.partial(layer_kernel, (bits, rows, width, groups...  159 us
    pallas_call x1, Pallas kernels, finish(): pl.pallas_call(functools.partial(finish_kernel, count, width // 128, widt...  4.03 us

profile of v3, /device:TPU:0, one launch (start us, length us, event | category | flops | bytes accessed | tf_op | source)
XLA Modules:
  0.0 164.1 jit_solution(4217605594372351434)
XLA Ops:
  1.3 158.5 %layer.1 = (bf16[128,1024]{1,0:T(8,128)(2,1)}, f32[128,1024]{1,0:T(8,128)}, f32[32,1024]{1,0:T(8,128)}, f32[64,256]{1,0:T(8,128)}, f32[64,256]{1,0:T(8,128)}, /*...) custom-call(s32[1]{0:T(128)S(6)} %copy.37.refs_0_, ...), custom_call_target="tpu_custom_call" | custom-call | tf_op jit(solution)/shard_map/layer/pallas_call | solution.py:1007
  159.9 4.0 %finish.1 = (bf16[128,1024]{1,0:T(8,128)(2,1)}, f32[128,1024]{1,0:T(8,128)}, f32[32,1024]{1,0:T(8,128)}, f32[64,256]{1,0:T(8,128)}, f32[64,256]{1,0:T(8,128)}, /...) custom-call(bf16[128,1024]{1,0:T(8,128)(2,1)} %get-tuple-element.51., ...), custom_call_target="tpu_custom_call" | custom-call | tf_op jit(solution)/shard_map/finish/pallas_call | solution.py:884

commit v4 on v3

--- a/solution.py
+++ b/solution.py
@@ -43,6 +43,12 @@
 
 def lane_tiles(width, step=512):
     return [(first, min(step, width - first)) for first in range(0, width, step)]
+SHARED_BIT = dict(gf=1, gc=1, gs=1)
+DIRECT = ("ck", "cv", "sk", "sv")
+
+
+def shared_bit(name):
+    return SHARED_BIT.get(LEFT_OF.get(name, name), 0)
 
 
 class Stop(Exception):
@@ -52,6 +58,7 @@
 class Copies:
     def __init__(self):
         self.made, self.started, self.received, self.sent = {}, [], set(), set()
+        self.last = []
 
     def start(self, key, copy):
         self.made[key] = copy
@@ -66,13 +73,19 @@
         else:
             copy.wait_recv()
 
+    def leave(self, key):
+        self.sent.add(key)
+        self.made[key].wait_send()
+
     def drain(self):
         for key in self.started:
             if key not in self.received:
                 self.receive(key)
         for key in self.started:
-            if key[0] != "load":
-                self.made[key].wait_send()
+            if key[0] != "load" and key not in self.sent:
+                self.leave(key)
+        for wait in self.last:
+            wait()
 
 
 def layer_kernel(shapes, stop, *refs):
@@ -108,7 +121,7 @@
     left_all = dict(zip(LEFTS, take(len(LEFTS))))
     right_all = dict(zip(NAMES, take(11)))
     partial = dict(zip(NAMES, take(11)))
-    landing = {name: take(bits - 1) for name in NAMES}
+    landing = {name: take(1 if name in DIRECT else bits - 1) for name in NAMES}
     staged = dict(zip(results, take(len(results))))
     (memory, kbuf, vbuf, vT, kT, tab, near, scores, qs, cqs, ags, att_self, att_cross) = take(13)
     (lse, probs, mk, mv, mkT, mvT, pushed, landed) = take(8)
@@ -117,7 +130,7 @@
     dkv_land = take(bits)
     (dmem,) = take(1)
     dmem_land = take(bits)
-    (mem_push, mem_land, small, small_land, bias_sum) = take(5)
+    (mem_push, mem_land, small, small_far, far_sum) = take(5)
     (load_sem, hx_send, hx_recv, ag_send, ag_recv, rs_send, rs_recv) = take(7)
     (lf_send, lf_recv, rt_send, rt_recv, out_sem) = take(5)
     (dk_send, dk_recv, dm_send, dm_recv, mg_send, mg_recv, sm_send, sm_recv) = take(8)
@@ -130,32 +143,47 @@
 
     other_seq = (1 - seq, blk, head)
     other_head = (seq, blk, 1 - head)
-    next_blk = across(0)
-    member = 2 * seq + mine[0]
-    peers = (other_seq, next_blk, (1 - seq, next_blk[1], head))
-    peer_slots = (
-        2 * (1 - seq) + mine[0],
-        2 * seq + 1 - mine[0],
-        2 * (1 - seq) + 1 - mine[0],
-    )
+
+    def hop(mask):
+        target = blk
+        for bit in range(bits):
+            if mask >> bit & 1:
+                target = target + (1 - 2 * mine[bit]) * (1 << bit)
+        return (seq, target, head)
+
+    def member(bit):
+        return 2 * seq + mine[bit]
+
+    def peers(bit):
+        far = across(bit)
+        return (other_seq, far, (1 - seq, far[1], head))
+
+    far_masks = [step << 1 for step in range(1, 1 << (bits - 1))]
+    own = {name: member(shared_bit(name)) for name in NAMES}
 
     loads = {
         name: pltpu.make_async_copy(weights_in[name], weight[name], load_sem.at[slot])
         for slot, name in enumerate(NAMES)
     }
     memory_load = pltpu.make_async_copy(memory_in, memory, load_sem.at[len(NAMES)])
-    for name in ("sk", "sv", "sq"):
+    for name in ("sk", "sv"):
         copies.start(("load", name), loads[name])
-    copies.start(("load", "memory"), memory_load)
-    for name in NAMES[3:]:
-        copies.start(("load", name), loads[name])
+
+    def more_loads():
+        copies.start(("load", "sq"), loads["sq"])
+        copies.start(("load", "memory"), memory_load)
+        for name in NAMES[3:]:
+            copies.start(("load", name), loads[name])
 
     def checkpoint(place):
         if stop == place:
             raise Stop
 
     barrier = pltpu.get_barrier_semaphore()
-    friends = [*peers, other_head, *(across(bit) for bit in range(1, bits))]
+    bits_used = sorted({shared_bit(name) for name in LEFTS})
+    friends = [other_seq, other_head, across(0)]
+    friends += [peers(bit)[2] for bit in bits_used]
+    friends += [hop(mask) for mask in far_masks]
     for friend in friends:
         pl.semaphore_signal(barrier, inc=1, device_id=friend, device_id_type=MESH)
 
@@ -177,7 +205,8 @@
 
     def norm_into(values, gain, plain, left):
         plain[...] = (values * inverse_norm(values) * gain[...]).astype(BF)
-        share_left(left, plain[...])
+        if left is not None:
+            share_left(left, plain[...])
 
     def norm_back(values, gain, normed_grad, slot):
         scale = inverse_norm(values)
@@ -185,15 +214,15 @@
         unit_grad = normed_grad * gain[...]
         line = jnp.sum(normed_grad * unit, axis=0, keepdims=True)
         for tile in range(width // 128):
-            small[0, slot * (width // 128) + tile : slot * (width // 128) + tile + 1, :] = line[
+            small[member(0), slot * (width // 128) + tile : slot * (width // 128) + tile + 1, :] = line[
                 :, tile * 128 : (tile + 1) * 128
             ]
         return scale * (unit_grad - unit * jnp.mean(unit_grad * unit, axis=-1, keepdims=True))
 
     def hx(which, tile):
         return pltpu.make_async_remote_copy(
-            src_ref=pushed.at[which, tile],
-            dst_ref=landed.at[which, tile],
+            src_ref=pushed.at[which % 4, tile],
+            dst_ref=landed.at[which % 4, tile],
             send_sem=hx_send.at[which, tile],
             recv_sem=hx_recv.at[which, tile],
             device_id=other_head,
@@ -201,12 +230,14 @@
         )
 
     def push(which, tile, value):
-        pushed[which, tile] = value.astype(BF)
+        if which >= 4:
+            copies.leave(("hx", which - 4, tile))
+        pushed[which % 4, tile] = value.astype(BF)
         copies.start(("hx", which, tile), hx(which, tile))
 
     def summed(which, tile):
         copies.receive(("hx", which, tile))
-        return pushed[which, tile].astype(F32) + landed[which, tile].astype(F32)
+        return pushed[which % 4, tile].astype(F32) + landed[which % 4, tile].astype(F32)
 
     tiles = width // TILE
 
@@ -222,19 +253,25 @@
         return left_all[name].at[(slice(None),) * bits + (lanes_of(slot, rows),)]
 
     def share_left(name, value):
-        own = left_own[name]
+        mine_left = left_own[name]
+        bit = shared_bit(name)
         turned = value.T
-        own[...] = turned.reshape(own.shape)
-        here = (seq, *(slice(None),) * (bits - 1), mine[0])
-        left_place(name, member)[...] = own[here]
+        mine_left[...] = turned.reshape(mine_left.shape)
+
+        def rows_of(half, low):
+            index = [half]
+            index += [low if place == bit else slice(None) for place in reversed(range(bits))]
+            return tuple(index)
+
+        left_place(name, member(bit))[...] = mine_left[rows_of(seq, mine[bit])]
         slot = LEFTS.index(name)
-        for way, peer in enumerate(peers):
-            there = (peer[0], *(slice(None),) * (bits - 1), mine[0] if way == 0 else 1 - mine[0])
+        for way, peer in enumerate(peers(bit)):
+            there = rows_of(peer[0], mine[bit] if way == 0 else 1 - mine[bit])
             copies.start(
                 ("left", name, way),
                 pltpu.make_async_remote_copy(
-                    src_ref=own.at[there],
-                    dst_ref=left_place(name, member),
+                    src_ref=mine_left.at[there],
+                    dst_ref=left_place(name, member(bit)),
                     send_sem=lf_send.at[slot, way],
                     recv_sem=lf_recv.at[slot, way],
                     device_id=peer,
@@ -244,13 +281,14 @@
 
     def right_copy(name, way):
         slot = NAMES.index(name)
-        place = right_all[name].at[member if way < 2 else peer_slots[1]]
+        bit = shared_bit(name)
+        place = right_all[name].at[own[name] if way < 2 else 2 * seq + 1 - mine[bit]]
         return pltpu.make_async_remote_copy(
             src_ref=place,
             dst_ref=place,
             send_sem=rt_send.at[slot, way],
             recv_sem=rt_recv.at[slot, way],
-            device_id=next_blk if way == 1 else other_seq,
+            device_id=across(bit) if way == 1 else other_seq,
             device_id_type=MESH,
         )
 
@@ -286,11 +324,14 @@
                     right_all[name][:, :, lanes].reshape(count * depth, step),
                 )
             out[..., lanes] = total.astype(BF).reshape(*out.shape[:-1], step)
-        copies.start(("rs", name, 0), rs_copy(name, 0))
-
-    def bit_view(order, stage, keep, low_bit=0):
+        for stage in range(len(far_masks) if name in DIRECT else 1):
+            copies.start(("rs", name, stage), rs_copy(name, stage))
+
+    def bit_view(order, stage, keep):
         index = []
-        for bit in reversed(range(low_bit, bits)):
+        for bit in reversed(range(bits)):
+            if bit not in order:
+                continue
             place = order.index(bit)
             if place < stage:
                 index.append(mine[bit])
@@ -300,19 +341,29 @@
                 index.append(slice(None))
         return tuple(index)
 
-    rs_order = list(range(1, bits))
+    def rs_order(name):
+        return [bit for bit in range(bits) if bit != shared_bit(name)]
 
     def rs_view(name, stage, keep):
-        return partial[name].at[bit_view(rs_order, stage, keep, 1)]
+        return partial[name].at[bit_view(rs_order(name), stage, keep)]
 
     def rs_copy(name, stage):
         slot = NAMES.index(name)
+        if name in DIRECT:
+            mask = far_masks[stage]
+            place = tuple(
+                1 - mine[bit] if mask >> bit & 1 else mine[bit] for bit in reversed(range(1, bits))
+            )
+            source, target, to = partial[name].at[place], landing[name][0].at[stage], hop(mask)
+        else:
+            source, target = rs_view(name, stage, False), landing[name][stage]
+            to = across(rs_order(name)[stage])
         return pltpu.make_async_remote_copy(
-            src_ref=rs_view(name, stage, False),
-            dst_ref=landing[name][stage],
+            src_ref=source,
+            dst_ref=target,
             send_sem=rs_send.at[slot, stage],
             recv_sem=rs_recv.at[slot, stage],
-            device_id=across(rs_order[stage]),
+            device_id=to,
             device_id_type=MESH,
         )
 
@@ -321,6 +372,14 @@
         for flat in range(int(np.prod(lead))):
             index = tuple(int(value) for value in np.unravel_index(flat, lead)) if lead else (Ellipsis,)
             kept[index] = (kept[index].astype(F32) + got[index].astype(F32)).astype(BF)
+
+    def rs_finish(name):
+        total = partial[name][tuple(mine[bit] for bit in reversed(range(1, bits)))].astype(F32)
+        for stage in range(len(far_masks)):
+            copies.receive(("rs", name, stage))
+            total = total + landing[name][0][stage].astype(F32)
+        staged[name][...] = total
+        give(name)
 
     def rs_step(name, stage):
         copies.receive(("rs", name, stage))
@@ -366,26 +425,65 @@
 
     dmem_args = ("dmem", dmem, dmem_land, dm_send, dm_recv)
 
-    def ag_copy(which, step):
-        bit = bits - 1 - step
-        index = (slice(None),) + tuple(
-            slice(None) if place > bit else mine[place] for place in reversed(range(bits))
-        )
+    level = blk // 2
+    top = half_count - 1
+
+    def ag_copy(which, step, up):
+        place, digits = jnp.maximum(level - step, 0), []
+        for _ in range(bits - 1):
+            digits.append(lax.rem(place, 2))
+            place = place // 2
         buffer = (kbuf, vbuf)[which]
+        block = buffer.at[(slice(None), *reversed(digits), mine[0])]
+        above = (seq, 2 * jnp.minimum(level + 1, top) + mine[0], head)
         return pltpu.make_async_remote_copy(
-            src_ref=buffer.at[index],
-            dst_ref=buffer.at[index],
-            send_sem=ag_send.at[which, step],
-            recv_sem=ag_recv.at[which, step],
-            device_id=across(bit),
+            src_ref=block,
+            dst_ref=block,
+            send_sem=ag_send.at[which, step, 0 if up else 1],
+            recv_sem=ag_recv.at[which, step, 0 if up else 1],
+            device_id=above if up else across(0),
             device_id_type=MESH,
         )
 
-    def ag_next(step):
-        for which in range(2):
-            copies.receive(("ag", which, step))
-            if step + 1 < bits:
-                copies.start(("ag", which, step + 1), ag_copy(which, step + 1))
+    def ag_step(which, step):
+        @pl.when(level >= step)
+        def _():
+            if step > 0:
+                ag_copy(which, step - 1, True).wait_recv()
+
+            @pl.when(level < top)
+            def _():
+                ag_copy(which, step, True).start()
+
+            ag_copy(which, step, False).start()
+
+        def wait():
+            @pl.when(level >= step)
+            def _():
+                @pl.when(level < top)
+                def _():
+                    ag_copy(which, step, True).wait_send()
+
+                ag_copy(which, step, False).wait_send()
+
+        copies.last.append(wait)
+
+    def ag_end(which):
+        for step in range(half_count):
+
+            @pl.when(level >= step)
+            def _(step=step):
+                ag_copy(which, step, False).wait_recv()
+
+    def clear_later():
+        for place in range(1, half_count):
+            digits = tuple(place >> bit & 1 for bit in reversed(range(bits - 1)))
+
+            @pl.when(place > level)
+            def _(digits=digits):
+                for buffer in (kbuf, vbuf):
+                    for pair in range(pairs):
+                        buffer[(pair, *digits)] = jnp.zeros((2, rows, 128), BF)
 
     def half_index(chunk):
         index, left = [], chunk
@@ -422,6 +520,7 @@
         return jnp.sum(laid * attended[group], axis=0, keepdims=True)
 
     length = lengths[0]
+    reach = jnp.minimum(length, (blk + 1) * rows)
     key_row = lax.broadcasted_iota(jnp.int32, (rows, 2 * rows), 0)
 
     def kind_of(block):
@@ -433,41 +532,48 @@
         for inner_block in range(2):
             block = 2 * chunk + inner_block
             part = raw[inner_block * rows : (inner_block + 1) * rows, :]
-            part = part + tab[kind_of(block), group]
-            parts.append(jnp.where(key_row + block * rows < length, part, MASKED))
+            part = part + tab[jnp.minimum(kind_of(block), 2), group]
+            parts.append(jnp.where(key_row + block * rows < reach, part, MASKED))
         return jnp.concatenate(parts, axis=0)
 
     checkpoint(0)
     pl.semaphore_wait(barrier, len(friends))
     x = hidden[...].astype(F32)
-    norm_into(x, ln_self, ns, "ns")
+    norm_into(x, ln_self, ns, None)
     copies.receive(("load", "sk"))
+    more_loads()
     keys = dot(ns[...], whole("sk")).astype(BF)
     for pair in range(pairs):
         kbuf[(pair, *reversed(mine))] = keys[:, pair * 128 : (pair + 1) * 128]
-    copies.start(("ag", 0, 0), ag_copy(0, 0))
+    ag_step(0, 0)
     copies.receive(("load", "sv"))
     values = dot(ns[...], whole("sv")).astype(BF)
     for pair in range(pairs):
         vbuf[(pair, *reversed(mine))] = values[:, pair * 128 : (pair + 1) * 128]
-    copies.start(("ag", 1, 0), ag_copy(1, 0))
+    ag_step(1, 0)
+    clear_later()
     copies.receive(("load", "sq"))
     split_heads(dot(ns[...], whole("sq")).astype(BF), qs)
-    ag_next(0)
-
+    for which in range(2):
+        ag_step(which, 1)
     copies.receive(("load", "memory"))
     share = mem_rows // blk_count
-    share_left("mem", memory[pl.ds(pl.multiple_of(blk * share, share), share), :])
-    for source, plain, turned in (("ck", mk, mkT), ("cv", mv, mvT)):
+
+    def project_memory(source, plain, turned):
         copies.receive(("load", source))
         result = dot(memory[...], whole(source)).astype(BF)
         for pair in range(pairs):
             plain[pair] = result[:, pair * 128 : (pair + 1) * 128]
             turned[pair * 128 : (pair + 1) * 128, :] = result[:, pair * 128 : (pair + 1) * 128].T
-    if bits > 1:
-        ag_next(1)
-
-    checkpoint(2)
+
+    project_memory("ck", mk, mkT)
+    for which in range(2):
+        ag_step(which, 2)
+    project_memory("cv", mv, mvT)
+    for step in range(3, half_count):
+        for which in range(2):
+            ag_step(which, step)
+
     starts = bucket_starts()
     distance = lane - lax.broadcasted_iota(jnp.int32, (rows, 128), 0)
 
@@ -486,12 +592,13 @@
         tab[0, group, :, lanes] = jnp.full((rows, rows), rel_bias[head_slot, BUCKETS - 1], F32)
         tab[1, group, :, lanes] = bias_of(1, head_slot)
         tab[2, group, :, lanes] = bias_of(2, head_slot)
-        tab[3, group, :, lanes] = jnp.full((rows, rows), MASKED, F32)
         return carry
 
     lax.fori_loop(0, 2 * groups, bias_tables, 0)
-    for step in range(2, bits):
-        ag_next(step)
+    share_left("ns", ns[...])
+    share_left("mem", memory[pl.ds(pl.multiple_of(blk * share, share), share), :])
+    for which in range(2):
+        ag_end(which)
 
     def turn_chunk(chunk):
         for pair in range(pairs):
@@ -537,7 +644,7 @@
         precise = acc / total
         att_self[group] = precise
         lse[group] = tops + jnp.log(total)
-        right_all["so"][member, :, group * 128 : (group + 1) * 128] = join_heads(precise).astype(BF)
+        right_all["so"][own["so"], :, group * 128 : (group + 1) * 128] = join_heads(precise).astype(BF)
 
     checkpoint(4)
     for group in range(groups):
@@ -546,7 +653,7 @@
     checkpoint(5)
     copies.receive(("load", "so"))
     for tile in range(tiles):
-        push(0, tile, dot_nt(right_all["so"][member], row_tile("so", tile)))
+        push(0, tile, dot_nt(right_all["so"][own["so"]], row_tile("so", tile)))
     valid = lax.broadcasted_iota(jnp.int32, (rows, 1), 0) + blk * rows < length
     bg[...] = jnp.where(valid, out_grad[...].astype(F32), 0.0).astype(BF)
     share_left("gf", bg[...])
@@ -563,11 +670,11 @@
         probs[group] = part
         acc = dot(mvT[group * HEAD_DIM : (group + 1) * HEAD_DIM, :], part.astype(BF))
         att_cross[group] = acc
-        right_all["co"][member, :, group * 128 : (group + 1) * 128] = join_heads(acc).astype(BF)
+        right_all["co"][own["co"], :, group * 128 : (group + 1) * 128] = join_heads(acc).astype(BF)
     checkpoint(7)
     copies.receive(("load", "co"))
     for tile in range(tiles):
-        push(1, tile, dot_nt(right_all["co"][member], row_tile("co", tile)))
+        push(1, tile, dot_nt(right_all["co"][own["co"]], row_tile("co", tile)))
     share_right("so")
     share_right("co")
     after_cross[...] = after_self[...] + summed_all(1)
@@ -587,20 +694,20 @@
             GELU_A * (1.0 + 3.0 * GELU_B * gate * gate)
         )
         bell = gate * opened
-        right_all["fd"][member, :, lanes] = (bell * up).astype(BF)
-        right_all["fg"][member, :, lanes] = (back * up * slope).astype(BF)
-        right_all["fu"][member, :, lanes] = (back * bell).astype(BF)
+        right_all["fd"][own["fd"], :, lanes] = (bell * up).astype(BF)
+        right_all["fg"][own["fg"], :, lanes] = (back * up * slope).astype(BF)
+        right_all["fu"][own["fu"], :, lanes] = (back * bell).astype(BF)
     for name in ("fd", "fg", "fu"):
         share_right(name)
     for tile in range(tiles):
         push(
             2,
             tile,
-            dot_nt(right_all["fg"][member], row_tile("fg", tile))
-            + dot_nt(right_all["fu"][member], row_tile("fu", tile)),
+            dot_nt(right_all["fg"][own["fg"]], row_tile("fg", tile))
+            + dot_nt(right_all["fu"][own["fu"]], row_tile("fu", tile)),
         )
     for tile in range(tiles):
-        push(3, tile, dot_nt(right_all["fd"][member], row_tile("fd", tile)))
+        push(3, tile, dot_nt(right_all["fd"][own["fd"]], row_tile("fd", tile)))
 
     pass_right("so")
     pass_right("co")
@@ -622,7 +729,7 @@
             prob_grad = dot_nt(mv[pair], ags[group])
             score_grad = (prob * (prob_grad - head_deltas(back, att_cross, group))).astype(BF)
             turned = dot(mkT[group * HEAD_DIM : (group + 1) * HEAD_DIM, :], score_grad)
-            right_all["cq"][member, :, group * 128 : (group + 1) * 128] = join_heads(turned).astype(BF)
+            right_all["cq"][own["cq"], :, group * 128 : (group + 1) * 128] = join_heads(turned).astype(BF)
             key_new = dot(score_grad, cqs[group])
             value_new = dot(prob.astype(BF), ags[group])
             key_part = key_new if key_part is None else key_part + key_new
@@ -634,12 +741,11 @@
         )
     checkpoint(11)
     for tile in range(tiles):
-        push(4, tile, dot_nt(right_all["cq"][member], row_tile("cq", tile)))
+        push(4, tile, dot_nt(right_all["cq"][own["cq"]], row_tile("cq", tile)))
     part_start(*dmem_args, 0)
-    share_right("cq")
+    pass_right("fg")
+    make_partial("fg")
     make_partial("fd")
-    pass_right("fg")
-    make_partial("co")
     for tile in range(tiles):
         lanes = slice(tile * TILE, (tile + 1) * TILE)
         staged["layer_out"][:, lanes] = (after_cross[:, lanes] + summed(3, tile)).astype(BF)
@@ -649,12 +755,47 @@
     bg[...] = cot[...].astype(BF)
     share_left("gs", bg[...])
 
+    def add_bias_gradient():
+        row = lax.broadcasted_iota(jnp.int32, (rows, rows), 0)
+        column = lax.broadcasted_iota(jnp.int32, (rows, rows), 1)
+        slot_row = lax.broadcasted_iota(jnp.int32, (2 * groups, rows), 0)
+        slot_lane = lax.broadcasted_iota(jnp.int32, (2 * groups, rows), 1)
+        bucket = jnp.minimum(slot_lane, BUCKETS // 2)
+        for start in bucket_starts()[BUCKETS // 2 :]:
+            bucket = bucket + (slot_lane >= start).astype(jnp.int32)
+        lines = jnp.zeros((2 * groups, rows), F32)
+        last = jnp.zeros((2 * groups, rows), F32)
+        for group in range(groups):
+            for half in range(2):
+                lanes = slice(half * rows, (half + 1) * rows)
+                here = near[2, group, :, lanes].astype(F32)
+                before = near[1, group, :, lanes].astype(F32)
+                tile = here + jnp.where(column < row, before, 0.0)
+                for bit in range(rows.bit_length() - 1):
+                    moved = pltpu.roll(tile, rows - (1 << bit), 1)
+                    tile = jnp.where(lax.rem(row // (1 << bit), 2) == 1, moved, tile)
+                line = jnp.sum(tile, axis=0, keepdims=True)
+                beyond = jnp.sum(jnp.where(column < row, 0.0, before), axis=0, keepdims=True)
+                beyond = beyond + far_sum[group, :, lanes]
+                slot = 2 * group + half
+                lines = jnp.where(slot_row == slot, line, lines)
+                last = jnp.where(slot_row == slot, beyond, last)
+        wide = lax.broadcasted_iota(jnp.int32, (2 * groups, rows), 1)
+        grid = jnp.zeros((2 * groups, rows), F32)
+        for place in range(BUCKETS):
+            total = jnp.sum(jnp.where(bucket == place, lines, 0.0), axis=1, keepdims=True)
+            if place == BUCKETS - 1:
+                total = total + jnp.sum(last, axis=1, keepdims=True)
+            grid = jnp.where(wide == place, total, grid)
+        first_bias = 3 * (width // 128)
+        small[member(0), first_bias : first_bias + 2 * groups, :] = grid
+
     checkpoint(12)
     back = dot(bg[...], whole("so")).astype(BF)
     split_heads(back, ags)
-    part_step(*dmem_args, 0)
-    make_partial("fg")
     pass_right("fu")
+    make_partial("fu")
+    rs_step("fg", 0)
     near[1] = jnp.zeros(near.shape[1:], BF)
     for pair in range(pairs):
         members = (2 * pair, 2 * pair + 1)
@@ -698,45 +839,45 @@
         else:
             state = lax.fori_loop(0, half_count, visit, state)
         part_start(*dkv_args(pair), 0)
+        if pair == 0:
+            part_step(*dmem_args, 0)
+            rs_step("fu", 0)
         for slot, group in enumerate(members):
-            right_all["sq"][member, :, group * 128 : (group + 1) * 128] = join_heads(
+            right_all["sq"][own["sq"], :, group * 128 : (group + 1) * 128] = join_heads(
                 state[2 * slot]
             ).astype(BF)
-            bias_sum[BUCKETS : BUCKETS + 1, group * 2 * rows : (group + 1) * 2 * rows] = state[
-                2 * slot + 1
-            ]
+            far_sum[group] = state[2 * slot + 1]
     checkpoint(13)
+    share_right("cq")
+    make_partial("co")
     share_right("sq")
-    make_partial("fu")
     part_step(*dkv_args(0), 0)
-    part_step(*dmem_args, 1)
-    pass_right("cq")
     rs_step("fd", 0)
     make_partial("so")
+    query_part = [
+        dot_nt(right_all["sq"][own["sq"]], row_tile("sq", tile)) for tile in range(tiles)
+    ]
+    for step in range(1, bits - 1):
+        rs_step("fg", step)
     part_step(*dkv_args(1), 0)
-    make_partial("cq")
+    part_step(*dmem_args, 1)
+    for step in range(1, bits - 1):
+        part_step(*dkv_args(0), step)
+        part_step(*dkv_args(1), step)
     mem_sum = None
     for step in range(2, bits):
         mem_sum = part_step(*dmem_args, step)
     mem_sum = mem_sum.astype(BF)
-    right_all["ck"][member] = mem_sum[:, : pairs * 128]
-    right_all["cv"][member] = mem_sum[:, pairs * 128 :]
+    right_all["ck"][own["ck"]] = mem_sum[:, : pairs * 128]
+    right_all["cv"][own["cv"]] = mem_sum[:, pairs * 128 :]
     share_right("ck")
     share_right("cv")
-    query_part = [
-        dot_nt(right_all["sq"][member], row_tile("sq", tile)) for tile in range(tiles)
-    ]
-    for step in range(1, bits - 1):
-        part_step(*dkv_args(0), step)
-    rs_step("co", 0)
-    rs_step("fg", 0)
-    for step in range(1, bits - 1):
-        part_step(*dkv_args(1), step)
-    pass_right("sq")
+    pass_right("cq")
+    make_partial("cq")
     sums = [part_step(*dkv_args(pair), bits - 1).astype(BF) for pair in range(pairs)]
     for pair, value in enumerate(sums):
-        right_all["sk"][member, :, pair * 128 : (pair + 1) * 128] = value[:, :128]
-        right_all["sv"][member, :, pair * 128 : (pair + 1) * 128] = value[:, 128:]
+        right_all["sk"][own["sk"], :, pair * 128 : (pair + 1) * 128] = value[:, :128]
+        right_all["sv"][own["sv"], :, pair * 128 : (pair + 1) * 128] = value[:, 128:]
     share_right("sk")
     share_right("sv")
     for tile in range(tiles):
@@ -744,16 +885,22 @@
             5,
             tile,
             query_part[tile]
-            + dot_nt(right_all["sk"][member], row_tile("sk", tile))
-            + dot_nt(right_all["sv"][member], row_tile("sv", tile)),
+            + dot_nt(right_all["sk"][own["sk"]], row_tile("sk", tile))
+            + dot_nt(right_all["sv"][own["sv"]], row_tile("sv", tile)),
         )
-    pass_right("ck")
-    pass_right("cv")
+    pass_right("sq")
     make_partial("sq")
-    rs_step("fu", 0)
+    rs_step("co", 0)
+    rs_step("so", 0)
+    for name in ("ck", "cv"):
+        pass_right(name)
+    for step in range(1, bits - 1):
+        rs_step("fu", step)
+        rs_step("fd", step)
+    add_bias_gradient()
 
     checkpoint(14)
-    mkg, mvg = right_all["ck"][member], right_all["cv"][member]
+    mkg, mvg = right_all["ck"][own["ck"]], right_all["cv"][own["cv"]]
     mem_part = dot_nt(mkg, whole("ck")) + dot_nt(mvg, whole("cv"))
     half = share // 2
     mem_push[0] = mem_part[:half, :].astype(BF)
@@ -767,85 +914,58 @@
         device_id_type=MESH,
     )
     copies.start(("mem",), mem_copy)
-    pass_right("sk")
-    pass_right("sv")
-    rs_step("so", 0)
+    for name in ("sk", "sv"):
+        pass_right(name)
+    for name in ("ck", "cv", "sk", "sv"):
+        make_partial(name)
     rs_step("cq", 0)
-
-    checkpoint(15)
-    def bucket_line(group, lower, upper):
-        line = jnp.zeros((1, 2 * rows), F32)
-        wide = jnp.concatenate([distance, distance], axis=1)
-        for kind in (1, 2):
-            shifted = wide + (rows if kind == 1 else 0)
-            here = shifted >= lower
-            if upper is not None:
-                here = jnp.logical_and(here, shifted < upper)
-            piece = near[kind, group].astype(F32)
-            line = line + jnp.sum(jnp.where(here, piece, 0.0), axis=0, keepdims=True)
-        return line
-
-    bounds = [0, *starts, None]
-    for group in range(groups):
-        lanes = slice(group * 2 * rows, (group + 1) * 2 * rows)
-        for bucket in range(BUCKETS):
-            line = bucket_line(group, bounds[bucket], bounds[bucket + 1])
-            if bucket == BUCKETS - 1:
-                line = line + bias_sum[BUCKETS : BUCKETS + 1, lanes]
-            bias_sum[bucket : bucket + 1, lanes] = line
-    bias_lane = lax.broadcasted_iota(jnp.int32, (BUCKETS, 128), 1)
-    bias_grad = jnp.zeros((BUCKETS, 128), F32)
-    for head_slot in range(2 * groups):
-        column = jnp.sum(
-            bias_sum[:BUCKETS, head_slot * rows : (head_slot + 1) * rows], axis=1, keepdims=True
-        )
-        bias_grad = jnp.where(bias_lane == head_slot, column, bias_grad)
-    first_bias = 3 * (width // 128)
-    small[0, first_bias : first_bias + BUCKETS, :] = bias_grad
 
     checkpoint(16)
     normed_grad = summed_all(5)
     staged["hidden_grad"][...] = cot[...] + norm_back(hidden[...].astype(F32), ln_self, normed_grad, 0)
     give("hidden_grad")
 
-    def small_copy(stage):
+    def small_near(way):
         return pltpu.make_async_remote_copy(
-            src_ref=small.at[stage],
-            dst_ref=small_land.at[stage],
-            send_sem=sm_send.at[stage],
-            recv_sem=sm_recv.at[stage],
-            device_id=other_seq if stage == 0 else across(stage - 1),
+            src_ref=small.at[member(0)],
+            dst_ref=small.at[member(0)],
+            send_sem=sm_send.at[way],
+            recv_sem=sm_recv.at[way],
+            device_id=peers(0)[way],
             device_id_type=MESH,
         )
 
-    def small_step(stage):
-        copies.receive(("small", stage))
-        total = small[stage] + small_land[stage]
-        if stage < stages - 1:
-            small[stage + 1] = total
-            copies.start(("small", stage + 1), small_copy(stage + 1))
-        else:
-            small_out[...] = total
-
-    copies.start(("small", 0), small_copy(0))
-    for name in ("ck", "cv", "sk", "sv"):
-        make_partial(name)
-    small_step(0)
-    for name in ("fd", "co", "fg", "fu", "so", "cq"):
-        for step in range(1, bits - 1):
+    def small_across(way):
+        return pltpu.make_async_remote_copy(
+            src_ref=small_far.at[blk // 2],
+            dst_ref=small_far.at[blk // 2],
+            send_sem=sm_send.at[3 + way],
+            recv_sem=sm_recv.at[3 + way],
+            device_id=hop(far_masks[way]),
+            device_id_type=MESH,
+        )
+
+    for way in (1, 2, 0):
+        copies.start(("small", way), small_near(way))
+    for step in range(1, bits - 1):
+        for name in ("co", "so", "cq"):
             rs_step(name, step)
     rs_step("sq", 0)
-    small_step(1)
+    for way in range(3):
+        copies.receive(("small", way))
+    small_far[blk // 2] = small[0] + small[1] + small[2] + small[3]
+    for way in range(len(far_masks)):
+        copies.start(("small", 3 + way), small_across(way))
+    for name in ("ck", "cv", "sk", "sv"):
+        rs_finish(name)
     for step in range(1, bits - 1):
         rs_step("sq", step)
-    for name in ("ck", "cv", "sk", "sv"):
-        rs_step(name, 0)
-    small_step(2)
-    for step in range(1, bits - 1):
-        for name in ("ck", "cv", "sk", "sv"):
-            rs_step(name, step)
-    for stage in range(3, stages):
-        small_step(stage)
+    for way in range(len(far_masks)):
+        copies.receive(("small", 3 + way))
+    total = small_far[0]
+    for slot in range(1, blk_count // 2):
+        total = total + small_far[slot]
+    small_out[...] = total
     copies.receive(("mem",))
     staged["memory_grad"][...] = mem_push[head].astype(F32) + mem_land[...].astype(F32)
     give("memory_grad")
@@ -872,7 +992,7 @@
             def _(target=target, line=line, part=part):
                 target[...] = line[0, part * share : (part + 1) * share]
 
-    bias_out[...] = small[3 * lines :, :].T[: bias_out.shape[0], :]
+    bias_out[...] = small[3 * lines :, : bias_out.shape[1]]
     for move in moves:
         move.wait()
 
@@ -906,11 +1026,12 @@
         raise ValueError("unexpected sizes")
     pairs = groups // 2
     half_count = blk_count // 2
-    stored = 1 if half_count > 4 else half_count
+    long = half_count > 4
+    stored = 1 if long else half_count
     piece = width // (2 * blk_count)
     widths = {name: weights[name].shape[1] for name in NAMES}
     share = mem_rows // blk_count
-    small_rows = 3 * (width // 128) + BUCKETS
+    small_rows = 3 * (width // 128) + heads
 
     vm, sem = pltpu.VMEM, pltpu.SemaphoreType.DMA
     high = (2,) * (bits - 1)
@@ -926,6 +1047,9 @@
     scratch += [vm((4, depth[name], widths[name]), BF) for name in NAMES]
     scratch += [vm((*high, piece, widths[name]), BF) for name in NAMES]
     for name in NAMES:
+        if name in DIRECT:
+            scratch.append(vm((half_count - 1, piece, widths[name]), BF))
+            continue
         for stage in range(bits - 1):
             scratch.append(vm((2,) * (bits - 2 - stage) + (piece, widths[name]), BF))
     by_bit = (2,) * bits
@@ -937,9 +1061,9 @@
         vm((pairs, *by_bit, rows, 128), BF),
         vm((stored, groups * HEAD_DIM, 2 * rows), BF),
         vm((stored, groups * HEAD_DIM, 2 * rows), BF),
-        vm((4, groups, rows, 2 * rows), F32),
+        vm((3, groups, rows, 2 * rows), F32),
         vm((3, groups, rows, 2 * rows), BF),
-        vm((2, stored, 2 * rows, 2 * rows), F32),
+        vm((2, stored, 8 if long else 2 * rows, 2 * rows), F32),
         vm((groups, 2 * rows, 128), BF),
         vm((groups, 2 * rows, 128), BF),
         vm((groups, 2 * rows, 128), BF),
@@ -951,8 +1075,8 @@
         vm((pairs, mem_rows, 128), BF),
         vm((groups * HEAD_DIM, mem_rows), BF),
         vm((groups * HEAD_DIM, mem_rows), BF),
-        vm((6, width // TILE, rows, TILE), BF),
-        vm((6, width // TILE, rows, TILE), BF),
+        vm((4, width // TILE, rows, TILE), BF),
+        vm((4, width // TILE, rows, TILE), BF),
         vm((rows, width), F32),
         vm((rows, width), F32),
         vm((rows, width), F32),
@@ -970,16 +1094,16 @@
     scratch += [
         vm((2, share // 2, width), BF),
         vm((share // 2, width), BF),
-        vm((stages, small_rows, 128), F32),
-        vm((stages, small_rows, 128), F32),
-        vm((BUCKETS + 8, heads * rows), F32),
+        vm((4, small_rows, 128), F32),
+        vm((half_count, small_rows, 128), F32),
+        vm((groups, 1, 2 * rows), F32),
         sem((len(NAMES) + 1,)),
         sem((6, width // TILE)),
         sem((6, width // TILE)),
-        sem((2, bits)),
-        sem((2, bits)),
-        sem((len(NAMES), bits - 1)),
-        sem((len(NAMES), bits - 1)),
+        sem((2, half_count, 2)),
+        sem((2, half_count, 2)),
+        sem((len(NAMES), half_count)),
+        sem((len(NAMES), half_count)),
         sem((len(LEFTS), 3)),
         sem((len(LEFTS), 3)),
         sem((len(NAMES), 3)),
@@ -991,8 +1115,8 @@
         sem((bits,)),
         sem,
         sem,
-        sem((stages,)),
-        sem((stages,)),
+        sem((half_count + 2,)),
+        sem((half_count + 2,)),
     ]
     in_vmem = pl.BlockSpec(memory_space=pltpu.VMEM)
     in_smem = pl.BlockSpec(memory_space=pltpu.SMEM)

time: 164 us -> 147 us (0.90)
  Pallas kernels: 163 us -> 145 us
    pallas_call x1, Pallas kernels: 159 us -> 141 us  [run_layer(): pl.pallas_call(functools.partial(layer_kernel, (bits, rows, width, groups...]
where the time goes in v4:
time: 147 us
  Pallas kernels  145 us (99%)
  between operations  1.48 us (1%)
    pallas_call x1, Pallas kernels, run_layer(): pl.pallas_call(functools.partial(layer_kernel, (bits, rows, width, groups...  141 us
    pallas_call x1, Pallas kernels, finish(): pl.pallas_call(functools.partial(finish_kernel, count, width // 128, widt...  4.03 us

profile of v4, /device:TPU:0, one launch (start us, length us, event | category | flops | bytes accessed | tf_op | source)
XLA Modules:
  0.0 147.0 jit_solution(7716161379384366829)
XLA Ops:
  1.3 141.4 %layer.1 = (bf16[128,1024]{1,0:T(8,128)(2,1)}, f32[128,1024]{1,0:T(8,128)}, f32[32,1024]{1,0:T(8,128)}, f32[64,256]{1,0:T(8,128)}, f32[64,256]{1,0:T(8,128)}, /*...) custom-call(s32[1]{0:T(128)S(6)} %copy.37.refs_0_, ...), custom_call_target="tpu_custom_call" | custom-call | tf_op jit(solution)/shard_map/layer/pallas_call | solution.py:1131
  142.8 4.0 %finish.1 = (bf16[128,1024]{1,0:T(8,128)(2,1)}, f32[128,1024]{1,0:T(8,128)}, f32[32,1024]{1,0:T(8,128)}, f32[64,256]{1,0:T(8,128)}, f32[64,256]{1,0:T(8,128)}, /...) custom-call(bf16[128,1024]{1,0:T(8,128)(2,1)} %get-tuple-element.51., ...), custom_call_target="tpu_custom_call" | custom-call | tf_op jit(solution)/shard_map/finish/pallas_call | solution.py:1004

commit v5 on v4

--- a/solution.py
+++ b/solution.py
@@ -279,34 +279,41 @@
                 ),
             )
 
-    def right_copy(name, way):
+    def right_copy(name, way, part=0, lanes=None):
         slot = NAMES.index(name)
         bit = shared_bit(name)
         place = right_all[name].at[own[name] if way < 2 else 2 * seq + 1 - mine[bit]]
+        if lanes is not None:
+            place = place.at[:, lanes]
         return pltpu.make_async_remote_copy(
             src_ref=place,
             dst_ref=place,
-            send_sem=rt_send.at[slot, way],
-            recv_sem=rt_recv.at[slot, way],
+            send_sem=rt_send.at[slot, way, part],
+            recv_sem=rt_recv.at[slot, way, part],
             device_id=across(bit) if way == 1 else other_seq,
             device_id_type=MESH,
         )
 
-    def share_right(name):
+    def share_right(name, part=0, lanes=None):
         for way in (1, 0):
-            copies.start(("right", name, way), right_copy(name, way))
+            copies.start(("right", name, way, part), right_copy(name, way, part, lanes))
+
+    def parts_of(name, way):
+        return [key for key in copies.started if key[:3] == ("right", name, way)]
 
     def pass_right(name):
-        copies.receive(("right", name, 1))
-        copies.start(("right", name, 2), right_copy(name, 2))
+        for key in parts_of(name, 1):
+            copies.receive(key)
+        copies.start(("right", name, 2, 0), right_copy(name, 2))
 
     def make_partial(name):
         left = LEFT_OF[name]
         for way in range(3):
             if ("left", left, way) not in copies.received:
                 copies.receive(("left", left, way))
-        copies.receive(("right", name, 0))
-        copies.receive(("right", name, 2))
+        for way in (0, 2):
+            for key in parts_of(name, way):
+                copies.receive(key)
         out = partial[name]
         count, depth, size = right_all[name].shape
         for first, step in lane_tiles(size):
@@ -683,7 +690,7 @@
     norm_into(after_cross[...], ln_ffn, nf, "nf")
     for name in ("fg", "fu", "fd"):
         copies.receive(("load", name))
-    for first, size in lane_tiles(weight["fg"].shape[1]):
+    for part, (first, size) in enumerate(lane_tiles(weight["fg"].shape[1])):
         lanes = slice(first, first + size)
         gate = dot(nf[...], whole("fg", lanes))
         up = dot(nf[...], whole("fu", lanes))
@@ -697,8 +704,9 @@
         right_all["fd"][own["fd"], :, lanes] = (bell * up).astype(BF)
         right_all["fg"][own["fg"], :, lanes] = (back * up * slope).astype(BF)
         right_all["fu"][own["fu"], :, lanes] = (back * bell).astype(BF)
-    for name in ("fd", "fg", "fu"):
-        share_right(name)
+        share_right("fd", part, lanes)
+        share_right("fg", part, lanes)
+    share_right("fu")
     for tile in range(tiles):
         push(
             2,
@@ -711,7 +719,6 @@
 
     pass_right("so")
     pass_right("co")
-    pass_right("fd")
     normed_grad = summed_all(2)
     cot[...] = jnp.where(valid, out_grad[...].astype(F32), 0.0) + norm_back(
         after_cross[...], ln_ffn, normed_grad, 2
@@ -742,9 +749,12 @@
     checkpoint(11)
     for tile in range(tiles):
         push(4, tile, dot_nt(right_all["cq"][own["cq"]], row_tile("cq", tile)))
+    share_right("cq")
     part_start(*dmem_args, 0)
+    pass_right("fd")
     pass_right("fg")
     make_partial("fg")
+    make_partial("co")
     make_partial("fd")
     for tile in range(tiles):
         lanes = slice(tile * TILE, (tile + 1) * TILE)
@@ -795,6 +805,7 @@
     split_heads(back, ags)
     pass_right("fu")
     make_partial("fu")
+    pass_right("cq")
     rs_step("fg", 0)
     near[1] = jnp.zeros(near.shape[1:], BF)
     for pair in range(pairs):
@@ -840,6 +851,7 @@
             state = lax.fori_loop(0, half_count, visit, state)
         part_start(*dkv_args(pair), 0)
         if pair == 0:
+            make_partial("so")
             part_step(*dmem_args, 0)
             rs_step("fu", 0)
         for slot, group in enumerate(members):
@@ -848,22 +860,18 @@
             ).astype(BF)
             far_sum[group] = state[2 * slot + 1]
     checkpoint(13)
-    share_right("cq")
-    make_partial("co")
     share_right("sq")
+    make_partial("cq")
+    rs_step("co", 0)
+    part_step(*dmem_args, 1)
     part_step(*dkv_args(0), 0)
     rs_step("fd", 0)
-    make_partial("so")
     query_part = [
         dot_nt(right_all["sq"][own["sq"]], row_tile("sq", tile)) for tile in range(tiles)
     ]
     for step in range(1, bits - 1):
         rs_step("fg", step)
     part_step(*dkv_args(1), 0)
-    part_step(*dmem_args, 1)
-    for step in range(1, bits - 1):
-        part_step(*dkv_args(0), step)
-        part_step(*dkv_args(1), step)
     mem_sum = None
     for step in range(2, bits):
         mem_sum = part_step(*dmem_args, step)
@@ -872,8 +880,14 @@
     right_all["cv"][own["cv"]] = mem_sum[:, pairs * 128 :]
     share_right("ck")
     share_right("cv")
-    pass_right("cq")
-    make_partial("cq")
+    for step in range(1, bits - 1):
+        part_step(*dkv_args(0), step)
+        part_step(*dkv_args(1), step)
+    rs_step("so", 0)
+    pass_right("sq")
+    make_partial("sq")
+    for step in range(1, bits - 1):
+        rs_step("fu", step)
     sums = [part_step(*dkv_args(pair), bits - 1).astype(BF) for pair in range(pairs)]
     for pair, value in enumerate(sums):
         right_all["sk"][own["sk"], :, pair * 128 : (pair + 1) * 128] = value[:, :128]
@@ -888,16 +902,14 @@
             + dot_nt(right_all["sk"][own["sk"]], row_tile("sk", tile))
             + dot_nt(right_all["sv"][own["sv"]], row_tile("sv", tile)),
         )
-    pass_right("sq")
-    make_partial("sq")
-    rs_step("co", 0)
-    rs_step("so", 0)
+    rs_step("cq", 0)
     for name in ("ck", "cv"):
         pass_right(name)
+        make_partial(name)
+    add_bias_gradient()
     for step in range(1, bits - 1):
-        rs_step("fu", step)
+        rs_step("co", step)
         rs_step("fd", step)
-    add_bias_gradient()
 
     checkpoint(14)
     mkg, mvg = right_all["ck"][own["ck"]], right_all["cv"][own["cv"]]
@@ -916,9 +928,8 @@
     copies.start(("mem",), mem_copy)
     for name in ("sk", "sv"):
         pass_right(name)
-    for name in ("ck", "cv", "sk", "sv"):
+    for name in ("sk", "sv"):
         make_partial(name)
-    rs_step("cq", 0)
 
     checkpoint(16)
     normed_grad = summed_all(5)
@@ -947,15 +958,15 @@
 
     for way in (1, 2, 0):
         copies.start(("small", way), small_near(way))
-    for step in range(1, bits - 1):
-        for name in ("co", "so", "cq"):
-            rs_step(name, step)
-    rs_step("sq", 0)
     for way in range(3):
         copies.receive(("small", way))
     small_far[blk // 2] = small[0] + small[1] + small[2] + small[3]
     for way in range(len(far_masks)):
         copies.start(("small", 3 + way), small_across(way))
+    rs_step("sq", 0)
+    for step in range(1, bits - 1):
+        for name in ("so", "cq"):
+            rs_step(name, step)
     for name in ("ck", "cv", "sk", "sv"):
         rs_finish(name)
     for step in range(1, bits - 1):
@@ -1106,8 +1117,8 @@
         sem((len(NAMES), half_count)),
         sem((len(LEFTS), 3)),
         sem((len(LEFTS), 3)),
-        sem((len(NAMES), 3)),
-        sem((len(NAMES), 3)),
+        sem((len(NAMES), 3, 3)),
+        sem((len(NAMES), 3, 3)),
         sem((3 + len(NAMES),)),
         sem((pairs, bits)),
         sem((pairs, bits)),

time: 147 us -> 138 us (0.939)
  Pallas kernels: 145 us -> 136 us
    pallas_call x1, Pallas kernels: 141 us -> 132 us  [run_layer(): pl.pallas_call(functools.partial(layer_kernel, (bits, rows, width, groups...]
where the time goes in v5:
time: 138 us
  Pallas kernels  136 us (99%)
  between operations  1.48 us (1%)
    pallas_call x1, Pallas kernels, run_layer(): pl.pallas_call(functools.partial(layer_kernel, (bits, rows, width, groups...  132 us
    pallas_call x1, Pallas kernels, finish(): pl.pallas_call(functools.partial(finish_kernel, count, width // 128, widt...  4.03 us

profile of v5, /device:TPU:0, one launch (start us, length us, event | category | flops | bytes accessed | tf_op | source)
XLA Modules:
  0.0 137.9 jit_solution(4812813350626606265)
XLA Ops:
  1.3 132.4 %layer.1 = (bf16[128,1024]{1,0:T(8,128)(2,1)}, f32[128,1024]{1,0:T(8,128)}, f32[32,1024]{1,0:T(8,128)}, f32[64,256]{1,0:T(8,128)}, f32[64,256]{1,0:T(8,128)}, /*...) custom-call(s32[1]{0:T(128)S(6)} %copy.37.refs_0_, ...), custom_call_target="tpu_custom_call" | custom-call | tf_op jit(solution)/shard_map/layer/pallas_call | solution.py:1142
  133.7 4.0 %finish.1 = (bf16[128,1024]{1,0:T(8,128)(2,1)}, f32[128,1024]{1,0:T(8,128)}, f32[32,1024]{1,0:T(8,128)}, f32[64,256]{1,0:T(8,128)}, f32[64,256]{1,0:T(8,128)}, /...) custom-call(bf16[128,1024]{1,0:T(8,128)(2,1)} %get-tuple-element.51., ...), custom_call_target="tpu_custom_call" | custom-call | tf_op jit(solution)/shard_map/finish/pallas_call | solution.py:1015

commit v6 on v5

--- a/solution.py
+++ b/solution.py
@@ -44,7 +44,7 @@
 def lane_tiles(width, step=512):
     return [(first, min(step, width - first)) for first in range(0, width, step)]
 SHARED_BIT = dict(gf=1, gc=1, gs=1)
-DIRECT = ("ck", "cv", "sk", "sv")
+DIRECT = ("sk", "sv")
 
 
 def shared_bit(name):
@@ -125,7 +125,7 @@
     staged = dict(zip(results, take(len(results))))
     (memory, kbuf, vbuf, vT, kT, tab, near, scores, qs, cqs, ags, att_self, att_cross) = take(13)
     (lse, probs, mk, mv, mkT, mvT, pushed, landed) = take(8)
-    (after_self, after_cross, cot, ns, nc, nf, bg) = take(7)
+    (after_self, after_cross, cot, ns, nc, nf, bg, inner_grad) = take(8)
     (dkv,) = take(1)
     dkv_land = take(bits)
     (dmem,) = take(1)
@@ -664,6 +664,9 @@
     valid = lax.broadcasted_iota(jnp.int32, (rows, 1), 0) + blk * rows < length
     bg[...] = jnp.where(valid, out_grad[...].astype(F32), 0.0).astype(BF)
     share_left("gf", bg[...])
+    if not long:
+        copies.receive(("load", "fd"))
+        inner_grad[...] = dot(bg[...], whole("fd"))
     after_self[...] = x + summed_all(0)
 
     checkpoint(6)
@@ -689,12 +692,13 @@
     checkpoint(8)
     norm_into(after_cross[...], ln_ffn, nf, "nf")
     for name in ("fg", "fu", "fd"):
-        copies.receive(("load", name))
+        if ("load", name) not in copies.received:
+            copies.receive(("load", name))
     for part, (first, size) in enumerate(lane_tiles(weight["fg"].shape[1])):
         lanes = slice(first, first + size)
         gate = dot(nf[...], whole("fg", lanes))
         up = dot(nf[...], whole("fu", lanes))
-        back = dot(bg[...], whole("fd", lanes))
+        back = dot(bg[...], whole("fd", lanes)) if long else inner_grad[:, lanes]
         bent = jnp.tanh(GELU_A * (gate + GELU_B * gate * gate * gate))
         opened = 0.5 * (1.0 + bent)
         slope = opened + 0.5 * gate * (1.0 - bent * bent) * (
@@ -714,8 +718,6 @@
             dot_nt(right_all["fg"][own["fg"]], row_tile("fg", tile))
             + dot_nt(right_all["fu"][own["fu"]], row_tile("fu", tile)),
         )
-    for tile in range(tiles):
-        push(3, tile, dot_nt(right_all["fd"][own["fd"]], row_tile("fd", tile)))
 
     pass_right("so")
     pass_right("co")
@@ -754,12 +756,10 @@
     pass_right("fd")
     pass_right("fg")
     make_partial("fg")
+    for tile in range(tiles):
+        push(3, tile, dot_nt(right_all["fd"][own["fd"]], row_tile("fd", tile)))
+    make_partial("fd")
     make_partial("co")
-    make_partial("fd")
-    for tile in range(tiles):
-        lanes = slice(tile * TILE, (tile + 1) * TILE)
-        staged["layer_out"][:, lanes] = (after_cross[:, lanes] + summed(3, tile)).astype(BF)
-    give("layer_out")
     normed_grad = summed_all(4)
     cot[...] = cot[...] + norm_back(after_self[...], ln_cross, normed_grad, 1)
     bg[...] = cot[...].astype(BF)
@@ -862,6 +862,10 @@
     checkpoint(13)
     share_right("sq")
     make_partial("cq")
+    for tile in range(tiles):
+        lanes = slice(tile * TILE, (tile + 1) * TILE)
+        staged["layer_out"][:, lanes] = (after_cross[:, lanes] + summed(3, tile)).astype(BF)
+    give("layer_out")
     rs_step("co", 0)
     part_step(*dmem_args, 1)
     part_step(*dkv_args(0), 0)
@@ -930,6 +934,8 @@
         pass_right(name)
     for name in ("sk", "sv"):
         make_partial(name)
+    for name in ("ck", "cv"):
+        rs_step(name, 0)
 
     checkpoint(16)
     normed_grad = summed_all(5)
@@ -967,7 +973,10 @@
     for step in range(1, bits - 1):
         for name in ("so", "cq"):
             rs_step(name, step)
-    for name in ("ck", "cv", "sk", "sv"):
+    for step in range(1, bits - 1):
+        for name in ("ck", "cv"):
+            rs_step(name, step)
+    for name in ("sk", "sv"):
         rs_finish(name)
     for step in range(1, bits - 1):
         rs_step("sq", step)
@@ -1095,6 +1104,7 @@
         vm((rows, width), BF),
         vm((rows, width), BF),
         vm((rows, width), BF),
+        vm((8 if long else rows, widths["fd"]), F32),
         vm((pairs, *by_bit, rows, 256), BF),
     ]
     scratch += [vm((pairs, *(2,) * (bits - 1 - stage), rows, 256), BF) for stage in range(bits)]

time: 138 us -> 137 us (level)
    pallas_call x1, Pallas kernels: 132 us -> 131 us  [run_layer(): pl.pallas_call(functools.partial(layer_kernel, (bits, rows, width, groups...]
where the time goes in v6:
time: 137 us; the launch traced here: 136 us
  Pallas kernels  135 us (99%)
  between operations  1.48 us (1%)
    pallas_call x1, Pallas kernels, run_layer(): pl.pallas_call(functools.partial(layer_kernel, (bits, rows, width, groups...  131 us
    pallas_call x1, Pallas kernels, finish(): pl.pallas_call(functools.partial(finish_kernel, count, width // 128, widt...  4.03 us

profile of v6, /device:TPU:0, one launch (start us, length us, event | category | flops | bytes accessed | tf_op | source)
XLA Modules:
  0.0 136.4 jit_solution(8664604207048131429)
XLA Ops:
  1.3 130.9 %layer.1 = (bf16[128,1024]{1,0:T(8,128)(2,1)}, f32[128,1024]{1,0:T(8,128)}, f32[32,1024]{1,0:T(8,128)}, f32[64,256]{1,0:T(8,128)}, f32[64,256]{1,0:T(8,128)}, /*...) custom-call(s32[1]{0:T(128)S(6)} %copy.37.refs_0_, ...), custom_call_target="tpu_custom_call" | custom-call | tf_op jit(solution)/shard_map/layer/pallas_call | solution.py:1152
  132.2 4.0 %finish.1 = (bf16[128,1024]{1,0:T(8,128)(2,1)}, f32[128,1024]{1,0:T(8,128)}, f32[32,1024]{1,0:T(8,128)}, f32[64,256]{1,0:T(8,128)}, f32[64,256]{1,0:T(8,128)}, /...) custom-call(bf16[128,1024]{1,0:T(8,128)(2,1)} %get-tuple-element.51., ...), custom_call_target="tpu_custom_call" | custom-call | tf_op jit(solution)/shard_map/finish/pallas_call | solution.py:1024
